TPU v7x, 32 devices: a whole 2x2x4 slice. The times are simulated.
32 devices in a mesh: dp: 8 (over z, core), tensor: 4 (over y, x).
Axes of the slice: x: 2, y: 2, z: 4, core: 2. Of those that a mesh axis runs over, the one named last changes fastest.
Arguments:
- tokens: bfloat16 [24576, 1024], P('dp'), may hold values from -6 to 6
- lengths: int32 [24], P('dp'), may hold values from 512 to 1024, as said below
- routes: int32 [24576, 1], P('dp'), may hold values from 0 to 7
- fill_order: int32 [8, 3072], P('dp'), may hold values from 0 to 3071, each once within a row
- norm_gain: float32 [1024], replicated, may hold values from 0.1 to 1.9
- norm_bias: float32 [1024], replicated, may hold values from -3 to 3
- qkv_weight: bfloat16 [1024, 16, 192], P(None, 'tensor'), may hold values from -0.1875 to 0.1875
- out_weight: bfloat16 [16, 64, 1024], P('tensor'), may hold values from -0.75 to 0.75
- centroids: bfloat16 [8, 1024], P('dp'), may hold values from -0.125 to 0.125
- expert_in: bfloat16 [8, 2, 1024, 4096], P('dp', None, None, 'tensor'), may hold values from -0.1875 to 0.1875
- expert_out: bfloat16 [8, 2, 4096, 1024], P('dp', None, 'tensor'), may hold values from -0.09375 to 0.09375
- cotangent: bfloat16 [24576, 1024], P('dp'), may hold values from -6 to 6
Outputs:
- output: bfloat16 [24576, 1024], P('dp')
- grad_tokens: bfloat16 [24576, 1024], P('dp')
- grad_norm_gain: float32 [1024], P('tensor')
- grad_norm_bias: float32 [1024], P('tensor')
- grad_qkv_weight: float32 [1024, 16, 192], P(None, 'tensor')
- grad_out_weight: float32 [16, 64, 1024], P('tensor')
- grad_centroids: float32 [8, 1024], P('dp')
- grad_expert_in: float32 [8, 2, 1024, 4096], P('dp', None, None, 'tensor')
- grad_expert_out: float32 [8, 2, 4096, 1024], P('dp', None, 'tensor')
Inputs may be any that keep to these rules, and one draw needn't show every extreme that they name: `lengths`: valid tokens of each sequence; one sequence has exactly 1024 and one exactly 512.
All inputs are finite; a program needn't handle non-finite values.
Results may differ from a plain program's by a relative error of at most 0.015.
Values may be sent and summed in bfloat16 or wider, within the bound.
A program may use at most 448 MiB of HBM per device.

v0:
```python
import jax
import jax.numpy as jnp
from jax import lax
from jax.sharding import PartitionSpec as P

EPSILON = 1e-05
HIGHEST = lax.Precision.HIGHEST


def widen(part):
    return lax.all_gather(part, "tensor", axis=1, tiled=True)


def narrow(term):
    return lax.psum_scatter(term, "tensor", scatter_dimension=1, tiled=True)


def widen_grad(part):
    return lax.all_gather(part, "tensor", axis=1, tiled=True)


def narrow_grad(term):
    return lax.psum_scatter(term, "tensor", scatter_dimension=1, tiled=True)


def row_totals(parts):
    return lax.psum(parts, "tensor")


def gelu_exact(values_in):
    return jax.nn.gelu(values_in, approximate=False)


def plan_slots(routes, order, lengths, seq_len, experts, capacity):
    count = routes.shape[0]
    seq_count = lengths.shape[0]
    places = jnp.arange(count, dtype=jnp.int32)
    limits = jnp.broadcast_to(lengths[:, None], (seq_count, seq_len)).reshape(count)
    is_valid = places % seq_len < limits
    order_row = order.reshape(count)
    route_sorted = routes.reshape(count)[order_row]
    valid_sorted = is_valid[order_row]
    matches = (
        (route_sorted[:, None] == jnp.arange(experts, dtype=jnp.int32)[None, :])
        & valid_sorted[:, None]
    ).astype(jnp.int32)
    before = jnp.cumsum(matches, axis=0) - matches
    rank_sorted = jnp.sum(before * matches, axis=1)
    kept_sorted = valid_sorted & (rank_sorted < capacity)
    slot_sorted = jnp.where(kept_sorted, route_sorted * capacity + rank_sorted, experts * capacity)
    slot_token = (
        jnp.full((experts * capacity + 1,), count, jnp.int32)
        .at[slot_sorted]
        .set(order_row)[: experts * capacity]
    )
    token_slot = jnp.zeros((count,), jnp.int32).at[order_row].set(slot_sorted)
    return (slot_token, token_slot)


def to_slots(token_rows, slot_token):
    padded = jnp.concatenate(
        [token_rows, jnp.zeros((1, token_rows.shape[1]), token_rows.dtype)], axis=0
    )
    return padded[slot_token]


def from_slots(slotted, token_slot):
    padded = jnp.concatenate([slotted, jnp.zeros((1, slotted.shape[1]), slotted.dtype)], axis=0)
    return padded[token_slot]


def body(
    tokens,
    lengths,
    routes,
    fill_order,
    norm_gain,
    norm_bias,
    qkv_weight,
    out_weight,
    centroids,
    expert_in,
    expert_out,
    cotangent,
):
    tok_count, model_width = tokens.shape
    seq_count = lengths.shape[0]
    seq_len = tok_count // seq_count
    heads_here = qkv_weight.shape[1]
    head_size = out_weight.shape[1]
    experts = lax.axis_size("dp")
    shards = lax.axis_size("tensor")
    capacity = (9 * tok_count + 8 * experts - 1) // (8 * experts)
    column_count = model_width // shards
    column_start = lax.axis_index("tensor") * column_count
    score_scale = head_size ** (-0.5)
    slot_rows = experts * capacity
    input_rows = tokens.astype(jnp.float32)
    centre = input_rows - jnp.mean(input_rows, axis=1, keepdims=True)
    inverse_scale = lax.rsqrt(jnp.mean(centre * centre, axis=1, keepdims=True) + EPSILON)
    normed = centre * inverse_scale
    ln_in = (normed * norm_gain + norm_bias).astype(jnp.bfloat16)
    projected = jnp.einsum(
        "td,dhe->the", ln_in, qkv_weight, preferred_element_type=jnp.float32
    ).astype(jnp.bfloat16)
    projected = projected.reshape(seq_count, seq_len, heads_here, 3 * head_size)
    queries = projected[..., :head_size]
    key_vectors = projected[..., head_size : 2 * head_size]
    values = projected[..., 2 * head_size :]
    positions = jnp.arange(seq_len, dtype=jnp.int32)
    allowed = (positions[None, None, :] <= positions[None, :, None]) & (
        positions[None, None, :] < lengths[:, None, None]
    )

    def attention_probs(log_total):
        scores = (
            jnp.einsum("sqhd,skhd->shqk", queries, key_vectors, preferred_element_type=jnp.float32)
            * score_scale
        )
        scores = jnp.where(allowed[:, None], scores, -1e30)
        if log_total is None:
            row_max = jnp.max(scores, axis=-1, keepdims=True)
            log_total = row_max + jnp.log(
                jnp.sum(jnp.exp(scores - row_max), axis=-1, keepdims=True)
            )
        return (jnp.exp(scores - log_total), log_total)

    attention_weights, log_total = attention_probs(None)
    attended = jnp.einsum(
        "shqk,skhd->sqhd",
        attention_weights.astype(jnp.bfloat16),
        values,
        preferred_element_type=jnp.float32,
    ).astype(jnp.bfloat16)
    attended = attended.reshape(tok_count, heads_here * head_size)
    out_flat = out_weight.reshape(heads_here * head_size, model_width)
    attn_cols = narrow(jnp.dot(attended, out_flat, preferred_element_type=jnp.float32))
    mixed_cols = lax.dynamic_slice_in_dim(input_rows, column_start, column_count, 1) + attn_cols
    sent_cols = mixed_cols.astype(jnp.bfloat16)
    slot_token, token_slot = plan_slots(routes, fill_order, lengths, seq_len, experts, capacity)
    sent_rows = widen(sent_cols)
    arrived = lax.all_to_all(
        to_slots(sent_rows, slot_token).reshape(experts, capacity, model_width),
        "dp",
        split_axis=0,
        concat_axis=0,
        tiled=True,
    )
    expert_rows = arrived.reshape(slot_rows, model_width)
    expert_cols = lax.dynamic_slice_in_dim(expert_rows, column_start, column_count, 1)
    centroid = centroids[0]
    gate_values = jax.nn.sigmoid(jnp.dot(expert_rows, centroid, preferred_element_type=jnp.float32))
    current = expert_cols.astype(jnp.float32)
    inputs_full = expert_rows
    saved_layers = []
    for sublayer in range(2):
        if sublayer > 0:
            inputs_full = widen(current.astype(jnp.bfloat16))
        hidden_pre = jnp.dot(
            inputs_full, expert_in[0, sublayer], preferred_element_type=jnp.float32
        )
        hidden_act = gelu_exact(hidden_pre).astype(jnp.bfloat16)
        current = current + narrow(
            jnp.dot(hidden_act, expert_out[0, sublayer], preferred_element_type=jnp.float32)
        )
        saved_layers.append((inputs_full, hidden_pre, hidden_act))
    returned = (gate_values[:, None] * current).astype(jnp.bfloat16)
    came_back = lax.all_to_all(
        returned.reshape(experts, capacity, column_count),
        "dp",
        split_axis=0,
        concat_axis=0,
        tiled=True,
    )
    expert_share = from_slots(came_back.reshape(slot_rows, column_count), token_slot).astype(
        jnp.float32
    )
    output = widen((mixed_cols + expert_share).astype(jnp.bfloat16))
    grad_cols = lax.dynamic_slice_in_dim(cotangent, column_start, column_count, 1)
    grad_slots = lax.all_to_all(
        to_slots(grad_cols, slot_token).reshape(experts, capacity, column_count),
        "dp",
        split_axis=0,
        concat_axis=0,
        tiled=True,
    )
    grad_slots = grad_slots.reshape(slot_rows, column_count).astype(jnp.float32)
    grad_gate = row_totals((jnp.sum(grad_slots * current, axis=1),))[0]
    grad_logit = grad_gate * gate_values * (1.0 - gate_values)
    grad_current = gate_values[:, None] * grad_slots
    grads_in = [None, None]
    grads_back = [None, None]
    for sublayer in (1, 0):
        inputs_full, hidden_pre, hidden_act = saved_layers[sublayer]
        grad_branch = widen_grad(grad_current.astype(jnp.bfloat16))
        grads_back[sublayer] = jnp.einsum(
            "rf,rd->fd", hidden_act, grad_branch, preferred_element_type=jnp.float32
        )
        grad_act = jnp.einsum(
            "rd,fd->rf", grad_branch, expert_out[0, sublayer], preferred_element_type=jnp.float32
        )
        grad_pre = jax.vjp(gelu_exact, hidden_pre)[1](grad_act)[0].astype(jnp.bfloat16)
        grads_in[sublayer] = jnp.einsum(
            "rd,rf->df", inputs_full, grad_pre, preferred_element_type=jnp.float32
        )
        grad_current = grad_current + narrow_grad(
            jnp.einsum(
                "rf,df->rd", grad_pre, expert_in[0, sublayer], preferred_element_type=jnp.float32
            )
        )
    centroid_cols = lax.dynamic_slice_in_dim(centroid, column_start, column_count, 0).astype(
        jnp.float32
    )
    grad_current = grad_current + grad_logit[:, None] * centroid_cols[None, :]
    grad_centroid = jnp.dot(grad_logit, expert_rows.astype(jnp.float32), precision=HIGHEST)
    grad_return = lax.all_to_all(
        grad_current.astype(jnp.bfloat16).reshape(experts, capacity, column_count),
        "dp",
        split_axis=0,
        concat_axis=0,
        tiled=True,
    )
    grad_mixed = grad_cols.astype(jnp.float32) + from_slots(
        grad_return.reshape(slot_rows, column_count), token_slot
    ).astype(jnp.float32)
    grad_attn = widen_grad(grad_mixed.astype(jnp.bfloat16))
    grad_out_local = jnp.einsum(
        "ta,td->ad", attended, grad_attn, preferred_element_type=jnp.float32
    ).reshape(heads_here, head_size, model_width)
    grad_attended = jnp.einsum(
        "td,ad->ta", grad_attn, out_flat, preferred_element_type=jnp.float32
    ).astype(jnp.bfloat16)
    grad_attended = grad_attended.reshape(seq_count, seq_len, heads_here, head_size)
    attention_weights, unused_total = attention_probs(log_total)
    grad_probs = jnp.einsum(
        "sqhd,skhd->shqk", grad_attended, values, preferred_element_type=jnp.float32
    )
    row_delta = jnp.sum(attention_weights * grad_probs, axis=-1, keepdims=True)
    grad_scores = (attention_weights * (grad_probs - row_delta)).astype(jnp.bfloat16)
    grad_query = (
        jnp.einsum("shqk,skhd->sqhd", grad_scores, key_vectors, preferred_element_type=jnp.float32)
        * score_scale
    ).astype(jnp.bfloat16)
    grad_key = (
        jnp.einsum("shqk,sqhd->skhd", grad_scores, queries, preferred_element_type=jnp.float32)
        * score_scale
    ).astype(jnp.bfloat16)
    grad_value = jnp.einsum(
        "shqk,sqhd->skhd",
        attention_weights.astype(jnp.bfloat16),
        grad_attended,
        preferred_element_type=jnp.float32,
    ).astype(jnp.bfloat16)
    grad_projected = jnp.concatenate([grad_query, grad_key, grad_value], axis=-1).reshape(
        tok_count, heads_here, 3 * head_size
    )
    grad_qkv_local = jnp.einsum(
        "td,the->dhe", ln_in, grad_projected, preferred_element_type=jnp.float32
    )
    grad_ln = narrow_grad(
        jnp.einsum("the,dhe->td", grad_projected, qkv_weight, preferred_element_type=jnp.float32)
    )
    normed_cols = lax.dynamic_slice_in_dim(normed, column_start, column_count, 1)
    gain_cols = lax.dynamic_slice_in_dim(norm_gain, column_start, column_count, 0)
    grad_normed = grad_ln * gain_cols
    total_plain, total_cross = row_totals(
        (jnp.sum(grad_normed, axis=1), jnp.sum(grad_normed * normed_cols, axis=1))
    )
    grad_input_cols = grad_mixed + inverse_scale * (
        grad_normed
        - total_plain[:, None] / model_width
        - normed_cols * total_cross[:, None] / model_width
    )
    grad_tokens = widen_grad(grad_input_cols.astype(jnp.bfloat16))
    gain_part = jnp.sum(grad_ln * normed_cols, axis=0)
    bias_part = jnp.sum(grad_ln, axis=0)
    grad_qkv_weight, grad_out_weight, grad_norm_gain, grad_norm_bias = lax.psum(
        (grad_qkv_local, grad_out_local, gain_part, bias_part), "dp"
    )
    grad_expert_in = jnp.stack(grads_in)[None]
    grad_expert_out = jnp.stack(grads_back)[None]
    return (
        output,
        grad_tokens,
        grad_norm_gain,
        grad_norm_bias,
        grad_qkv_weight,
        grad_out_weight,
        grad_centroid[None],
        grad_expert_in,
        grad_expert_out,
    )


def solution(mesh):
    return jax.shard_map(
        body,
        mesh=mesh,
        in_specs=(
            P("dp", None),
            P("dp"),
            P("dp", None),
            P("dp", None),
            P(),
            P(),
            P(None, "tensor", None),
            P("tensor", None, None),
            P("dp", None),
            P("dp", None, None, "tensor"),
            P("dp", None, "tensor", None),
            P("dp", None),
        ),
        out_specs=(
            P("dp", None),
            P("dp", None),
            P("tensor"),
            P("tensor"),
            P(None, "tensor", None),
            P("tensor", None, None),
            P("dp", None),
            P("dp", None, None, "tensor"),
            P("dp", None, "tensor", None),
        ),
        check_vma=False,
    )
```

profile of v0, /device:TPU:0, one launch (start us, length us, event | category | flops | bytes accessed | tf_op | source)
XLA Modules:
  0.0 2078.8 jit_solution(8050757125903381133)
XLA Ops:
  62.0 21.2 %exponential_reduce_fusion = f32[3,4,1024]{2,1,0:T(4,128)S(1)} fusion(f32[3,4,1024,1024]{2,3,1,0:T(8,128)} %get-tuple-element.32, f32[3,4,1024]{2,1,0:T(4,128)S(1)} %get-tuple-element.31, pred[3,1024,1024]{1,2,0:T(8,128)(4,1)S(1)} %broadcast_and_fusion), kind=kLoop, calls=%fused_computation.11 | loop fusion | flops 50319360 | bytes 53575680 | tf_op jit(solution)/shard_map/reduce_sum | solution.py:124
  83.2 20.1 fusion.53
  121.9 114.7 %reduce-scatter.7.cloned.1.call-done = f32[3072,256]{1,0:T(8,128)} async-done(((f32[3072,1024]{1,0:T(8,128)}), f32[3072,256]{1,0:T(8,128)}) %reduce-scatter.7.cloned.1.call-update) | async-done | bytes 3145744 | tf_op jit(solution)/shard_map/reduce_scatter | solution.py:15
  337.2 160.9 %all_to_all.20 = bf16[8,432,1024]{2,1,0:T(8,128)(2,1)S(1)} all-to-all(bf16[8,432,1024]{2,1,0:T(8,128)(2,1)} %bitcast.166), channel_id=1, replica_groups=mesh['dp'=8,'tensor'=4] {'dp'}, dimensions={0} | all-to-all | bytes 14155776 | tf_op jit(solution)/shard_map/all_to_all | solution.py:142
  498.1 38.4 %multiply_convert_fusion.2 = (bf16[3456,1024]{1,0:T(8,128)(2,1)S(1)}, f32[3456,1024]{1,0:T(8,128)}, f32[3456,1024]{1,0:T(8,128)}) fusion(bf16[3456,1024]{1,0:T(8,128)(2,1)S(1)} %bitcast.158, bf16[1,2,1024,1024]{3,2,1,0:T(8,128)(2,1)S(1)} %copy-done.43), kind=kOutput, calls=%fused_computation.34 | convolution fusion | flops 7477788672 | bytes 44564480 | tf_op jit(solution)/shard_map/dot_general | solution.py:159
  549.7 131.3 %reduce-scatter.9.cloned.1.call-done = f32[3456,256]{1,0:T(8,128)} async-done(((f32[3456,1024]{1,0:T(8,128)}), f32[3456,256]{1,0:T(8,128)}) %reduce-scatter.9.cloned.1.call-update) | async-done | bytes 3538960 | tf_op jit(solution)/shard_map/reduce_scatter | solution.py:15
  708.0 36.4 %all-to-all-done.2 = bf16[8,432,256]{2,1,0:T(8,128)(2,1)S(1)} async-done(((bf16[8,432,256]{2,1,0:T(8,128)(2,1)}), bf16[8,432,256]{2,1,0:T(8,128)(2,1)S(1)}, u32[]{:S(2)}, u32[]{:S(2)}) %all-to-all-start.2) | async-done | bytes 1769504 | tf_op jit(solution)/shard_map/all_to_all | solution.py:180
  761.9 41.2 %multiply_convert_fusion.1 = (bf16[3456,1024]{1,0:T(8,128)(2,1)}, f32[3456,1024]{1,0:T(8,128)}, f32[3456,1024]{1,0:T(8,128)}) fusion(bf16[3456,1024]{1,0:T(8,128)(2,1)} %all-gather.10.cloned.1.call-done, bf16[1,2,1024,1024]{3,2,1,0:T(8,128)(2,1)} %param.21), kind=kOutput, calls=%fused_computation.21 | convolution fusion | flops 7477788672 | bytes 44564480 | tf_op jit(solution)/shard_map/dot_general | solution.py:159
  803.1 37.1 %all-gather.14.cloned.1.call-done = bf16[3456,1024]{1,0:T(8,128)(2,1)} async-done(((bf16[3456,256]{1,0:T(8,128)(2,1)}), bf16[3456,1024]{1,0:T(8,128)(2,1)}) %all-gather.14.cloned.1.call-update) | async-done | bytes 7077904 | tf_op jit(solution)/shard_map/all_gather | solution.py:19
  840.2 24.2 %add_convert_fusion.1 = bf16[3456,1024]{1,0:T(8,128)(2,1)} fusion(f32[3456,1024]{1,0:T(8,128)} %get-tuple-element.20, f32[3456,1024]{1,0:T(8,128)} %get-tuple-element.34, bf16[3456,1024]{1,0:T(8,128)(2,1)} %all-gather.14.cloned.1.call-done, bf16[1,2,1024,1024]{3,2,1,0:T(8,128)(2,1)} %param.22), kind=kOutput, calls=%fused_computation.20 | convolution fusion | flops 7297302528 | bytes 44564480 | tf_op jit(solution)/shard_map/rd,fd->rf/dot_general | solution.py:199
  892.6 119.6 %reduce-scatter.13.cloned.1.call-done = f32[3456,256]{1,0:T(8,128)} async-done(((f32[3456,1024]{1,0:T(8,128)}), f32[3456,256]{1,0:T(8,128)}) %reduce-scatter.13.cloned.1.call-update) | async-done | bytes 3538960 | tf_op jit(solution)/shard_map/reduce_scatter | solution.py:23
  1012.2 136.8 %reduce-scatter.11.cloned.1.call-done = f32[3456,256]{1,0:T(8,128)} async-done(((f32[3456,1024]{1,0:T(8,128)}), f32[3456,256]{1,0:T(8,128)}) %reduce-scatter.11.cloned.1.call-update) | async-done | bytes 3538960 | tf_op jit(solution)/shard_map/reduce_scatter | solution.py:15
  1156.8 76.7 %all-gather.16.cloned.1.call-done = bf16[3456,1024]{1,0:T(8,128)(2,1)} async-done(((bf16[3456,256]{1,0:T(8,128)(2,1)}), bf16[3456,1024]{1,0:T(8,128)(2,1)}) %all-gather.16.cloned.1.call-update) | async-done | bytes 7077904 | tf_op jit(solution)/shard_map/all_gather | solution.py:19
  1233.4 24.2 %add_convert_fusion = bf16[3456,1024]{1,0:T(8,128)(2,1)} fusion(f32[3456,1024]{1,0:T(8,128)} %get-tuple-element.22, f32[3456,1024]{1,0:T(8,128)} %get-tuple-element.33, bf16[3456,1024]{1,0:T(8,128)(2,1)} %all-gather.16.cloned.1.call-done, bf16[1,2,1024,1024]{3,2,1,0:T(8,128)(2,1)} %param.22), kind=kOutput, calls=%fused_computation.19 | convolution fusion | flops 7297302528 | bytes 44564480 | tf_op jit(solution)/shard_map/rd,fd->rf/dot_general | solution.py:199
  1287.8 117.8 %reduce-scatter.15.cloned.1.call-done = f32[3456,256]{1,0:T(8,128)} async-done(((f32[3456,1024]{1,0:T(8,128)}), f32[3456,256]{1,0:T(8,128)}) %reduce-scatter.15.cloned.1.call-update) | async-done | bytes 3538960 | tf_op jit(solution)/shard_map/reduce_scatter | solution.py:23
  1427.5 29.6 %all-to-all-done.3 = bf16[8,432,256]{2,1,0:T(8,128)(2,1)S(1)} async-done(((bf16[8,432,256]{2,1,0:T(8,128)(2,1)}), bf16[8,432,256]{2,1,0:T(8,128)(2,1)S(1)}, u32[]{:S(2)}, u32[]{:S(2)}) %all-to-all-start.3) | async-done | bytes 1769504 | tf_op jit(solution)/shard_map/all_to_all | solution.py:216
  1476.5 68.1 %all-gather.18.cloned.1.call-done = bf16[3072,1024]{1,0:T(8,128)(2,1)} async-done(((bf16[3072,256]{1,0:T(8,128)(2,1)}), bf16[3072,1024]{1,0:T(8,128)(2,1)}) %all-gather.18.cloned.1.call-update) | async-done | bytes 6291472 | tf_op jit(solution)/shard_map/all_gather | solution.py:19
  1556.3 36.9 %multiply_reduce_fusion = (f32[3,4,1024]{2,1,0:T(4,128)S(1)}, f32[3,4,1024,1024]{2,3,1,0:T(8,128)}) fusion(f32[3,4,1024,1024]{2,3,1,0:T(8,128)} %get-tuple-element.32, f32[3,4,1024]{2,1,0:T(4,128)S(1)} %copy-done.20, pred[3,1024,1024]{1,2,0:T(8,128)(4,1)} %copy-done.4, bf16[3,1024,4,64]{1,3,2,0:T(8,128)(2,1)S(1)} %copy.36, ...), kind=kOutput, calls=%fused_computation.9 | convolution fusion | flops 1673515008 | bytes 107053056 | tf_op jit(solution)/shard_map/sqhd,skhd->shqk/dot_general | solution.py:235
  1593.2 41.9 %multiply_convert_fusion = bf16[3,4,1024,1024]{2,3,1,0:T(8,128)(2,1)} fusion(f32[3,4,1024,1024]{2,3,1,0:T(8,128)} %get-tuple-element.36, f32[3,4,1024,1024]{2,3,1,0:T(8,128)} %get-tuple-element.32, f32[3,4,1024]{2,1,0:T(4,128)S(1)} %get-tuple-element.35, f32[3,4,1024]{2,1,0:T(4,128)S(1)} %copy-done.20, pred[3,1024,1024]{1,2,0:T(8,128)(4,1)} %copy-done.4), kind=kLoop, calls=%fused_computation.8 | loop fusion | flops 75497472 | bytes 129073152 | tf_op jit(solution)/shard_map/convert_element_type | solution.py:239
  1662.8 20.3 fusion.54
  1695.8 46.4 %all_to_all.21 = bf16[8,432,256]{2,1,0:T(8,128)(2,1)S(1)} all-to-all(bf16[8,432,256]{2,1,0:T(8,128)(2,1)S(1)} %bitcast.170), channel_id=1, replica_groups=mesh['dp'=8,'tensor'=4] {'dp'}, dimensions={0} | all-to-all | bytes 3538944 | tf_op jit(solution)/shard_map/all_to_all | solution.py:168
  1768.5 46.6 %reduce-scatter.17.cloned.1.call-done = f32[3072,256]{1,0:T(8,128)} async-done(((f32[3072,1024]{1,0:T(8,128)}), f32[3072,256]{1,0:T(8,128)}) %reduce-scatter.17.cloned.1.call-update) | async-done | bytes 3145744 | tf_op jit(solution)/shard_map/reduce_scatter | solution.py:23
  1938.2 20.8 %all-gather.20.cloned.1.call-done = bf16[3072,1024]{1,0:T(8,128)(2,1)} async-done(((bf16[3072,256]{1,0:T(8,128)(2,1)}), bf16[3072,1024]{1,0:T(8,128)(2,1)}) %all-gather.20.cloned.1.call-update) | async-done | bytes 6291472 | tf_op jit(solution)/shard_map/all_gather | solution.py:19
  1959.0 99.8 %all-reduce.9.cloned.1.call-done = (f32[1024,4,192]{0,2,1:T(8,128)}, f32[4,64,1024]{2,1,0:T(8,128)}) async-done(((f32[1024,4,192]{0,2,1:T(8,128)}, f32[4,64,1024]{2,1,0:T(8,128)}), (f32[1024,4,192]{0,2,1:T(8,128)}, f32[4,64,1024]{2,1,0:T(8,128)})) %all-reduce.9.cloned.1.call-update) | async-done | bytes 4194320 | tf_op jit(solution)/shard_map/psum | solution.py:277
  (240 shorter events, 553.0 us)
Async XLA Ops:
  7.2 229.4 %reduce-scatter.7.cloned.1.call-start = ((), (), s32[]{:S(2)}) async-start(), calls=%async_computation.10 | async-start | bytes 15728640 | tf_op jit(solution)/shard_map/reduce_scatter | solution.py:15
  113.0 198.1 %all-gather.8.cloned.1.call-start = ((), (), s32[]{:S(2)}) async-start(), calls=%async_computation.11 | async-start | bytes 7864320 | tf_op jit(solution)/shard_map/all_gather | solution.py:11
  121.9 119.2 %copy-start.37 = (s32[1,3072]{1,0:T(1,128)S(1)}, s32[1,3072]{1,0:T(1,128)}, u32[]{:S(2)}) copy-start(s32[1,3072]{1,0:T(1,128)} %param.15) | copy-start | bytes 36868
  121.9 139.6 %copy-start.1 = (s32[3072,1]{0,1:T(1,128)S(1)}, s32[3072,1]{0,1:T(1,128)}, u32[]{:S(2)}) copy-start(s32[3072,1]{0,1:T(1,128)} %param.14) | copy-start | bytes 36868
  240.9 440.1 %reduce-scatter.9.cloned.1.call-start = ((), (), s32[]{:S(2)}) async-start(), calls=%async_computation.12 | async-start | bytes 17694720 | tf_op jit(solution)/shard_map/reduce_scatter | solution.py:15
  337.2 160.9 %copy-start.43 = (bf16[1,2,1024,1024]{3,2,1,0:T(8,128)(2,1)S(1)}, bf16[1,2,1024,1024]{3,2,1,0:T(8,128)(2,1)}, u32[]{:S(2)}) copy-start(bf16[1,2,1024,1024]{3,2,1,0:T(8,128)(2,1)} %param.21) | copy-start | bytes 12582916
  549.5 212.4 %all-gather.10.cloned.1.call-start = ((), (), s32[]{:S(2)}) async-start(), calls=%async_computation.13 | async-start | bytes 8847360 | tf_op jit(solution)/shard_map/all_gather | solution.py:11
  697.8 46.7 %all-to-all-start.2 = ((bf16[8,432,256]{2,1,0:T(8,128)(2,1)}), bf16[8,432,256]{2,1,0:T(8,128)(2,1)S(1)}, u32[]{:S(2)}, u32[]{:S(2)}) async-start(bf16[8,432,256]{2,1,0:T(8,128)(2,1)} %bitcast.171), calls=%async_computation.5 | async-start | bytes 3538944 | tf_op jit(solution)/shard_map/all_to_all | solution.py:180
  702.4 137.8 %all-gather.14.cloned.1.call-start = ((), (), s32[]{:S(2)}) async-start(), calls=%async_computation.16 | async-start | bytes 8847360 | tf_op jit(solution)/shard_map/all_gather | solution.py:19
  708.0 95.1 %copy-start.23 = (f32[3456]{0:T(1024)}, f32[3456]{0:T(1024)S(1)}, u32[]{:S(2)}) copy-start(f32[3456]{0:T(1024)S(1)} %add_divide_fusion) | copy-start | bytes 41476
  746.2 266.0 %reduce-scatter.13.cloned.1.call-start = ((), (), s32[]{:S(2)}) async-start(), calls=%async_computation.17 | async-start | bytes 17694720 | tf_op jit(solution)/shard_map/reduce_scatter | solution.py:23
  878.4 270.6 %reduce-scatter.11.cloned.1.call-start = ((), (), s32[]{:S(2)}) async-start(), calls=%async_computation.14 | async-start | bytes 17694720 | tf_op jit(solution)/shard_map/reduce_scatter | solution.py:15
  892.5 256.5 %copy-start.6 = (bf16[8,432,256]{2,1,0:T(8,128)(2,1)S(1)}, bf16[8,432,256]{2,1,0:T(8,128)(2,1)}, u32[]{:S(2)}) copy-start(bf16[8,432,256]{2,1,0:T(8,128)(2,1)} %copy-done.5) | copy-start | bytes 5308420
  892.5 256.5 %copy-start.24 = (f32[3456]{0:T(1024)S(1)}, f32[3456]{0:T(1024)}, u32[]{:S(2)}) copy-start(f32[3456]{0:T(1024)} %copy-done.23) | copy-start | bytes 41476
  892.6 340.9 %all-gather.16.cloned.1.call-start = ((), (), s32[]{:S(2)}) async-start(), calls=%async_computation.18 | async-start | bytes 8847360 | tf_op jit(solution)/shard_map/all_gather | solution.py:19
  1156.7 248.9 %reduce-scatter.15.cloned.1.call-start = ((), (), s32[]{:S(2)}) async-start(), calls=%async_computation.19 | async-start | bytes 17694720 | tf_op jit(solution)/shard_map/reduce_scatter | solution.py:23
  1287.8 122.7 %copy-start.27 = (f32[3456]{0:T(1024)}, f32[3456]{0:T(1024)S(1)}, u32[]{:S(2)}) copy-start(f32[3456]{0:T(1024)S(1)} %subtract_multiply_fusion.1) | copy-start | bytes 41476
  1410.5 46.6 %all-to-all-start.3 = ((bf16[8,432,256]{2,1,0:T(8,128)(2,1)}), bf16[8,432,256]{2,1,0:T(8,128)(2,1)S(1)}, u32[]{:S(2)}, u32[]{:S(2)}) async-start(bf16[8,432,256]{2,1,0:T(8,128)(2,1)} %bitcast.174), calls=%async_computation.8 | async-start | bytes 3538944 | tf_op jit(solution)/shard_map/all_to_all | solution.py:216
  1415.1 129.5 %all-gather.18.cloned.1.call-start = ((), (), s32[]{:S(2)}) async-start(), calls=%async_computation.20 | async-start | bytes 7864320 | tf_op jit(solution)/shard_map/all_gather | solution.py:19
  1427.5 128.8 %copy-start.31 = (s32[3072]{0:T(1024)}, s32[3072]{0:T(1024)S(1)}, u32[]{:S(2)}) copy-start(s32[3072]{0:T(1024)S(1)} %fusion.73) | copy-start | bytes 36868
  1476.5 338.7 %reduce-scatter.17.cloned.1.call-start = ((), (), s32[]{:S(2)}) async-start(), calls=%async_computation.21 | async-start | bytes 15728640 | tf_op jit(solution)/shard_map/reduce_scatter | solution.py:23
  1694.3 229.8 %all-gather.12.cloned.1.call-start = ((), (), s32[]{:S(2)}) async-start(), calls=%async_computation.15 | async-start | bytes 7864320 | tf_op jit(solution)/shard_map/all_gather | solution.py:11
  1760.6 198.5 %all-gather.20.cloned.1.call-start = ((), (), s32[]{:S(2)}) async-start(), calls=%async_computation.22 | async-start | bytes 7864320 | tf_op jit(solution)/shard_map/all_gather | solution.py:19
  1840.5 218.3 %all-reduce.9.cloned.1.call-start = ((), (), s32[]{:S(2)}) async-start(), calls=%async_computation.23 | async-start | bytes 8388608 | tf_op jit(solution)/shard_map/psum | solution.py:277
  (47 other events, 723.1 us)
Sparse Core Ops, SparseCore 0:
  113.1 123.4 reduce-scatter.6
  241.1 69.9 all-gather.7
  549.6 131.3 reduce-scatter.8
  685.3 76.5 all-gather.9
  763.6 76.5 all-gather.13
  878.6 133.6 reduce-scatter.12
  1015.3 133.6 reduce-scatter.10
  1156.9 76.5 all-gather.15
  1271.8 133.7 reduce-scatter.14
  1476.6 67.9 all-gather.17
  1694.4 120.7 reduce-scatter.16
  1816.9 70.2 all-gather.11
  1889.0 70.0 all-gather.19
  1961.9 96.8 all-reduce.8
where the time goes:
time: 2090 us; the launch traced here: 2080 us
  waiting for transfers between devices  1070 us (51%)
  matrix products  399 us (19%)
  blocking collectives  253 us (12%)
  local copies, waits for them, and re-layouts  188 us (9%)
  other arithmetic  146 us (7%)
    reduce_scatter x3, waiting for transfers between devices, narrow(): return lax.psum_scatter(term, 'tensor', scatter_dimension=1, tiled=True)  383 us
    reduce_scatter x3, waiting for transfers between devices, narrow_grad(): return lax.psum_scatter(term, 'tensor', scatter_dimension=1, tiled=True)  284 us
    all_gather x4, waiting for transfers between devices, widen_grad(): return lax.all_gather(part, 'tensor', axis=1, tiled=True)  203 us
    all_to_all x1, blocking collectives, body(): lax.all_to_all(to_slots(sent_rows, slot_token).reshape(experts, capacity,...  161 us
    psum x1, waiting for transfers between devices, body(): lax.psum((grad_qkv_local, grad_out_local, gain_part, bias_part), 'dp')  99.8 us
    dot_general x2, matrix products, body(): jnp.dot(inputs_full, expert_in[0, sublayer], preferred_element_type=jnp.f...  79.6 us
    dot_general x2, matrix products, body(): jnp.einsum('rd,fd->rf', grad_branch, expert_out[0, sublayer], preferred_e...  48.3 us
    all_to_all x1, blocking collectives, body(): lax.all_to_all(returned.reshape(experts, capacity, column_count), 'dp', s...  46.4 us
  transfers between devices with their start and end apart: 16, of which 15 were waited for; matrix products, arithmetic and copies ran while one was open for 13% of the time, Pallas kernels for 0%

commit v1 on v0

v1 whole, which is shorter than its diff:
```python
import math

import jax
import jax.numpy as jnp
from jax import lax
from jax.sharding import PartitionSpec as P

EPSILON = 1e-05
HIGHEST = lax.Precision.HIGHEST
F32 = jnp.float32
BF16 = jnp.bfloat16


class Grid:
    def __init__(self, size):
        inner = int(math.isqrt(size))
        while size % inner:
            inner -= 1
        self.size = size
        self.parts = {"x": inner, "y": size // inner}

    def _pairs(self, axis, shift):
        wide, tall = self.parts["x"], self.parts["y"]
        pairs = []
        for row in range(tall):
            for col in range(wide):
                if axis == "x":
                    other = row * wide + (col + shift) % wide
                else:
                    other = ((row + shift) % tall) * wide + col
                pairs.append((other, row * wide + col))
        return pairs

    def fetch(self, value, axis, shift=1):
        return lax.ppermute(value, "tensor", self._pairs(axis, shift))

    def gather_list(self, value, axis):
        return [value] + [self.fetch(value, axis, s) for s in range(1, self.parts[axis])]

    def scatter_list(self, parts, axis):
        total = parts[0]
        for s in range(1, self.parts[axis]):
            total = total + self.fetch(parts[s].astype(BF16), axis, -s).astype(F32)
        return total


def gather_rows(grid, value):
    if grid.size != 4:
        return lax.all_gather(value, "tensor", axis=0, tiled=False)
    half = value.shape[0] // 2
    me = lax.axis_index("tensor")
    first, second = value[:half], value[half:]
    first_x = grid.fetch(first, "x")
    second_y = grid.fetch(second, "y")
    first_y = grid.fetch(first, "y")
    second_x = grid.fetch(second, "x")
    first_xy = grid.fetch(first_x, "y")
    second_xy = grid.fetch(second_y, "x")
    out = jnp.zeros((4,) + value.shape, value.dtype)
    out = lax.dynamic_update_slice(out, value[None], (me, 0, 0))
    for other, top, bottom in ((1, first_x, second_x), (2, first_y, second_y), (3, first_xy, second_xy)):
        place = jnp.bitwise_xor(me, other)
        out = lax.dynamic_update_slice(out, top[None], (place, 0, 0))
        out = lax.dynamic_update_slice(out, bottom[None], (place, half, 0))
    return out


def scatter_rows(grid, term):
    size, rows, width = term.shape
    if size != 4:
        return lax.psum_scatter(term.astype(BF16), "tensor", scatter_dimension=0, tiled=False).astype(F32)
    me = lax.axis_index("tensor")
    half = width // 2

    def pick(other, low):
        place = jnp.bitwise_xor(me, other)
        return lax.dynamic_slice(term, (place, 0, low), (1, rows, half))[0]

    totals = []
    for low, near, far, near_axis, far_axis in ((0, 1, 2, "x", "y"), (half, 2, 1, "y", "x")):
        got_far = grid.fetch(pick(3, low).astype(BF16), near_axis)
        got_own = grid.fetch(pick(near, low).astype(BF16), near_axis)
        onward = pick(far, low).astype(F32) + got_far.astype(F32)
        got = grid.fetch(onward.astype(BF16), far_axis)
        totals.append(pick(0, low).astype(F32) + got_own.astype(F32) + got.astype(F32))
    return jnp.concatenate(totals, axis=1)


def gelu_pair(pre):
    cdf = 0.5 * (1.0 + lax.erf(pre * (2.0**-0.5)))
    density = jnp.exp(-0.5 * pre * pre) * ((2.0 * math.pi) ** -0.5)
    return (pre * cdf).astype(BF16), (cdf + pre * density).astype(BF16)


def plan_slots(routes, order, lengths, seq_len, experts, capacity, padded):
    count = routes.shape[0]
    seq_count = lengths.shape[0]
    places = jnp.arange(count, dtype=jnp.int32)
    limits = jnp.broadcast_to(lengths[:, None], (seq_count, seq_len)).reshape(count)
    is_valid = places % seq_len < limits
    order_row = order.reshape(count)
    route_sorted = routes.reshape(count)[order_row]
    valid_sorted = is_valid[order_row]
    matches = (
        (route_sorted[:, None] == jnp.arange(experts, dtype=jnp.int32)[None, :])
        & valid_sorted[:, None]
    ).astype(jnp.int32)
    before = jnp.cumsum(matches, axis=0) - matches
    rank_sorted = jnp.sum(before * matches, axis=1)
    kept_sorted = valid_sorted & (rank_sorted < capacity)
    slot_sorted = jnp.where(kept_sorted, route_sorted * padded + rank_sorted, experts * padded)
    slot_token = (
        jnp.full((experts * padded + 1,), count, jnp.int32)
        .at[slot_sorted]
        .set(order_row)[: experts * padded]
    )
    token_slot = jnp.zeros((count,), jnp.int32).at[order_row].set(slot_sorted)
    return (slot_token, token_slot)


def dot(a, b, contract):
    return lax.dot_general(a, b, (contract, ((), ())), preferred_element_type=F32)


def body(
    tokens,
    lengths,
    routes,
    fill_order,
    norm_gain,
    norm_bias,
    qkv_weight,
    out_weight,
    centroids,
    expert_in,
    expert_out,
    cotangent,
):
    tok_count, model_width = tokens.shape
    seq_count = lengths.shape[0]
    seq_len = tok_count // seq_count
    heads_here = qkv_weight.shape[1]
    head_size = out_weight.shape[1]
    experts = lax.axis_size("dp")
    shards = lax.axis_size("tensor")
    grid = Grid(shards)
    me = lax.axis_index("tensor")
    capacity = (9 * tok_count + 8 * experts - 1) // (8 * experts)
    share = 16 * -(-capacity // (16 * shards))
    padded = share * shards
    own_rows = experts * share
    tok_rows = tok_count // shards
    score_scale = head_size ** (-0.5)

    row_axis = ("y", "x")
    weight_axis = ("x", "y")
    win = [grid.gather_list(expert_in[0, k], weight_axis[k]) for k in range(2)]
    wout = [grid.gather_list(expert_out[0, k], weight_axis[k]) for k in range(2)]
    out_flat = out_weight.reshape(heads_here * head_size, model_width)
    out_all = lax.all_gather(out_flat, "tensor", axis=0, tiled=True)

    slot_token, token_slot = plan_slots(
        routes, fill_order, lengths, seq_len, experts, capacity, padded
    )
    own_slot = lax.dynamic_slice_in_dim(
        slot_token.reshape(experts, padded), me * share, share, 1
    ).reshape(own_rows)
    own_filled = (own_slot < tok_count)[:, None]
    own_index = jnp.minimum(own_slot, tok_count - 1)
    kept = (token_slot < experts * padded)[:, None]
    tok_expert = jnp.minimum(token_slot // padded, experts - 1)
    tok_rank = token_slot % padded
    tok_place = ((tok_rank // share) * experts + tok_expert) * share + tok_rank % share

    def to_experts(rows):
        picked = jnp.where(own_filled, rows[own_index], jnp.zeros((), rows.dtype))
        moved = lax.all_to_all(
            picked.reshape(experts, share, model_width), "dp", split_axis=0, concat_axis=0, tiled=True
        )
        return moved.reshape(own_rows, model_width)

    def from_experts(rows):
        moved = lax.all_to_all(
            rows.reshape(experts, share, model_width), "dp", split_axis=0, concat_axis=0, tiled=True
        )
        every = gather_rows(grid, moved.reshape(own_rows, model_width))
        picked = every.reshape(shards * own_rows, model_width)[tok_place]
        return jnp.where(kept, picked, jnp.zeros((), rows.dtype)).astype(F32)

    grad_ret = to_experts(cotangent).astype(F32)

    input_rows = tokens.astype(F32)
    centre = input_rows - jnp.mean(input_rows, axis=1, keepdims=True)
    inverse_scale = lax.rsqrt(jnp.mean(centre * centre, axis=1, keepdims=True) + EPSILON)
    normed = centre * inverse_scale
    ln_in = (normed * norm_gain + norm_bias).astype(BF16)
    projected = jnp.einsum(
        "td,dhe->the", ln_in, qkv_weight, preferred_element_type=F32
    ).astype(BF16)
    projected = projected.reshape(seq_count, seq_len, heads_here, 3 * head_size)
    queries = projected[..., :head_size]
    key_vectors = projected[..., head_size : 2 * head_size]
    values = projected[..., 2 * head_size :]
    positions = jnp.arange(seq_len, dtype=jnp.int32)
    allowed = (positions[None, None, :] <= positions[None, :, None]) & (
        positions[None, None, :] < lengths[:, None, None]
    )

    def attention_probs(log_total):
        scores = (
            jnp.einsum("sqhd,skhd->shqk", queries, key_vectors, preferred_element_type=F32)
            * score_scale
        )
        scores = jnp.where(allowed[:, None], scores, -1e30)
        if log_total is None:
            row_max = jnp.max(scores, axis=-1, keepdims=True)
            log_total = row_max + jnp.log(
                jnp.sum(jnp.exp(scores - row_max), axis=-1, keepdims=True)
            )
        return (jnp.exp(scores - log_total), log_total)

    attention_weights, log_total = attention_probs(None)
    attended = jnp.einsum(
        "shqk,skhd->sqhd",
        attention_weights.astype(BF16),
        values,
        preferred_element_type=F32,
    ).astype(BF16)
    attended = attended.reshape(tok_count, heads_here * head_size)
    every_attended = gather_rows(grid, attended)
    attended_all = jnp.swapaxes(every_attended, 0, 1).reshape(tok_count, -1)
    mixed = input_rows + dot(attended_all, out_all, ((1,), (0,)))
    sent = mixed.astype(BF16)

    expert_rows = to_experts(sent)
    centroid = centroids[0]
    gate = jax.nn.sigmoid(jnp.dot(expert_rows, centroid, preferred_element_type=F32))[:, None]
    current = expert_rows.astype(F32)
    saved = []
    for k in range(2):
        rows_in = jnp.concatenate(grid.gather_list(current.astype(BF16), row_axis[k]), axis=0)
        acts, slopes = [], []
        total = None
        for w_in, w_out in zip(win[k], wout[k]):
            act, slope = gelu_pair(dot(rows_in, w_in, ((1,), (0,))))
            term = dot(act, w_out, ((1,), (0,)))
            total = term if total is None else total + term
            acts.append(act)
            slopes.append(slope)
        parts = jnp.split(total, grid.parts[row_axis[k]], axis=0)
        current = current + grid.scatter_list(parts, row_axis[k])
        saved.append((rows_in, acts, slopes))
    output = (mixed + from_experts((gate * current).astype(BF16))).astype(BF16)

    grad_gate = jnp.sum(grad_ret * current, axis=1, keepdims=True)
    grad_logit = grad_gate * gate * (1.0 - gate)
    grad_current = gate * grad_ret
    grads_in = [None, None]
    grads_back = [None, None]
    for k in (1, 0):
        rows_in, acts, slopes = saved[k]
        branch = jnp.concatenate(grid.gather_list(grad_current.astype(BF16), row_axis[k]), axis=0)
        total = None
        in_parts, out_parts = [], []
        for w_in, w_out, act, slope in zip(win[k], wout[k], acts, slopes):
            grad_pre = (dot(branch, w_out, ((1,), (1,))) * slope.astype(F32)).astype(BF16)
            term = dot(grad_pre, w_in, ((1,), (1,)))
            total = term if total is None else total + term
            out_parts.append(dot(act, branch, ((0,), (0,))))
            in_parts.append(dot(rows_in, grad_pre, ((0,), (0,))))
        parts = jnp.split(total, grid.parts[row_axis[k]], axis=0)
        grad_current = grad_current + grid.scatter_list(parts, row_axis[k])
        grads_in[k] = grid.scatter_list(in_parts, weight_axis[k])
        grads_back[k] = grid.scatter_list(out_parts, weight_axis[k])
    grad_rows = (grad_current + grad_logit * centroid.astype(F32)[None, :]).astype(BF16)
    grad_centroid = lax.psum(
        jnp.sum(grad_logit * expert_rows.astype(F32), axis=0, keepdims=True), "tensor"
    )
    grad_mixed = cotangent.astype(F32) + from_experts(grad_rows)

    grad_attn = grad_mixed.astype(BF16)
    grad_out_local = dot(attended, grad_attn, ((0,), (0,))).reshape(
        heads_here, head_size, model_width
    )
    grad_attended = dot(grad_attn, out_flat, ((1,), (1,))).astype(BF16)
    grad_attended = grad_attended.reshape(seq_count, seq_len, heads_here, head_size)
    attention_weights, unused_total = attention_probs(log_total)
    grad_probs = jnp.einsum(
        "sqhd,skhd->shqk", grad_attended, values, preferred_element_type=F32
    )
    row_delta = jnp.sum(attention_weights * grad_probs, axis=-1, keepdims=True)
    grad_scores = (attention_weights * (grad_probs - row_delta)).astype(BF16)
    grad_query = (
        jnp.einsum("shqk,skhd->sqhd", grad_scores, key_vectors, preferred_element_type=F32)
        * score_scale
    ).astype(BF16)
    grad_key = (
        jnp.einsum("shqk,sqhd->skhd", grad_scores, queries, preferred_element_type=F32)
        * score_scale
    ).astype(BF16)
    grad_value = jnp.einsum(
        "shqk,sqhd->skhd",
        attention_weights.astype(BF16),
        grad_attended,
        preferred_element_type=F32,
    ).astype(BF16)
    grad_projected = jnp.concatenate([grad_query, grad_key, grad_value], axis=-1).reshape(
        tok_count, heads_here, 3 * head_size
    )
    grad_qkv_local = jnp.einsum(
        "td,the->dhe", ln_in, grad_projected, preferred_element_type=F32
    )
    grad_ln_part = jnp.einsum(
        "the,dhe->td", grad_projected, qkv_weight, preferred_element_type=F32
    )
    grad_ln = scatter_rows(grid, grad_ln_part.astype(BF16).reshape(shards, tok_rows, model_width))

    def own(rows):
        return lax.dynamic_slice_in_dim(rows, me * tok_rows, tok_rows, 0)

    own_scale = own(inverse_scale)
    own_normed = own(centre) * own_scale
    grad_normed = grad_ln * norm_gain
    mean_plain = jnp.mean(grad_normed, axis=1, keepdims=True)
    mean_cross = jnp.mean(grad_normed * own_normed, axis=1, keepdims=True)
    grad_input = own(grad_mixed) + own_scale * (grad_normed - mean_plain - own_normed * mean_cross)
    grad_tokens = gather_rows(grid, grad_input.astype(BF16)).reshape(tok_count, model_width)
    norm_parts = jnp.stack([jnp.sum(grad_ln * own_normed, axis=0), jnp.sum(grad_ln, axis=0)])
    norm_total = lax.dynamic_slice_in_dim(
        lax.psum(norm_parts, ("dp", "tensor")), me * (model_width // shards), model_width // shards, 1
    )
    grad_qkv_weight, grad_out_weight = lax.psum((grad_qkv_local, grad_out_local), "dp")
    return (
        output,
        grad_tokens,
        norm_total[0],
        norm_total[1],
        grad_qkv_weight,
        grad_out_weight,
        grad_centroid,
        jnp.stack(grads_in)[None],
        jnp.stack(grads_back)[None],
    )


def solution(mesh):
    return jax.shard_map(
        body,
        mesh=mesh,
        in_specs=(
            P("dp", None),
            P("dp"),
            P("dp", None),
            P("dp", None),
            P(),
            P(),
            P(None, "tensor", None),
            P("tensor", None, None),
            P("dp", None),
            P("dp", None, None, "tensor"),
            P("dp", None, "tensor", None),
            P("dp", None),
        ),
        out_specs=(
            P("dp", None),
            P("dp", None),
            P("tensor"),
            P("tensor"),
            P(None, "tensor", None),
            P("tensor", None, None),
            P("dp", None),
            P("dp", None, None, "tensor"),
            P("dp", None, "tensor", None),
        ),
        check_vma=False,
    )
```

time: 2090 us -> 1420 us (0.68)
  waiting for transfers between devices: 1070 us -> 494 us
  blocking collectives: 253 us -> 60.2 us
  local copies, waits for them, and re-layouts: 188 us -> 259 us
  starting transfers between devices: 9.96 us -> 79.7 us
  matrix products: 399 us -> 350 us
    reduce_scatter x6 -> x0, waiting for transfers between devices: 667 us -> none  [the longest x3 383 us: narrow(): return lax.psum_scatter(term, 'tensor', scatter_dimension=1, tiled=True)]
    ppermute x0 -> x46, waiting for transfers between devices: none -> 439 us  [fetch(): return lax.ppermute(value, 'tensor', self._pairs(axis, shift))]
    all_gather x7 -> x1, waiting for transfers between devices: 235 us -> 0.01 us  [body(): out_all = lax.all_gather(out_flat, 'tensor', axis=0, tiled=True)]
    all_to_all x2 -> x0, blocking collectives: 207 us -> none  [the longest x1 161 us: body(): lax.all_to_all(to_slots(sent_rows, slot_token).reshape(experts, capacity,...]
    psum x1, waiting for transfers between devices: 99.8 us -> 16.4 us  [body(): lax.psum((grad_qkv_local, grad_out_local), 'dp')]
    ppermute x0 -> x46, starting transfers between devices: none -> 58.3 us  [fetch(): return lax.ppermute(value, 'tensor', self._pairs(axis, shift))]
    dot_general x19 -> x30, matrix products: 295 us -> 248 us  [the longest x27 207 us: dot(): lax.dot_general(a, b, (contract, ((), ())), preferred_element_type=F32)]
    dynamic_update_slice x0 -> x26, local copies, waits for them, and re-layouts: none -> 38.5 us  [the longest x12 16 us: gather_rows(): out = lax.dynamic_update_slice(out, top[None], (place, 0, 0))]
  transfers between devices with their start and end apart: 16 -> 52, of which waited for: 15 -> 31; matrix products, arithmetic and copies ran while one was open for 13% -> 37% of each run, Pallas kernels for 0% -> 0%
where the time goes in v1:
time: 1420 us; the launch traced here: 1410 us
  waiting for transfers between devices  494 us (35%)
  matrix products  350 us (25%)
  local copies, waits for them, and re-layouts  259 us (18%)
  other arithmetic  150 us (11%)
  starting transfers between devices  79.7 us (6%)
  blocking collectives  60.2 us (4%)
  between operations  15.8 us (1%)
    ppermute x46, waiting for transfers between devices, fetch(): return lax.ppermute(value, 'tensor', self._pairs(axis, shift))  439 us
    dot_general x27, matrix products, dot(): lax.dot_general(a, b, (contract, ((), ())), preferred_element_type=F32)  207 us
    ppermute x46, starting transfers between devices, fetch(): return lax.ppermute(value, 'tensor', self._pairs(axis, shift))  58.3 us
    psum x1, blocking collectives, body(): lax.psum(norm_parts, ('dp', 'tensor'))  49.7 us
    convert_element_type x1, other arithmetic, body(): grad_scores = (attention_weights * (grad_probs - row_delta)).astype(BF16)  42.3 us
    gather x2, local copies, waits for them, and re-layouts, from_experts(): picked = every.reshape(shards * own_rows, model_width)[tok_place]  39.8 us
    all_to_all x2, waiting for transfers between devices, to_experts(): lax.all_to_all(picked.reshape(experts, share, model_width), 'dp', split_a...  37.3 us
    dot_general x1, matrix products, body(): jnp.einsum('sqhd,skhd->shqk', grad_attended, values, preferred_element_ty...  36.9 us
  transfers between devices with their start and end apart: 52, of which 31 were waited for; matrix products, arithmetic and copies ran while one was open for 37% of the time, Pallas kernels for 0%

profile of v1, /device:TPU:0, one launch (start us, length us, event | category | flops | bytes accessed | tf_op | source)
XLA Modules:
  0.0 1408.5 jit_solution(3828291646385503996)
XLA Ops:
  46.0 19.2 %fusion = (f32[3,4,1024]{2,1,0:T(4,128)S(1)}, f32[3,4,1024,1024]{2,3,1,0:T(8,128)}) fusion(pred[3,1024,1024]{1,2,0:T(8,128)(4,1)S(1)} %broadcast_and_fusion, bf16[3,1024,4,64]{1,0,3,2:T(4,128)(2,1)S(1)} %get-tuple-element.29, bf16[3,1024,4,64]{1,0,3,2:T(4,128)(2,1)S(1)} %get-tuple-element.27), kind=kOutput, calls=%fused_computation.13 | convolution fusion | flops 1648349184 | bytes 56672256 | tf_op jit(solution)/shard_map/sqhd,skhd->shqk/dot_general | solution.py:211
  65.2 21.3 %exponential_reduce_fusion = f32[3,4,1024]{2,1,0:T(4,128)S(1)} fusion(f32[3,4,1024,1024]{2,3,1,0:T(8,128)} %get-tuple-element.54, f32[3,4,1024]{2,1,0:T(4,128)S(1)} %get-tuple-element.53, pred[3,1024,1024]{1,2,0:T(8,128)(4,1)S(1)} %broadcast_and_fusion), kind=kLoop, calls=%fused_computation.11 | loop fusion | flops 50319360 | bytes 53575680 | tf_op jit(solution)/shard_map/reduce_sum | solution.py:218
  86.6 20.1 %fusion.39 = bf16[3,1024,4,64]{1,3,2,0:T(8,128)(2,1)S(1)} fusion(bf16[3,1024,4,64]{1,0,3,2:T(4,128)(2,1)S(1)} %get-tuple-element.28, f32[3,4,1024,1024]{2,3,1,0:T(8,128)} %get-tuple-element.54, f32[3,4,1024]{2,1,0:T(4,128)S(1)} %log_add_fusion, pred[3,1024,1024]{1,2,0:T(8,128)(4,1)S(1)} %broadcast_and_fusion), kind=kOutput, calls=%fused_computation.133 | convolution fusion | flops 1661730816 | bytes 56672256 | tf_op jit(solution)/shard_map/shqk,skhd->sqhd/dot_general | solution.py:223
  120.9 19.4 %gather_fusion = pred[3072]{0:T(1024)(128)(4,1)S(1)} fusion(pred[3072]{0:T(1024)(128)(4,1)S(1)} %fusion.60, s32[3072]{0:T(1024)S(1)} %broadcast_clamp_fusion), kind=kCustom, calls=%fused_computation | custom fusion | bytes 18432 | tf_op jit(solution)/shard_map/gather | solution.py:103
  140.3 17.4 %gather_fusion.1 = s32[3072]{0:T(1024)S(1)} fusion(s32[3072]{0:T(1024)S(1)} %bitcast.249, s32[3072]{0:T(1024)S(1)} %broadcast_clamp_fusion), kind=kCustom, calls=%fused_computation.1 | custom fusion | bytes 36864 | tf_op jit(solution)/shard_map/gather | solution.py:102
  245.4 37.3 %all-to-all-done = bf16[8,112,1024]{2,1,0:T(8,128)(2,1)S(1)} async-done(((bf16[8,112,1024]{2,1,0:T(8,128)(2,1)}), bf16[8,112,1024]{2,1,0:T(8,128)(2,1)S(1)}, u32[]{:S(2)}, u32[]{:S(2)}) %all-to-all-start) | async-done | bytes 1835040 | tf_op jit(solution)/shard_map/all_to_all | solution.py:177
  292.6 31.6 %collective-permute-done.6 = bf16[896,1024]{1,0:T(8,128)(2,1)S(1)} collective-permute-done((bf16[896,1024]{1,0:T(8,128)(2,1)S(1)}, bf16[896,1024]{1,0:T(8,128)(2,1)S(1)}, u32[]{:S(2)}, u32[]{:S(2)}) %collective-permute-start.6) | collective-permute-done | bytes 1835040 | tf_op jit(solution)/shard_map/ppermute | solution.py:35
  362.3 36.4 %collective-permute-done.9 = bf16[896,1024]{1,0:T(8,128)(2,1)} collective-permute-done((bf16[896,1024]{1,0:T(8,128)(2,1)}, bf16[896,1024]{1,0:T(8,128)(2,1)}, u32[]{:S(2)}, u32[]{:S(2)}) %collective-permute-start.9) | collective-permute-done | bytes 1835040 | tf_op jit(solution)/shard_map/ppermute | solution.py:35
  409.3 34.3 %collective-permute-done.11 = bf16[1024,1024]{1,0:T(8,128)(2,1)} collective-permute-done((bf16[1024,1024]{1,0:T(8,128)(2,1)}, bf16[1024,1024]{1,0:T(8,128)(2,1)}, u32[]{:S(2)}, u32[]{:S(2)}) %collective-permute-start.11) | collective-permute-done | bytes 2097184 | tf_op jit(solution)/shard_map/ppermute | solution.py:35
  540.4 19.4 %collective-permute-done.21 = bf16[896,1024]{1,0:T(8,128)(2,1)S(1)} collective-permute-done((bf16[896,1024]{1,0:T(8,128)(2,1)S(1)}, bf16[896,1024]{1,0:T(8,128)(2,1)S(1)}, u32[]{:S(2)}, u32[]{:S(2)}) %collective-permute-start.21) | collective-permute-done | bytes 1835040 | tf_op jit(solution)/shard_map/ppermute | solution.py:35
  559.8 33.0 %collective-permute-done.13 = bf16[896,1024]{1,0:T(8,128)(2,1)} collective-permute-done((bf16[896,1024]{1,0:T(8,128)(2,1)S(1)}, bf16[896,1024]{1,0:T(8,128)(2,1)}, u32[]{:S(2)}, u32[]{:S(2)}) %collective-permute-start.13) | collective-permute-done | bytes 1835040 | tf_op jit(solution)/shard_map/ppermute | solution.py:35
  600.3 34.3 %collective-permute-done.22 = bf16[896,1024]{1,0:T(8,128)(2,1)S(1)} collective-permute-done((bf16[896,1024]{1,0:T(8,128)(2,1)S(1)}, bf16[896,1024]{1,0:T(8,128)(2,1)S(1)}, u32[]{:S(2)}, u32[]{:S(2)}) %collective-permute-start.22) | collective-permute-done | bytes 1835040 | tf_op jit(solution)/shard_map/ppermute | solution.py:35
  672.0 33.6 %collective-permute-done.23 = bf16[896,1024]{1,0:T(8,128)(2,1)} collective-permute-done((bf16[896,1024]{1,0:T(8,128)(2,1)}, bf16[896,1024]{1,0:T(8,128)(2,1)}, u32[]{:S(2)}, u32[]{:S(2)}) %collective-permute-start.23) | collective-permute-done | bytes 1835040 | tf_op jit(solution)/shard_map/ppermute | solution.py:35
  788.7 34.7 %collective-permute-done.43 = bf16[1024,1024]{1,0:T(8,128)(2,1)} collective-permute-done((bf16[1024,1024]{1,0:T(8,128)(2,1)}, bf16[1024,1024]{1,0:T(8,128)(2,1)}, u32[]{:S(2)}, u32[]{:S(2)}) %collective-permute-start.43) | collective-permute-done | bytes 2097184 | tf_op jit(solution)/shard_map/ppermute | solution.py:35
  904.9 17.3 %collective-permute-done.25 = bf16[448,1024]{1,0:T(8,128)(2,1)S(1)} collective-permute-done((bf16[448,1024]{1,0:T(8,128)(2,1)S(1)}, bf16[448,1024]{1,0:T(8,128)(2,1)S(1)}, u32[]{:S(2)}, u32[]{:S(2)}) %collective-permute-start.25) | collective-permute-done | bytes 917536 | tf_op jit(solution)/shard_map/ppermute | solution.py:35
  967.9 18.9 %collective-permute-done.19 = bf16[448,1024]{1,0:T(8,128)(2,1)S(1)} collective-permute-done((bf16[448,1024]{1,0:T(8,128)(2,1)S(1)}, bf16[448,1024]{1,0:T(8,128)(2,1)S(1)}, u32[]{:S(2)}, u32[]{:S(2)}) %collective-permute-start.19) | collective-permute-done | bytes 917536 | tf_op jit(solution)/shard_map/ppermute | solution.py:35
  986.8 19.7 %collective-permute-done.29 = bf16[448,1024]{1,0:T(8,128)(2,1)S(1)} collective-permute-done((bf16[448,1024]{1,0:T(8,128)(2,1)S(1)}, bf16[448,1024]{1,0:T(8,128)(2,1)S(1)}, u32[]{:S(2)}, u32[]{:S(2)}) %collective-permute-start.29) | collective-permute-done | bytes 917536 | tf_op jit(solution)/shard_map/ppermute | solution.py:35
  1007.8 19.9 %gather_fusion.3 = bf16[3072,1024]{1,0:T(8,128)(2,1)} fusion(bf16[3584,1024]{1,0:T(8,128)(2,1)} %bitcast.37, s32[3072]{0:T(1024)S(1)} %fusion.66), kind=kCustom, calls=%fused_computation.3 | custom fusion | bytes 12595200 | tf_op jit(solution)/shard_map/gather | solution.py:187
  1027.7 19.9 %gather_fusion.5 = bf16[3072,1024]{1,0:T(8,128)(2,1)} fusion(bf16[3584,1024]{1,0:T(8,128)(2,1)} %bitcast.51, s32[3072]{0:T(1024)S(1)} %fusion.66), kind=kCustom, calls=%fused_computation.5 | custom fusion | bytes 12595200 | tf_op jit(solution)/shard_map/gather | solution.py:187
  1047.6 17.5 %convert_add_fusion.1 = (f32[3072,1024]{1,0:T(8,128)S(1)}, bf16[3072,1024]{1,0:T(8,128)(2,1)}) fusion(bf16[3072,1024]{1,0:T(8,128)(2,1)} %param.23, bf16[3072,1024]{1,0:T(8,128)(2,1)} %gather_fusion.5, pred[3072]{0:T(1024)(128)(4,1)S(1)} %broadcast_compare_fusion, bf16[3072,1024]{1,0:T(8,128)(2,1)} %gather_fusion.3, f32[3072,1024]{1,0:T(8,128)} %get-tuple-element.56, ...), kind=kLoop, calls=%fused_computation.19 | loop fusion | flops 31457280 | bytes 56626176 | tf_op jit(solution)/shard_map/add | solution.py:279
  1078.7 36.9 %multiply_reduce_fusion = (f32[3,4,1024]{2,1,0:T(4,128)S(1)}, f32[3,4,1024,1024]{2,3,1,0:T(8,128)}) fusion(f32[3,4,1024,1024]{2,3,1,0:T(8,128)} %get-tuple-element.54, f32[3,4,1024]{2,1,0:T(4,128)S(1)} %copy-done.33, pred[3,1024,1024]{1,2,0:T(8,128)(4,1)} %copy-done.3, bf16[3,1024,4,64]{1,3,2,0:T(8,128)(2,1)S(1)} %copy.37, ...), kind=kOutput, calls=%fused_computation.9 | convolution fusion | flops 1673515008 | bytes 107053056 | tf_op jit(solution)/shard_map/sqhd,skhd->shqk/dot_general | solution.py:288
  1115.6 42.3 %multiply_convert_fusion = bf16[3,4,1024,1024]{2,3,1,0:T(8,128)(2,1)} fusion(f32[3,4,1024,1024]{2,3,1,0:T(8,128)} %get-tuple-element.66, f32[3,4,1024,1024]{2,3,1,0:T(8,128)} %get-tuple-element.54, f32[3,4,1024]{2,1,0:T(4,128)S(1)} %get-tuple-element.65, f32[3,4,1024]{2,1,0:T(4,128)S(1)} %copy-done.33, pred[3,1024,1024]{1,2,0:T(8,128)(4,1)} %copy-done.3), kind=kLoop, calls=%fused_computation.8 | loop fusion | flops 75497472 | bytes 129073152 | tf_op jit(solution)/shard_map/convert_element_type | solution.py:292
  1185.4 20.3 %fusion.40 = bf16[3,1024,4,64]{1,3,2,0:T(8,128)(2,1)S(1)} fusion(bf16[3,1024,4,64]{1,3,2,0:T(8,128)(2,1)} %copy-done.12, f32[3,4,1024,1024]{2,3,1,0:T(8,128)} %get-tuple-element.54, f32[3,4,1024]{2,1,0:T(4,128)S(1)} %copy-done.33, pred[3,1024,1024]{1,2,0:T(8,128)(4,1)} %copy-done.3), kind=kOutput, calls=%fused_computation.134 | convolution fusion | flops 1661730816 | bytes 56672256 | tf_op jit(solution)/shard_map/shqk,sqhd->skhd/dot_general | solution.py:301
  1308.7 49.7 %psum.28 = f32[2,1024]{1,0:T(2,128)S(1)} all-reduce(f32[2,1024]{1,0:T(2,128)S(1)} %pad_maximum_fusion.6), channel_id=1, replica_groups=mesh['dp'=8,'tensor'=4] {'dp','tensor'}, use_global_device_ids=true, to_apply=%region_15.16 | all-reduce | flops 2048 | bytes 16384 | tf_op jit(solution)/shard_map/psum | solution.py:330
  (396 shorter events, 738.5 us)
Async XLA Ops:
  7.2 200.2 %all-gather.2.cloned.1.call-start = ((), (), s32[]{:S(2)}) async-start(), calls=%async_computation.4 | async-start | bytes 2621440 | tf_op jit(solution)/shard_map/all_gather | solution.py:160
  110.7 75.7 %collective-permute-start = (bf16[1536,256]{0,1:T(8,128)(2,1)}, bf16[1536,256]{0,1:T(8,128)(2,1)}, u32[]{:S(2)}, u32[]{:S(2)}) collective-permute-start(bf16[1536,256]{0,1:T(8,128)(2,1)} %get-tuple-element.44), channel_id=1, source_target_pairs={{1,0},{0,1},{3,2},{2,3},{5,4},{4,5},{7,6},{6,7},{9,8},{8,9},{11,10... | collective-permute-start | bytes 2359304 | tf_op jit(solution)/shard_map/ppermute | solution.py:35
  113.6 80.4 %collective-permute-start.2 = (bf16[1536,256]{0,1:T(8,128)(2,1)}, bf16[1536,256]{0,1:T(8,128)(2,1)}, u32[]{:S(2)}, u32[]{:S(2)}) collective-permute-start(bf16[1536,256]{0,1:T(8,128)(2,1)} %get-tuple-element.44), channel_id=1, source_target_pairs={{2,0},{3,1},{0,2},{1,3},{6,4},{7,5},{4,6},{5,7},{10,8},{11,9},{8,1... | collective-permute-start | bytes 2359304 | tf_op jit(solution)/shard_map/ppermute | solution.py:35
  115.1 76.8 %collective-permute-start.1 = (bf16[1536,256]{0,1:T(8,128)(2,1)}, bf16[1536,256]{0,1:T(8,128)(2,1)}, u32[]{:S(2)}, u32[]{:S(2)}) collective-permute-start(bf16[1536,256]{0,1:T(8,128)(2,1)} %get-tuple-element.43), channel_id=1, source_target_pairs={{1,0},{0,1},{3,2},{2,3},{5,4},{4,5},{7,6},{6,7},{9,8},{8,9},{11,10... | collective-permute-start | bytes 2359304 | tf_op jit(solution)/shard_map/ppermute | solution.py:35
  115.7 72.7 %collective-permute-start.3 = (bf16[1536,256]{0,1:T(8,128)(2,1)}, bf16[1536,256]{0,1:T(8,128)(2,1)}, u32[]{:S(2)}, u32[]{:S(2)}) collective-permute-start(bf16[1536,256]{0,1:T(8,128)(2,1)} %get-tuple-element.43), channel_id=1, source_target_pairs={{2,0},{3,1},{0,2},{1,3},{6,4},{7,5},{4,6},{5,7},{10,8},{11,9},{8,1... | collective-permute-start | bytes 2359304 | tf_op jit(solution)/shard_map/ppermute | solution.py:35
  287.9 58.7 %collective-permute-start.8 = (bf16[1024,1024]{1,0:T(8,128)(2,1)S(1)}, bf16[1024,1024]{1,0:T(8,128)(2,1)S(1)}, u32[]{:S(2)}, u32[]{:S(2)}) collective-permute-start(bf16[1024,1024]{1,0:T(8,128)(2,1)S(1)} %get-tuple-element.33), channel_id=1, source_target_pairs={{1,0},{0,1},{3,2},{2,3},{5,4},{4,5},{7,6},{6,7},{9,8},{8,9},{11,10... | collective-permute-start | bytes 6291464 | tf_op jit(solution)/shard_map/ppermute | solution.py:35
  361.4 82.3 %collective-permute-start.11 = (bf16[1024,1024]{1,0:T(8,128)(2,1)}, bf16[1024,1024]{1,0:T(8,128)(2,1)}, u32[]{:S(2)}, u32[]{:S(2)}) collective-permute-start(bf16[1024,1024]{1,0:T(8,128)(2,1)} %get-tuple-element.34), channel_id=1, source_target_pairs={{2,0},{3,1},{0,2},{1,3},{6,4},{7,5},{4,6},{5,7},{10,8},{11,9},{8,1... | collective-permute-start | bytes 6291464 | tf_op jit(solution)/shard_map/ppermute | solution.py:35
  407.5 73.0 %collective-permute-start.20 = (bf16[896,1024]{1,0:T(8,128)(2,1)S(1)}, bf16[896,1024]{1,0:T(8,128)(2,1)S(1)}, u32[]{:S(2)}, u32[]{:S(2)}) collective-permute-start(bf16[896,1024]{1,0:T(8,128)(2,1)S(1)} %fusion.26), channel_id=1, source_target_pairs={{1,0},{0,1},{3,2},{2,3},{5,4},{4,5},{7,6},{6,7},{9,8},{8,9},{11,10... | collective-permute-start | bytes 5505032 | tf_op jit(solution)/shard_map/ppermute | solution.py:35
  408.2 88.7 %collective-permute-start.12 = (bf16[1024,1024]{1,0:T(8,128)(2,1)}, bf16[1024,1024]{1,0:T(8,128)(2,1)S(1)}, u32[]{:S(2)}, u32[]{:S(2)}) collective-permute-start(bf16[1024,1024]{1,0:T(8,128)(2,1)} %get-tuple-element.32), channel_id=1, source_target_pairs={{2,0},{3,1},{0,2},{1,3},{6,4},{7,5},{4,6},{5,7},{10,8},{11,9},{8,1... | collective-permute-start | bytes 6291464 | tf_op jit(solution)/shard_map/ppermute | solution.py:35
  538.8 54.1 %collective-permute-start.13 = (bf16[896,1024]{1,0:T(8,128)(2,1)S(1)}, bf16[896,1024]{1,0:T(8,128)(2,1)}, u32[]{:S(2)}, u32[]{:S(2)}) collective-permute-start(bf16[896,1024]{1,0:T(8,128)(2,1)S(1)} %split.74), channel_id=1, source_target_pairs={{1,0},{0,1},{3,2},{2,3},{5,4},{4,5},{7,6},{6,7},{9,8},{8,9},{11,10... | collective-permute-start | bytes 5505032 | tf_op jit(solution)/shard_map/ppermute | solution.py:35
  713.9 50.9 %all-to-all-start.1 = ((bf16[8,112,1024]{2,1,0:T(8,128)(2,1)}), bf16[8,112,1024]{2,1,0:T(8,128)(2,1)}, u32[]{:S(2)}, u32[]{:S(2)}) async-start(bf16[8,112,1024]{2,1,0:T(8,128)(2,1)} %bitcast.268), calls=%async_computation.1 | async-start | bytes 3670016 | tf_op jit(solution)/shard_map/all_to_all | solution.py:183
  738.6 84.8 %collective-permute-start.43 = (bf16[1024,1024]{1,0:T(8,128)(2,1)}, bf16[1024,1024]{1,0:T(8,128)(2,1)}, u32[]{:S(2)}, u32[]{:S(2)}) collective-permute-start(bf16[1024,1024]{1,0:T(8,128)(2,1)} %convolution_convert_fusion.3), channel_id=1, source_target_pairs={{2,0},{3,1},{0,2},{1,3},{6,4},{7,5},{4,6},{5,7},{10,8},{11,9},{8,1... | collective-permute-start | bytes 6291464 | tf_op jit(solution)/shard_map/ppermute | solution.py:35
  764.8 84.2 %all-to-all-start.3 = ((bf16[8,112,1024]{2,1,0:T(8,128)(2,1)}), bf16[8,112,1024]{2,1,0:T(8,128)(2,1)}, u32[]{:S(2)}, u32[]{:S(2)}) async-start(bf16[8,112,1024]{2,1,0:T(8,128)(2,1)} %bitcast.267), calls=%async_computation.3 | async-start | bytes 3670016 | tf_op jit(solution)/shard_map/all_to_all | solution.py:183
  769.1 627.1 %all-reduce.3.cloned.1.call-start = ((), (), s32[]{:S(2)}) async-start(), calls=%async_computation.5 | async-start | bytes 8388608 | tf_op jit(solution)/shard_map/psum | solution.py:332
  850.6 51.9 %collective-permute-start.24 = (bf16[448,1024]{1,0:T(8,128)(2,1)S(1)}, bf16[448,1024]{1,0:T(8,128)(2,1)S(1)}, u32[]{:S(2)}, u32[]{:S(2)}) collective-permute-start(bf16[448,1024]{1,0:T(8,128)(2,1)S(1)} %bitcast.283), channel_id=1, source_target_pairs={{1,0},{0,1},{3,2},{2,3},{5,4},{4,5},{7,6},{6,7},{9,8},{8,9},{11,10... | collective-permute-start | bytes 2752520 | tf_op jit(solution)/shard_map/ppermute | solution.py:35
  866.0 58.5 %collective-permute-start.26 = (bf16[448,1024]{1,0:T(8,128)(2,1)S(1)}, bf16[448,1024]{1,0:T(8,128)(2,1)S(1)}, u32[]{:S(2)}, u32[]{:S(2)}) collective-permute-start(bf16[448,1024]{1,0:T(8,128)(2,1)S(1)} %bitcast.284), channel_id=1, source_target_pairs={{2,0},{3,1},{0,2},{1,3},{6,4},{7,5},{4,6},{5,7},{10,8},{11,9},{8,1... | collective-permute-start | bytes 2752520 | tf_op jit(solution)/shard_map/ppermute | solution.py:35
  890.2 327.1 %collective-permute-start.44 = (bf16[1024,1024]{1,0:T(8,128)(2,1)}, bf16[1024,1024]{1,0:T(8,128)(2,1)}, u32[]{:S(2)}, u32[]{:S(2)}) collective-permute-start(bf16[1024,1024]{1,0:T(8,128)(2,1)} %convolution_convert_fusion.2), channel_id=1, source_target_pairs={{1,0},{0,1},{3,2},{2,3},{5,4},{4,5},{7,6},{6,7},{9,8},{8,9},{11,10... | collective-permute-start | bytes 6291464 | tf_op jit(solution)/shard_map/ppermute | solution.py:35
  924.5 62.2 %collective-permute-start.19 = (bf16[448,1024]{1,0:T(8,128)(2,1)S(1)}, bf16[448,1024]{1,0:T(8,128)(2,1)S(1)}, u32[]{:S(2)}, u32[]{:S(2)}) collective-permute-start(bf16[448,1024]{1,0:T(8,128)(2,1)S(1)} %collective-permute-done.17), channel_id=1, source_target_pairs={{1,0},{0,1},{3,2},{2,3},{5,4},{4,5},{7,6},{6,7},{9,8},{8,9},{11,10... | collective-permute-start | bytes 2752520 | tf_op jit(solution)/shard_map/ppermute | solution.py:35
  929.5 77.0 %collective-permute-start.29 = (bf16[448,1024]{1,0:T(8,128)(2,1)S(1)}, bf16[448,1024]{1,0:T(8,128)(2,1)S(1)}, u32[]{:S(2)}, u32[]{:S(2)}) collective-permute-start(bf16[448,1024]{1,0:T(8,128)(2,1)S(1)} %collective-permute-done.27), channel_id=1, source_target_pairs={{1,0},{0,1},{3,2},{2,3},{5,4},{4,5},{7,6},{6,7},{9,8},{8,9},{11,10... | collective-permute-start | bytes 2752520 | tf_op jit(solution)/shard_map/ppermute | solution.py:35
  949.2 288.1 %collective-permute-start.42 = (bf16[1024,1024]{1,0:T(8,128)(2,1)}, bf16[1024,1024]{1,0:T(8,128)(2,1)}, u32[]{:S(2)}, u32[]{:S(2)}) collective-permute-start(bf16[1024,1024]{1,0:T(8,128)(2,1)} %convolution_convert_fusion.4), channel_id=1, source_target_pairs={{1,0},{0,1},{3,2},{2,3},{5,4},{4,5},{7,6},{6,7},{9,8},{8,9},{11,10... | collective-permute-start | bytes 6291464 | tf_op jit(solution)/shard_map/ppermute | solution.py:35
  1293.1 65.9 %collective-permute-start.36 = (bf16[384,1024]{1,0:T(8,128)(2,1)}, bf16[384,1024]{1,0:T(8,128)(2,1)S(1)}, u32[]{:S(2)}, u32[]{:S(2)}) collective-permute-start(bf16[384,1024]{1,0:T(8,128)(2,1)} %get-tuple-element.42), channel_id=1, source_target_pairs={{1,0},{0,1},{3,2},{2,3},{5,4},{4,5},{7,6},{6,7},{9,8},{8,9},{11,10... | collective-permute-start | bytes 2359304 | tf_op jit(solution)/shard_map/ppermute | solution.py:35
  1293.6 67.7 %collective-permute-start.39 = (bf16[384,1024]{1,0:T(8,128)(2,1)}, bf16[384,1024]{1,0:T(8,128)(2,1)S(1)}, u32[]{:S(2)}, u32[]{:S(2)}) collective-permute-start(bf16[384,1024]{1,0:T(8,128)(2,1)} %get-tuple-element.41), channel_id=1, source_target_pairs={{2,0},{3,1},{0,2},{1,3},{6,4},{7,5},{4,6},{5,7},{10,8},{11,9},{8,1... | collective-permute-start | bytes 2359304 | tf_op jit(solution)/shard_map/ppermute | solution.py:35
  1297.9 65.0 %collective-permute-start.37 = (bf16[384,1024]{1,0:T(8,128)(2,1)}, bf16[384,1024]{1,0:T(8,128)(2,1)}, u32[]{:S(2)}, u32[]{:S(2)}) collective-permute-start(bf16[384,1024]{1,0:T(8,128)(2,1)} %get-tuple-element.41), channel_id=1, source_target_pairs={{1,0},{0,1},{3,2},{2,3},{5,4},{4,5},{7,6},{6,7},{9,8},{8,9},{11,10... | collective-permute-start | bytes 2359304 | tf_op jit(solution)/shard_map/ppermute | solution.py:35
  1299.3 65.7 %collective-permute-start.38 = (bf16[384,1024]{1,0:T(8,128)(2,1)}, bf16[384,1024]{1,0:T(8,128)(2,1)}, u32[]{:S(2)}, u32[]{:S(2)}) collective-permute-start(bf16[384,1024]{1,0:T(8,128)(2,1)} %get-tuple-element.42), channel_id=1, source_target_pairs={{2,0},{3,1},{0,2},{1,3},{6,4},{7,5},{4,6},{5,7},{10,8},{11,9},{8,1... | collective-permute-start | bytes 2359304 | tf_op jit(solution)/shard_map/ppermute | solution.py:35
  (105 other events, 3007.5 us)
Sparse Core Ops, SparseCore 0:
  115.9 50.9 all-gather.1
  1298.0 98.1 all-reduce.2

commit v2 on v1

--- a/solution.py
+++ b/solution.py
@@ -11,53 +11,109 @@
 BF16 = jnp.bfloat16
 
 
+CORES = 2
+
+
 class Grid:
-    def __init__(self, size):
-        inner = int(math.isqrt(size))
-        while size % inner:
-            inner -= 1
-        self.size = size
-        self.parts = {"x": inner, "y": size // inner}
-
-    def _pairs(self, axis, shift):
-        wide, tall = self.parts["x"], self.parts["y"]
-        pairs = []
-        for row in range(tall):
-            for col in range(wide):
-                if axis == "x":
-                    other = row * wide + (col + shift) % wide
-                else:
-                    other = ((row + shift) % tall) * wide + col
-                pairs.append((other, row * wide + col))
-        return pairs
-
-    def fetch(self, value, axis, shift=1):
-        return lax.ppermute(value, "tensor", self._pairs(axis, shift))
-
-    def gather_list(self, value, axis):
-        return [value] + [self.fetch(value, axis, s) for s in range(1, self.parts[axis])]
-
-    def scatter_list(self, parts, axis):
-        total = parts[0]
-        for s in range(1, self.parts[axis]):
-            total = total + self.fetch(parts[s].astype(BF16), axis, -s).astype(F32)
-        return total
-
-
-def gather_rows(grid, value):
+    def __init__(self, shards, experts):
+        self.size = shards
+        self.experts = experts
+        self.depth = experts // CORES
+
+    def over_core(self, value):
+        return lax.ppermute(value, "dp", [(d, d ^ 1) for d in range(self.experts)])
+
+    def over_tensor(self, value, other):
+        return lax.ppermute(value, "tensor", [(t, t ^ other) for t in range(self.size)])
+
+    def exchange_depth(self, value):
+        groups = [[CORES * z + c for z in range(self.depth)] for c in range(CORES)]
+        return lax.all_to_all(
+            value, "dp", split_axis=0, concat_axis=0, axis_index_groups=groups, tiled=True
+        )
+
+
+def slice_half(value, half, axis):
+    width = value.shape[axis] // 2
+    return lax.dynamic_slice_in_dim(value, half * width, width, axis)
+
+
+def owner_pairs(grid, flip, back=False):
+    pairs = []
+    for z in range(grid.depth):
+        for core in range(CORES):
+            for y in range(2):
+                for x in range(2):
+                    here = (CORES * z + core) * 4 + 2 * y + x
+                    there = (CORES * z + (x ^ flip)) * 4 + 2 * y + core
+                    pairs.append((there, here) if back else (here, there))
+    return pairs
+
+
+def fetch_halves(grid, weight, axis):
+    core = lax.axis_index("dp") % CORES
+    me = lax.axis_index("tensor")
+    if grid.size == 4:
+        near = [
+            lax.ppermute(
+                slice_half(weight, jnp.bitwise_xor(me % 2, flip), axis),
+                ("dp", "tensor"),
+                owner_pairs(grid, flip),
+            )
+            for flip in range(2)
+        ]
+        return near + [grid.over_tensor(piece, 2) for piece in near]
+    every = lax.all_gather(weight, "tensor", axis=0, tiled=False)
+    chosen = jnp.where(me % 2 == core, every, grid.over_core(every))
+    return [slice_half(chosen[t], core, axis) for t in range(grid.size)]
+
+
+def return_halves(grid, pieces, axis):
+    core = lax.axis_index("dp") % CORES
+    me = lax.axis_index("tensor")
+    if grid.size == 4:
+        halves = []
+        for flip in range(2):
+            far = grid.over_tensor(pieces[2 + flip].astype(BF16), 2)
+            total = pieces[flip] + far.astype(F32)
+            halves.append(
+                lax.ppermute(total.astype(BF16), ("dp", "tensor"), owner_pairs(grid, flip, True))
+            )
+        swapped = me % 2 == 1
+    else:
+        stacked = jnp.stack(pieces).astype(BF16)
+        wide = jnp.stack([jnp.where(me % 2 == p, stacked, jnp.zeros_like(stacked)) for p in range(2)])
+        mine = lax.psum_scatter(wide, "tensor", scatter_dimension=1, tiled=False)
+        halves = [
+            jnp.where(core == 0, mine[0], mine[1]),
+            grid.over_core(jnp.where(core == 0, mine[1], mine[0])),
+        ]
+        swapped = core == 1
+    halves = [half.astype(F32) for half in halves]
+    return jnp.where(swapped, jnp.concatenate(halves[::-1], axis), jnp.concatenate(halves, axis))
+
+
+def gather_rows(grid, value, balanced=True):
     if grid.size != 4:
         return lax.all_gather(value, "tensor", axis=0, tiled=False)
-    half = value.shape[0] // 2
     me = lax.axis_index("tensor")
-    first, second = value[:half], value[half:]
-    first_x = grid.fetch(first, "x")
-    second_y = grid.fetch(second, "y")
-    first_y = grid.fetch(first, "y")
-    second_x = grid.fetch(second, "x")
-    first_xy = grid.fetch(first_x, "y")
-    second_xy = grid.fetch(second_y, "x")
     out = jnp.zeros((4,) + value.shape, value.dtype)
     out = lax.dynamic_update_slice(out, value[None], (me, 0, 0))
+    if not balanced:
+        from_y = grid.over_tensor(value, 2)
+        from_x = grid.over_tensor(value, 1)
+        from_xy = grid.over_tensor(from_y, 1)
+        for other, piece in ((1, from_x), (2, from_y), (3, from_xy)):
+            out = lax.dynamic_update_slice(out, piece[None], (jnp.bitwise_xor(me, other), 0, 0))
+        return out
+    half = value.shape[0] // 2
+    first, second = value[:half], value[half:]
+    first_x = grid.over_tensor(first, 1)
+    second_y = grid.over_tensor(second, 2)
+    first_y = grid.over_tensor(first, 2)
+    second_x = grid.over_tensor(second, 1)
+    first_xy = grid.over_tensor(first_x, 2)
+    second_xy = grid.over_tensor(second_y, 1)
     for other, top, bottom in ((1, first_x, second_x), (2, first_y, second_y), (3, first_xy, second_xy)):
         place = jnp.bitwise_xor(me, other)
         out = lax.dynamic_update_slice(out, top[None], (place, 0, 0))
@@ -77,11 +133,11 @@
         return lax.dynamic_slice(term, (place, 0, low), (1, rows, half))[0]
 
     totals = []
-    for low, near, far, near_axis, far_axis in ((0, 1, 2, "x", "y"), (half, 2, 1, "y", "x")):
-        got_far = grid.fetch(pick(3, low).astype(BF16), near_axis)
-        got_own = grid.fetch(pick(near, low).astype(BF16), near_axis)
+    for low, near, far in ((0, 1, 2), (half, 2, 1)):
+        got_far = grid.over_tensor(pick(3, low).astype(BF16), near)
+        got_own = grid.over_tensor(pick(near, low).astype(BF16), near)
         onward = pick(far, low).astype(F32) + got_far.astype(F32)
-        got = grid.fetch(onward.astype(BF16), far_axis)
+        got = grid.over_tensor(onward.astype(BF16), far)
         totals.append(pick(0, low).astype(F32) + got_own.astype(F32) + got.astype(F32))
     return jnp.concatenate(totals, axis=1)
 
@@ -143,47 +199,48 @@
     head_size = out_weight.shape[1]
     experts = lax.axis_size("dp")
     shards = lax.axis_size("tensor")
-    grid = Grid(shards)
+    grid = Grid(shards, experts)
     me = lax.axis_index("tensor")
+    parity, part = me % 2, me // 2
+    core = lax.axis_index("dp") % CORES
+    depth = experts // CORES
+    row_parts = shards // 2
     capacity = (9 * tok_count + 8 * experts - 1) // (8 * experts)
-    share = 16 * -(-capacity // (16 * shards))
-    padded = share * shards
-    own_rows = experts * share
+    share = 16 * -(-capacity // (16 * row_parts))
+    padded = share * row_parts
+    own_rows = depth * share
     tok_rows = tok_count // shards
     score_scale = head_size ** (-0.5)
 
-    row_axis = ("y", "x")
-    weight_axis = ("x", "y")
-    win = [grid.gather_list(expert_in[0, k], weight_axis[k]) for k in range(2)]
-    wout = [grid.gather_list(expert_out[0, k], weight_axis[k]) for k in range(2)]
+    win, wout = [], []
+    for k in range(2):
+        win.append(fetch_halves(grid, expert_in[0, k], 1))
+        wout.append(fetch_halves(grid, expert_out[0, k], 0))
     out_flat = out_weight.reshape(heads_here * head_size, model_width)
-    out_all = lax.all_gather(out_flat, "tensor", axis=0, tiled=True)
+    out_all = gather_rows(grid, out_flat, False).reshape(shards * heads_here * head_size, model_width)
+    centroid = jnp.where(parity == core, centroids[0], grid.over_core(centroids[0]))
 
     slot_token, token_slot = plan_slots(
         routes, fill_order, lengths, seq_len, experts, capacity, padded
     )
-    own_slot = lax.dynamic_slice_in_dim(
-        slot_token.reshape(experts, padded), me * share, share, 1
+    own_slot = lax.dynamic_slice(
+        slot_token.reshape(depth, CORES, row_parts, share), (0, parity, part, 0), (depth, 1, 1, share)
     ).reshape(own_rows)
     own_filled = (own_slot < tok_count)[:, None]
     own_index = jnp.minimum(own_slot, tok_count - 1)
     kept = (token_slot < experts * padded)[:, None]
     tok_expert = jnp.minimum(token_slot // padded, experts - 1)
     tok_rank = token_slot % padded
-    tok_place = ((tok_rank // share) * experts + tok_expert) * share + tok_rank % share
+    tok_device = (tok_rank // share) * 2 + tok_expert % 2
+    tok_place = (tok_device * depth + tok_expert // 2) * share + tok_rank % share
 
     def to_experts(rows):
         picked = jnp.where(own_filled, rows[own_index], jnp.zeros((), rows.dtype))
-        moved = lax.all_to_all(
-            picked.reshape(experts, share, model_width), "dp", split_axis=0, concat_axis=0, tiled=True
-        )
-        return moved.reshape(own_rows, model_width)
-
-    def from_experts(rows):
-        moved = lax.all_to_all(
-            rows.reshape(experts, share, model_width), "dp", split_axis=0, concat_axis=0, tiled=True
-        )
-        every = gather_rows(grid, moved.reshape(own_rows, model_width))
+        return grid.exchange_depth(picked.reshape(depth, share, model_width)).reshape(own_rows, model_width)
+
+    def from_experts(rows, balanced):
+        moved = grid.exchange_depth(rows.reshape(depth, share, model_width))
+        every = gather_rows(grid, moved.reshape(own_rows, model_width), balanced)
         picked = every.reshape(shards * own_rows, model_width)[tok_place]
         return jnp.where(kept, picked, jnp.zeros((), rows.dtype)).astype(F32)
 
@@ -227,18 +284,23 @@
         preferred_element_type=F32,
     ).astype(BF16)
     attended = attended.reshape(tok_count, heads_here * head_size)
-    every_attended = gather_rows(grid, attended)
+    every_attended = gather_rows(grid, attended, False)
     attended_all = jnp.swapaxes(every_attended, 0, 1).reshape(tok_count, -1)
     mixed = input_rows + dot(attended_all, out_all, ((1,), (0,)))
     sent = mixed.astype(BF16)
 
+    def both_cores(value):
+        return jnp.concatenate([value, grid.over_core(value)], axis=0)
+
+    def sum_cores(total):
+        return total[:own_rows] + grid.over_core(total[own_rows:].astype(BF16)).astype(F32)
+
     expert_rows = to_experts(sent)
-    centroid = centroids[0]
     gate = jax.nn.sigmoid(jnp.dot(expert_rows, centroid, preferred_element_type=F32))[:, None]
     current = expert_rows.astype(F32)
     saved = []
     for k in range(2):
-        rows_in = jnp.concatenate(grid.gather_list(current.astype(BF16), row_axis[k]), axis=0)
+        rows_in = both_cores(current.astype(BF16))
         acts, slopes = [], []
         total = None
         for w_in, w_out in zip(win[k], wout[k]):
@@ -247,10 +309,9 @@
             total = term if total is None else total + term
             acts.append(act)
             slopes.append(slope)
-        parts = jnp.split(total, grid.parts[row_axis[k]], axis=0)
-        current = current + grid.scatter_list(parts, row_axis[k])
+        current = current + sum_cores(total)
         saved.append((rows_in, acts, slopes))
-    output = (mixed + from_experts((gate * current).astype(BF16))).astype(BF16)
+    output = (mixed + from_experts((gate * current).astype(BF16), False)).astype(BF16)
 
     grad_gate = jnp.sum(grad_ret * current, axis=1, keepdims=True)
     grad_logit = grad_gate * gate * (1.0 - gate)
@@ -259,7 +320,7 @@
     grads_back = [None, None]
     for k in (1, 0):
         rows_in, acts, slopes = saved[k]
-        branch = jnp.concatenate(grid.gather_list(grad_current.astype(BF16), row_axis[k]), axis=0)
+        branch = both_cores(grad_current.astype(BF16))
         total = None
         in_parts, out_parts = [], []
         for w_in, w_out, act, slope in zip(win[k], wout[k], acts, slopes):
@@ -268,15 +329,17 @@
             total = term if total is None else total + term
             out_parts.append(dot(act, branch, ((0,), (0,))))
             in_parts.append(dot(rows_in, grad_pre, ((0,), (0,))))
-        parts = jnp.split(total, grid.parts[row_axis[k]], axis=0)
-        grad_current = grad_current + grid.scatter_list(parts, row_axis[k])
-        grads_in[k] = grid.scatter_list(in_parts, weight_axis[k])
-        grads_back[k] = grid.scatter_list(out_parts, weight_axis[k])
+        grad_current = grad_current + sum_cores(total)
+        grads_in[k] = return_halves(grid, in_parts, 1)
+        grads_back[k] = return_halves(grid, out_parts, 0)
     grad_rows = (grad_current + grad_logit * centroid.astype(F32)[None, :]).astype(BF16)
-    grad_centroid = lax.psum(
-        jnp.sum(grad_logit * expert_rows.astype(F32), axis=0, keepdims=True), "tensor"
-    )
-    grad_mixed = cotangent.astype(F32) + from_experts(grad_rows)
+    centroid_part = jnp.sum(grad_logit * expert_rows.astype(F32), axis=0, keepdims=True)
+    centroid_parts = lax.psum(
+        jnp.concatenate([jnp.where(parity == p, centroid_part, 0.0) for p in range(2)], axis=0), "tensor"
+    )
+    centroid_parts = centroid_parts + grid.over_core(centroid_parts)
+    grad_centroid = lax.dynamic_slice_in_dim(centroid_parts, core, 1, 0)
+    grad_mixed = cotangent.astype(F32) + from_experts(grad_rows, True)
 
     grad_attn = grad_mixed.astype(BF16)
     grad_out_local = dot(attended, grad_attn, ((0,), (0,))).reshape(

time: 1420 us -> 1450 us (1.021)
  waiting for transfers between devices: 494 us -> 330 us
  matrix products: 350 us -> 411 us
  blocking collectives: 60.2 us -> 110 us
  starting transfers between devices: 79.7 us -> 122 us
  other arithmetic: 150 us -> 174 us
    ppermute x46 -> x69, waiting for transfers between devices: 439 us -> 279 us  [the longest x43 244 us: over_tensor(): lax.ppermute(value, 'tensor', [(t, t ^ other) for t in range(self.size)])]
    dot_general x27 -> x51, matrix products: 207 us -> 269 us  [dot(): lax.dot_general(a, b, (contract, ((), ())), preferred_element_type=F32)]
    ppermute x46 -> x69, starting transfers between devices: 58.3 us -> 108 us  [the longest x43 48.4 us: over_tensor(): lax.ppermute(value, 'tensor', [(t, t ^ other) for t in range(self.size)])]
    all_to_all x0 -> x1, blocking collectives: none -> 45.4 us  [exchange_depth(): lax.all_to_all(value, 'dp', split_axis=0, concat_axis=0, axis_index_group...]
    dynamic_update_slice x0 -> x9, local copies, waits for them, and re-layouts: none -> 16.5 us  [gather_rows(): lax.dynamic_update_slice(out, piece[None], (jnp.bitwise_xor(me, other), 0...]
    unnamed x158 -> x249, local copies, waits for them, and re-layouts: 26.7 us -> 33 us
    all_to_all x4 -> x3, waiting for transfers between devices: 38.5 us -> 33.7 us  [exchange_depth(): lax.all_to_all(value, 'dp', split_axis=0, concat_axis=0, axis_index_group...]
  transfers between devices with their start and end apart: 52 -> 73, of which waited for: 31 -> 23; matrix products, arithmetic and copies ran while one was open for 37% -> 46% of each run, Pallas kernels for 0% -> 0%
where the time goes in v2:
time: 1450 us; the launch traced here: 1440 us
  matrix products  411 us (28%)
  waiting for transfers between devices  330 us (23%)
  local copies, waits for them, and re-layouts  272 us (19%)
  other arithmetic  174 us (12%)
  starting transfers between devices  122 us (8%)
  blocking collectives  110 us (8%)
  between operations  16.4 us (1%)
    dot_general x51, matrix products, dot(): lax.dot_general(a, b, (contract, ((), ())), preferred_element_type=F32)  269 us
    ppermute x43, waiting for transfers between devices, over_tensor(): lax.ppermute(value, 'tensor', [(t, t ^ other) for t in range(self.size)])  244 us
    ppermute x43, starting transfers between devices, over_tensor(): lax.ppermute(value, 'tensor', [(t, t ^ other) for t in range(self.size)])  48.4 us
    psum x1, blocking collectives, body(): lax.psum(norm_parts, ('dp', 'tensor'))  47.8 us
    all_to_all x1, blocking collectives, exchange_depth(): lax.all_to_all(value, 'dp', split_axis=0, concat_axis=0, axis_index_group...  45.4 us
    convert_element_type x1, other arithmetic, body(): grad_scores = (attention_weights * (grad_probs - row_delta)).astype(BF16)  42.4 us
    gather x2, local copies, waits for them, and re-layouts, from_experts(): picked = every.reshape(shards * own_rows, model_width)[tok_place]  39.8 us
    dot_general x1, matrix products, body(): jnp.einsum('sqhd,skhd->shqk', grad_attended, values, preferred_element_ty...  36.9 us
  transfers between devices with their start and end apart: 73, of which 23 were waited for; matrix products, arithmetic and copies ran while one was open for 46% of the time, Pallas kernels for 0%

profile of v2, /device:TPU:0, one launch (start us, length us, event | category | flops | bytes accessed | tf_op | source)
XLA Modules:
  0.0 1437.1 jit_solution(9105231222505089362)
XLA Ops:
  46.1 19.2 %fusion = (f32[3,4,1024]{2,1,0:T(4,128)S(1)}, f32[3,4,1024,1024]{2,3,1,0:T(8,128)}) fusion(pred[3,1024,1024]{1,2,0:T(8,128)(4,1)S(1)} %broadcast_and_fusion, bf16[3,1024,4,64]{1,0,3,2:T(4,128)(2,1)S(1)} %get-tuple-element.31, bf16[3,1024,4,64]{1,0,3,2:T(4,128)(2,1)S(1)} %get-tuple-element.29), kind=kOutput, calls=%fused_computation.13 | convolution fusion | flops 1648349184 | bytes 56672256 | tf_op jit(solution)/shard_map/sqhd,skhd->shqk/dot_general | solution.py:268
  65.3 21.2 %exponential_reduce_fusion = f32[3,4,1024]{2,1,0:T(4,128)S(1)} fusion(f32[3,4,1024,1024]{2,3,1,0:T(8,128)} %get-tuple-element.62, f32[3,4,1024]{2,1,0:T(4,128)S(1)} %get-tuple-element.61, pred[3,1024,1024]{1,2,0:T(8,128)(4,1)S(1)} %broadcast_and_fusion), kind=kLoop, calls=%fused_computation.11 | loop fusion | flops 50319360 | bytes 53575680 | tf_op jit(solution)/shard_map/reduce_sum | solution.py:275
  86.5 20.1 %fusion.61 = bf16[3,1024,4,64]{1,3,2,0:T(8,128)(2,1)S(1)} fusion(bf16[3,1024,4,64]{1,0,3,2:T(4,128)(2,1)S(1)} %get-tuple-element.30, f32[3,4,1024,1024]{2,3,1,0:T(8,128)} %get-tuple-element.62, f32[3,4,1024]{2,1,0:T(4,128)S(1)} %log_add_fusion, pred[3,1024,1024]{1,2,0:T(8,128)(4,1)S(1)} %broadcast_and_fusion), kind=kOutput, calls=%fused_computation.174 | convolution fusion | flops 1661730816 | bytes 56672256 | tf_op jit(solution)/shard_map/shqk,skhd->sqhd/dot_general | solution.py:280
  114.7 19.4 %gather_fusion = pred[3072]{0:T(1024)(128)(4,1)S(1)} fusion(pred[3072]{0:T(1024)(128)(4,1)S(1)} %fusion.82, s32[3072]{0:T(1024)S(1)} %broadcast_clamp_fusion), kind=kCustom, calls=%fused_computation | custom fusion | bytes 18432 | tf_op jit(solution)/shard_map/gather | solution.py:159
  134.0 17.4 %gather_fusion.1 = s32[3072]{0:T(1024)S(1)} fusion(s32[3072]{0:T(1024)S(1)} %bitcast.301, s32[3072]{0:T(1024)S(1)} %broadcast_clamp_fusion), kind=kCustom, calls=%fused_computation.1 | custom fusion | bytes 36864 | tf_op jit(solution)/shard_map/gather | solution.py:158
  210.1 20.0 %collective-permute-done.2 = bf16[3072,256]{0,1:T(8,128)(2,1)} collective-permute-done((bf16[3072,256]{0,1:T(8,128)(2,1)}, bf16[3072,256]{0,1:T(8,128)(2,1)}, u32[]{:S(2)}, u32[]{:S(2)}) %collective-permute-start.2) | collective-permute-done | bytes 1572896 | tf_op jit(solution)/shard_map/ppermute | solution.py:27
  233.1 13.9 fusion.2
  259.5 45.4 %all_to_all.20 = bf16[4,224,1024]{2,1,0:T(8,128)(2,1)S(1)} all-to-all(bf16[4,224,1024]{2,1,0:T(8,128)(2,1)S(1)} %get-tuple-element.59), channel_id=1, replica_groups={{0,8,16,24},{4,12,20,28},{1,9,17,25},{5,13,21,29},{2,10,18,26},{6,14,22..., dimensions={0} | all-to-all | bytes 3670016 | tf_op jit(solution)/shard_map/all_to_all | solution.py:31
  327.6 30.1 %collective-permute-done.11 = bf16[512,1024]{1,0:T(8,128)(2,1)S(1)} collective-permute-done((bf16[512,1024]{1,0:T(8,128)(2,1)S(1)}, bf16[512,1024]{1,0:T(8,128)(2,1)S(1)}, u32[]{:S(2)}, u32[]{:S(2)}) %collective-permute-start.11) | collective-permute-done | bytes 1048608 | tf_op jit(solution)/shard_map/ppermute | solution.py:58
  501.8 47.6 %collective-permute-done.22 = bf16[1024,512]{1,0:T(8,128)(2,1)S(1)} collective-permute-done((bf16[1024,512]{1,0:T(8,128)(2,1)}, bf16[1024,512]{1,0:T(8,128)(2,1)S(1)}, u32[]{:S(2)}, u32[]{:S(2)}) %collective-permute-start.22) | collective-permute-done | bytes 1048608 | tf_op jit(solution)/shard_map/ppermute | solution.py:27
  764.4 17.4 %psum.31 = f32[2,1024]{1,0:T(2,128)S(1)} all-reduce(f32[2,1024]{1,0:T(2,128)S(1)} %pad_maximum_fusion.7), channel_id=1, replica_groups=mesh['dp'=8,'tensor'=4] {'tensor'}, use_global_device_ids=true, to_apply=%region_19.20 | all-reduce | flops 2048 | bytes 16384 | tf_op jit(solution)/shard_map/psum | solution.py:337
  816.6 21.5 %all-to-all-done.1 = bf16[4,224,1024]{2,1,0:T(8,128)(2,1)} async-done(((bf16[4,224,1024]{2,1,0:T(8,128)(2,1)}), bf16[4,224,1024]{2,1,0:T(8,128)(2,1)}, u32[]{:S(2)}, u32[]{:S(2)}) %all-to-all-start.1) | async-done | bytes 1835040 | tf_op jit(solution)/shard_map/all_to_all | solution.py:31
  857.7 15.7 %collective-permute-done.53 = bf16[1024,512]{1,0:T(8,128)(2,1)S(1)} collective-permute-done((bf16[1024,512]{1,0:T(8,128)(2,1)S(1)}, bf16[1024,512]{1,0:T(8,128)(2,1)S(1)}, u32[]{:S(2)}, u32[]{:S(2)}) %collective-permute-start.53) | collective-permute-done | bytes 1048608 | tf_op jit(solution)/shard_map/ppermute | solution.py:27
  878.1 17.8 %collective-permute-done.55 = bf16[1024,512]{1,0:T(8,128)(2,1)S(1)} collective-permute-done((bf16[1024,512]{1,0:T(8,128)(2,1)S(1)}, bf16[1024,512]{1,0:T(8,128)(2,1)S(1)}, u32[]{:S(2)}, u32[]{:S(2)}) %collective-permute-start.55) | collective-permute-done | bytes 1048608 | tf_op jit(solution)/shard_map/ppermute | solution.py:27
  948.3 48.8 %collective-permute-done.37 = bf16[448,1024]{1,0:T(8,128)(2,1)S(1)} collective-permute-done((bf16[448,1024]{1,0:T(8,128)(2,1)S(1)}, bf16[448,1024]{1,0:T(8,128)(2,1)S(1)}, u32[]{:S(2)}, u32[]{:S(2)}) %collective-permute-start.37) | collective-permute-done | bytes 917536 | tf_op jit(solution)/shard_map/ppermute | solution.py:27
  1026.8 19.9 %gather_fusion.5 = bf16[3072,1024]{1,0:T(8,128)(2,1)} fusion(bf16[3584,1024]{1,0:T(8,128)(2,1)} %bitcast.52, s32[3072]{0:T(1024)S(1)} %copy-done.51), kind=kCustom, calls=%fused_computation.5 | custom fusion | bytes 12595200 | tf_op jit(solution)/shard_map/gather | solution.py:244
  1063.2 19.9 %gather_fusion.3 = bf16[3072,1024]{1,0:T(8,128)(2,1)} fusion(bf16[3584,1024]{1,0:T(8,128)(2,1)} %bitcast.302, s32[3072]{0:T(1024)S(1)} %copy-done.51), kind=kCustom, calls=%fused_computation.3 | custom fusion | bytes 12595200 | tf_op jit(solution)/shard_map/gather | solution.py:244
  1083.1 17.3 %convert_add_fusion.1 = (f32[3072,1024]{1,0:T(8,128)S(1)}, bf16[3072,1024]{1,0:T(8,128)(2,1)}) fusion(bf16[3072,1024]{1,0:T(8,128)(2,1)} %param.23, bf16[3072,1024]{1,0:T(8,128)(2,1)} %gather_fusion.5, pred[3072]{0:T(1024)(128)(4,1)S(1)} %copy-done.64, bf16[3072,1024]{1,0:T(8,128)(2,1)} %gather_fusion.3, f32[3072,1024,1]{1,0,2:T(8,128)} %get-tuple-element.64, ...), kind=kLoop, calls=%fused_computation.19 | loop fusion | flops 31457280 | bytes 56626176 | tf_op jit(solution)/shard_map/add | solution.py:342
  1115.0 36.9 %multiply_reduce_fusion = (f32[3,4,1024]{2,1,0:T(4,128)S(1)}, f32[3,4,1024,1024]{2,3,1,0:T(8,128)}) fusion(f32[3,4,1024,1024]{2,3,1,0:T(8,128)} %get-tuple-element.62, f32[3,4,1024]{2,1,0:T(4,128)S(1)} %copy-done.43, pred[3,1024,1024]{1,2,0:T(8,128)(4,1)} %copy-done.4, bf16[3,1024,4,64]{1,3,2,0:T(8,128)(2,1)S(1)} %copy.59, ...), kind=kOutput, calls=%fused_computation.9 | convolution fusion | flops 1673515008 | bytes 107053056 | tf_op jit(solution)/shard_map/sqhd,skhd->shqk/dot_general | solution.py:351
  1151.9 42.4 %multiply_convert_fusion = bf16[3,4,1024,1024]{2,3,1,0:T(8,128)(2,1)} fusion(f32[3,4,1024,1024]{2,3,1,0:T(8,128)} %get-tuple-element.82, f32[3,4,1024,1024]{2,3,1,0:T(8,128)} %get-tuple-element.62, f32[3,4,1024]{2,1,0:T(4,128)S(1)} %get-tuple-element.81, f32[3,4,1024]{2,1,0:T(4,128)S(1)} %copy-done.43, pred[3,1024,1024]{1,2,0:T(8,128)(4,1)} %copy-done.4), kind=kLoop, calls=%fused_computation.8 | loop fusion | flops 75497472 | bytes 129073152 | tf_op jit(solution)/shard_map/convert_element_type | solution.py:355
  1207.9 14.0 fusion.64
  1221.9 20.4 %fusion.62 = bf16[3,1024,4,64]{1,3,2,0:T(8,128)(2,1)S(1)} fusion(bf16[3,1024,4,64]{1,3,2,0:T(8,128)(2,1)} %copy-done.12, f32[3,4,1024,1024]{2,3,1,0:T(8,128)} %get-tuple-element.62, f32[3,4,1024]{2,1,0:T(4,128)S(1)} %copy-done.43, pred[3,1024,1024]{1,2,0:T(8,128)(4,1)} %copy-done.4), kind=kOutput, calls=%fused_computation.175 | convolution fusion | flops 1661730816 | bytes 56672256 | tf_op jit(solution)/shard_map/shqk,sqhd->skhd/dot_general | solution.py:364
  1337.3 47.8 %psum.28 = f32[2,1024]{1,0:T(2,128)S(1)} all-reduce(f32[2,1024]{1,0:T(2,128)S(1)} %pad_maximum_fusion.6), channel_id=1, replica_groups=mesh['dp'=8,'tensor'=4] {'dp','tensor'}, use_global_device_ids=true, to_apply=%region_15.16 | all-reduce | flops 2048 | bytes 16384 | tf_op jit(solution)/shard_map/psum | solution.py:393
  1407.4 17.4 %all-reduce.3.cloned.1.call-done = (f32[1024,4,192]{0,2,1:T(8,128)}, f32[4,64,1024]{2,1,0:T(8,128)}) async-done(((f32[1024,4,192]{0,2,1:T(8,128)}, f32[4,64,1024]{2,1,0:T(8,128)}), (f32[1024,4,192]{0,2,1:T(8,128)}, f32[4,64,1024]{2,1,0:T(8,128)})) %all-reduce.3.cloned.1.call-update) | async-done | bytes 4194320 | tf_op jit(solution)/shard_map/psum | solution.py:395
  (573 shorter events, 809.2 us)
Async XLA Ops:
  108.8 93.8 %collective-permute-start = (bf16[3072,256]{0,1:T(8,128)(2,1)S(1)}, bf16[3072,256]{0,1:T(8,128)(2,1)}, u32[]{:S(2)}, u32[]{:S(2)}) collective-permute-start(bf16[3072,256]{0,1:T(8,128)(2,1)S(1)} %bitcast.319), channel_id=1, source_target_pairs={{0,1},{1,0},{2,3},{3,2},{4,5},{5,4},{6,7},{7,6},{8,9},{9,8},{10,11... | collective-permute-start | bytes 4718600 | tf_op jit(solution)/shard_map/ppermute | solution.py:27
  111.8 73.4 %collective-permute-start.1 = (bf16[3072,256]{0,1:T(8,128)(2,1)S(1)}, bf16[3072,256]{0,1:T(8,128)(2,1)}, u32[]{:S(2)}, u32[]{:S(2)}) collective-permute-start(bf16[3072,256]{0,1:T(8,128)(2,1)S(1)} %bitcast.320), channel_id=1, source_target_pairs={{0,2},{1,3},{2,0},{3,1},{4,6},{5,7},{6,4},{7,5},{8,10},{9,11},{10,... | collective-permute-start | bytes 4718600 | tf_op jit(solution)/shard_map/ppermute | solution.py:27
  113.4 83.7 %collective-permute-start.3 = (bf16[256,1024]{1,0:T(8,128)(2,1)}, bf16[256,1024]{1,0:T(8,128)(2,1)}, u32[]{:S(2)}, u32[]{:S(2)}) collective-permute-start(bf16[256,1024]{1,0:T(8,128)(2,1)} %bitcast.8), channel_id=1, source_target_pairs={{0,1},{1,0},{2,3},{3,2},{4,5},{5,4},{6,7},{7,6},{8,9},{9,8},{10,11... | collective-permute-start | bytes 1572872 | tf_op jit(solution)/shard_map/ppermute | solution.py:27
  113.9 69.3 %collective-permute-start.4 = (bf16[256,1024]{1,0:T(8,128)(2,1)}, bf16[256,1024]{1,0:T(8,128)(2,1)}, u32[]{:S(2)}, u32[]{:S(2)}) collective-permute-start(bf16[256,1024]{1,0:T(8,128)(2,1)} %bitcast.8), channel_id=1, source_target_pairs={{0,2},{1,3},{2,0},{3,1},{4,6},{5,7},{6,4},{7,5},{8,10},{9,11},{10,... | collective-permute-start | bytes 1572872 | tf_op jit(solution)/shard_map/ppermute | solution.py:27
  324.0 76.2 %collective-permute-start.14 = (bf16[1024,512]{1,0:T(8,128)(2,1)S(1)}, bf16[1024,512]{1,0:T(8,128)(2,1)S(1)}, u32[]{:S(2)}, u32[]{:S(2)}) collective-permute-start(bf16[1024,512]{1,0:T(8,128)(2,1)S(1)} %collective-permute-done.10), channel_id=1, source_target_pairs={{0,2},{1,3},{2,0},{3,1},{4,6},{5,7},{6,4},{7,5},{8,10},{9,11},{10,... | collective-permute-start | bytes 3145736 | tf_op jit(solution)/shard_map/ppermute | solution.py:27
  326.1 69.0 %collective-permute-start.13 = (bf16[512,1024]{1,0:T(8,128)(2,1)S(1)}, bf16[512,1024]{1,0:T(8,128)(2,1)S(1)}, u32[]{:S(2)}, u32[]{:S(2)}) collective-permute-start(bf16[512,1024]{1,0:T(8,128)(2,1)S(1)} %collective-permute-done.9), channel_id=1, source_target_pairs={{0,2},{1,3},{2,0},{3,1},{4,6},{5,7},{6,4},{7,5},{8,10},{9,11},{10,... | collective-permute-start | bytes 3145736 | tf_op jit(solution)/shard_map/ppermute | solution.py:27
  478.2 114.4 %collective-permute-start.24 = (bf16[1024,512]{1,0:T(8,128)(2,1)}, bf16[1024,512]{1,0:T(8,128)(2,1)S(1)}, u32[]{:S(2)}, u32[]{:S(2)}) collective-permute-start(bf16[1024,512]{1,0:T(8,128)(2,1)} %collective-permute-done.20), channel_id=1, source_target_pairs={{0,2},{1,3},{2,0},{3,1},{4,6},{5,7},{6,4},{7,5},{8,10},{9,11},{10,... | collective-permute-start | bytes 3145736 | tf_op jit(solution)/shard_map/ppermute | solution.py:27
  479.8 119.0 %collective-permute-start.25 = (bf16[512,1024]{1,0:T(8,128)(2,1)}, bf16[512,1024]{1,0:T(8,128)(2,1)S(1)}, u32[]{:S(2)}, u32[]{:S(2)}) collective-permute-start(bf16[512,1024]{1,0:T(8,128)(2,1)} %collective-permute-done.21), channel_id=1, source_target_pairs={{0,2},{1,3},{2,0},{3,1},{4,6},{5,7},{6,4},{7,5},{8,10},{9,11},{10,... | collective-permute-start | bytes 3145736 | tf_op jit(solution)/shard_map/ppermute | solution.py:27
  480.3 69.1 %collective-permute-start.22 = (bf16[1024,512]{1,0:T(8,128)(2,1)}, bf16[1024,512]{1,0:T(8,128)(2,1)S(1)}, u32[]{:S(2)}, u32[]{:S(2)}) collective-permute-start(bf16[1024,512]{1,0:T(8,128)(2,1)} %collective-permute-done.18), channel_id=1, source_target_pairs={{0,2},{1,3},{2,0},{3,1},{4,6},{5,7},{6,4},{7,5},{8,10},{9,11},{10,... | collective-permute-start | bytes 3145736 | tf_op jit(solution)/shard_map/ppermute | solution.py:27
  481.8 89.6 %collective-permute-start.23 = (bf16[512,1024]{1,0:T(8,128)(2,1)}, bf16[512,1024]{1,0:T(8,128)(2,1)S(1)}, u32[]{:S(2)}, u32[]{:S(2)}) collective-permute-start(bf16[512,1024]{1,0:T(8,128)(2,1)} %collective-permute-done.19), channel_id=1, source_target_pairs={{0,2},{1,3},{2,0},{3,1},{4,6},{5,7},{6,4},{7,5},{8,10},{9,11},{10,... | collective-permute-start | bytes 3145736 | tf_op jit(solution)/shard_map/ppermute | solution.py:27
  684.4 73.9 %collective-permute-start.57 = (bf16[1024,512]{1,0:T(8,128)(2,1)}, bf16[1024,512]{1,0:T(8,128)(2,1)}, u32[]{:S(2)}, u32[]{:S(2)}) collective-permute-start(bf16[1024,512]{1,0:T(8,128)(2,1)} %convolution_convert_fusion.8), channel_id=1, source_target_pairs={{0,2},{1,3},{2,0},{3,1},{4,6},{5,7},{6,4},{7,5},{8,10},{9,11},{10,... | collective-permute-start | bytes 3145736 | tf_op jit(solution)/shard_map/ppermute | solution.py:27
  690.7 103.9 %collective-permute-start.59 = (bf16[1024,512]{1,0:T(8,128)(2,1)}, bf16[1024,512]{1,0:T(8,128)(2,1)}, u32[]{:S(2)}, u32[]{:S(2)}) collective-permute-start(bf16[1024,512]{1,0:T(8,128)(2,1)} %convolution_convert_fusion.7), channel_id=1, source_target_pairs={{0,2},{1,3},{2,0},{3,1},{4,6},{5,7},{6,4},{7,5},{8,10},{9,11},{10,... | collective-permute-start | bytes 3145736 | tf_op jit(solution)/shard_map/ppermute | solution.py:27
  694.7 106.2 %collective-permute-start.66 = (bf16[512,1024]{1,0:T(8,128)(2,1)}, bf16[512,1024]{1,0:T(8,128)(2,1)}, u32[]{:S(2)}, u32[]{:S(2)}) collective-permute-start(bf16[512,1024]{1,0:T(8,128)(2,1)} %add_convert_fusion.4), channel_id=1, source_target_pairs={{4,0},{0,1},{6,2},{2,3},{5,4},{1,5},{7,6},{3,7},{12,8},{8,9},{14,1... | collective-permute-start | bytes 3145736 | tf_op jit(solution)/shard_map/ppermute | solution.py:80
  815.4 90.2 %collective-permute-start.61 = (bf16[512,1024]{1,0:T(8,128)(2,1)}, bf16[512,1024]{1,0:T(8,128)(2,1)}, u32[]{:S(2)}, u32[]{:S(2)}) collective-permute-start(bf16[512,1024]{1,0:T(8,128)(2,1)} %convolution_convert_fusion.6), channel_id=1, source_target_pairs={{0,2},{1,3},{2,0},{3,1},{4,6},{5,7},{6,4},{7,5},{8,10},{9,11},{10,... | collective-permute-start | bytes 3145736 | tf_op jit(solution)/shard_map/ppermute | solution.py:27
  842.5 582.3 %all-reduce.3.cloned.1.call-start = ((), (), s32[]{:S(2)}) async-start(), calls=%async_computation.4 | async-start | bytes 8388608 | tf_op jit(solution)/shard_map/psum | solution.py:395
  900.5 96.5 %collective-permute-start.28 = (bf16[896,1024]{1,0:T(8,128)(2,1)}, bf16[896,1024]{1,0:T(8,128)(2,1)}, u32[]{:S(2)}, u32[]{:S(2)}) collective-permute-start(bf16[896,1024]{1,0:T(8,128)(2,1)} %bitcast.34), channel_id=1, source_target_pairs={{0,2},{1,3},{2,0},{3,1},{4,6},{5,7},{6,4},{7,5},{8,10},{9,11},{10,... | collective-permute-start | bytes 5505032 | tf_op jit(solution)/shard_map/ppermute | solution.py:27
  910.4 89.7 %collective-permute-start.36 = (bf16[448,1024]{1,0:T(8,128)(2,1)S(1)}, bf16[448,1024]{1,0:T(8,128)(2,1)S(1)}, u32[]{:S(2)}, u32[]{:S(2)}) collective-permute-start(bf16[448,1024]{1,0:T(8,128)(2,1)S(1)} %bitcast.336), channel_id=1, source_target_pairs={{0,2},{1,3},{2,0},{3,1},{4,6},{5,7},{6,4},{7,5},{8,10},{9,11},{10,... | collective-permute-start | bytes 2752520 | tf_op jit(solution)/shard_map/ppermute | solution.py:27
  918.5 78.5 %collective-permute-start.37 = (bf16[448,1024]{1,0:T(8,128)(2,1)S(1)}, bf16[448,1024]{1,0:T(8,128)(2,1)S(1)}, u32[]{:S(2)}, u32[]{:S(2)}) collective-permute-start(bf16[448,1024]{1,0:T(8,128)(2,1)S(1)} %bitcast.338), channel_id=1, source_target_pairs={{0,2},{1,3},{2,0},{3,1},{4,6},{5,7},{6,4},{7,5},{8,10},{9,11},{10,... | collective-permute-start | bytes 2752520 | tf_op jit(solution)/shard_map/ppermute | solution.py:27
  926.8 119.9 %collective-permute-start.27 = (bf16[896,1024]{1,0:T(8,128)(2,1)}, bf16[896,1024]{1,0:T(8,128)(2,1)S(1)}, u32[]{:S(2)}, u32[]{:S(2)}) collective-permute-start(bf16[896,1024]{1,0:T(8,128)(2,1)} %bitcast.34), channel_id=1, source_target_pairs={{0,1},{1,0},{2,3},{3,2},{4,5},{5,4},{6,7},{7,6},{8,9},{9,8},{10,11... | collective-permute-start | bytes 5505032 | tf_op jit(solution)/shard_map/ppermute | solution.py:27
  946.5 68.9 %collective-permute-start.38 = (bf16[448,1024]{1,0:T(8,128)(2,1)S(1)}, bf16[448,1024]{1,0:T(8,128)(2,1)S(1)}, u32[]{:S(2)}, u32[]{:S(2)}) collective-permute-start(bf16[448,1024]{1,0:T(8,128)(2,1)S(1)} %collective-permute-done.34), channel_id=1, source_target_pairs={{0,2},{1,3},{2,0},{3,1},{4,6},{5,7},{6,4},{7,5},{8,10},{9,11},{10,... | collective-permute-start | bytes 2752520 | tf_op jit(solution)/shard_map/ppermute | solution.py:27
  1000.1 252.5 %collective-permute-start.62 = (bf16[512,1024]{1,0:T(8,128)(2,1)}, bf16[512,1024]{1,0:T(8,128)(2,1)}, u32[]{:S(2)}, u32[]{:S(2)}) collective-permute-start(bf16[512,1024]{1,0:T(8,128)(2,1)} %add_convert_fusion.6), channel_id=1, source_target_pairs={{4,0},{0,1},{6,2},{2,3},{5,4},{1,5},{7,6},{3,7},{12,8},{8,9},{14,1... | collective-permute-start | bytes 3145736 | tf_op jit(solution)/shard_map/ppermute | solution.py:80
  1015.4 239.5 %collective-permute-start.64 = (bf16[512,1024]{1,0:T(8,128)(2,1)}, bf16[512,1024]{1,0:T(8,128)(2,1)}, u32[]{:S(2)}, u32[]{:S(2)}) collective-permute-start(bf16[512,1024]{1,0:T(8,128)(2,1)} %add_convert_fusion.5), channel_id=1, source_target_pairs={{0,0},{4,1},{2,2},{6,3},{1,4},{5,5},{3,6},{7,7},{8,8},{12,9},{10,1... | collective-permute-start | bytes 3145736 | tf_op jit(solution)/shard_map/ppermute | solution.py:80
  1025.8 230.5 %collective-permute-start.54 = (bf16[1024,512]{1,0:T(8,128)(2,1)}, bf16[1024,512]{1,0:T(8,128)(2,1)}, u32[]{:S(2)}, u32[]{:S(2)}) collective-permute-start(bf16[1024,512]{1,0:T(8,128)(2,1)} %add_convert_fusion.10), channel_id=1, source_target_pairs={{4,0},{0,1},{6,2},{2,3},{5,4},{1,5},{7,6},{3,7},{12,8},{8,9},{14,1... | collective-permute-start | bytes 3145736 | tf_op jit(solution)/shard_map/ppermute | solution.py:80
  1046.7 227.9 %collective-permute-start.56 = (bf16[1024,512]{1,0:T(8,128)(2,1)}, bf16[1024,512]{1,0:T(8,128)(2,1)}, u32[]{:S(2)}, u32[]{:S(2)}) collective-permute-start(bf16[1024,512]{1,0:T(8,128)(2,1)} %add_convert_fusion.9), channel_id=1, source_target_pairs={{0,0},{4,1},{2,2},{6,3},{1,4},{5,5},{3,6},{7,7},{8,8},{12,9},{10,1... | collective-permute-start | bytes 3145736 | tf_op jit(solution)/shard_map/ppermute | solution.py:80
  (171 other events, 3479.6 us)
Sparse Core Ops, SparseCore 0:
  1326.5 98.3 all-reduce.2

commit v3 on v2

v3 whole, which is shorter than its diff:
```python
import functools
import math

import jax
import jax.numpy as jnp
from jax import lax
from jax.experimental import pallas as pl
from jax.experimental.pallas import tpu as pltpu
from jax.sharding import PartitionSpec as P

EPSILON = 1e-05
MASKED = -1e30
F32 = jnp.float32
BF16 = jnp.bfloat16
CORES = 2


def dot(a, b, contract):
    return lax.dot_general(a, b, (contract, ((), ())), preferred_element_type=F32)


def norm_project_kernel(x_ref, gain_ref, bias_ref, w_ref, ln_ref, out_ref):
    x = x_ref[...].astype(F32)
    centre = x - jnp.mean(x, axis=1, keepdims=True)
    scale = lax.rsqrt(jnp.mean(centre * centre, axis=1, keepdims=True) + EPSILON)
    ln = (centre * scale * gain_ref[...] + bias_ref[...]).astype(BF16)
    ln_ref[...] = ln
    out_ref[...] = dot(ln, w_ref[...], ((1,), (0,))).astype(BF16)


def norm_project(tokens, gain, bias, weight):
    rows, width = tokens.shape
    columns = weight.shape[1]
    tile = 512
    return pl.pallas_call(
        norm_project_kernel,
        grid=(rows // tile,),
        in_specs=[
            pl.BlockSpec((tile, width), lambda i: (i, 0)),
            pl.BlockSpec((1, width), lambda i: (0, 0)),
            pl.BlockSpec((1, width), lambda i: (0, 0)),
            pl.BlockSpec((width, columns), lambda i: (0, 0)),
        ],
        out_specs=[
            pl.BlockSpec((tile, width), lambda i: (i, 0)),
            pl.BlockSpec((tile, columns), lambda i: (i, 0)),
        ],
        out_shape=[
            jax.ShapeDtypeStruct((rows, width), BF16),
            jax.ShapeDtypeStruct((rows, columns), BF16),
        ],
        compiler_params=pltpu.CompilerParams(vmem_limit_bytes=40 << 20),
        cost_estimate=pl.CostEstimate(
            flops=2 * rows * width * columns,
            bytes_accessed=2 * (2 * rows * width + rows * columns + width * columns),
            transcendentals=rows,
        ),
    )(tokens, gain[None], bias[None], weight)


def attend_kernel(head_size, group, tile, len_ref, q_ref, k_ref, v_ref, o_ref, lse_ref):
    seq_len, lanes = q_ref.shape
    scale = head_size**-0.5
    limit = len_ref[pl.program_id(0)]
    keys = k_ref[...]
    values = v_ref[...]
    key_place = lax.broadcasted_iota(jnp.int32, (seq_len, lanes), 0)
    lane = lax.broadcasted_iota(jnp.int32, (seq_len, lanes), 1)
    causal = lax.broadcasted_iota(jnp.int32, (tile, tile), 0) <= lax.broadcasted_iota(
        jnp.int32, (tile, tile), 1
    )
    tall = lax.broadcasted_iota(jnp.int32, (lanes, tile), 0)
    lane_q = lax.broadcasted_iota(jnp.int32, (tile, lanes), 1)
    heads = []
    for a in range(group):
        mine = (lane >= a * head_size) & (lane < (a + 1) * head_size)
        spare = ((a + 1) % group) * head_size
        extra = jnp.where((lane == spare) & (key_place >= limit), MASKED, 0.0).astype(BF16)
        k_a = jnp.where(mine, keys, extra)
        v_a = jnp.where(mine, values, jnp.ones((), BF16))
        heads.append((k_a, v_a, spare))
    for i in range(seq_len // tile):
        end = (i + 1) * tile
        q = (q_ref[i * tile : end, :].astype(F32) * scale).astype(BF16)
        out = None
        for a in range(group):
            k_a, v_a, spare = heads[a]
            mine_q = (lane_q >= a * head_size) & (lane_q < (a + 1) * head_size)
            q_a = jnp.where(mine_q, q, jnp.where(lane_q == spare, 1.0, 0.0).astype(BF16))
            scores = dot(k_a[:end], q_a, ((1,), (1,)))
            last = jnp.where(causal, scores[i * tile :], MASKED)
            scores = jnp.concatenate([scores[: i * tile], last], axis=0) if i else last
            top = jnp.max(scores, axis=0, keepdims=True)
            probs = jnp.exp(scores - top).astype(BF16)
            result = dot(v_a[:end], probs, ((0,), (0,)))
            total = result[spare : spare + 1, :]
            lse_ref[0, 0, a : a + 1, i * tile : end] = top + jnp.log(total)
            result = result / total
            if out is None:
                out = result
            else:
                out = jnp.where((tall >= a * head_size) & (tall < (a + 1) * head_size), result, out)
        o_ref[i * tile : end, :] = out.T.astype(BF16)


def attend(projected, lengths, seqs, heads, head_size):
    rows = projected.shape[0]
    seq_len = rows // seqs
    group = 2
    lanes = group * head_size
    groups = heads // group
    tile = 256
    return pl.pallas_call(
        functools.partial(attend_kernel, head_size, group, tile),
        grid_spec=pltpu.PrefetchScalarGridSpec(
            num_scalar_prefetch=1,
            grid=(seqs, groups),
            in_specs=[
                pl.BlockSpec((seq_len, lanes), lambda s, g, n: (s, g)),
                pl.BlockSpec((seq_len, lanes), lambda s, g, n: (s, groups + g)),
                pl.BlockSpec((seq_len, lanes), lambda s, g, n: (s, 2 * groups + g)),
            ],
            out_specs=[
                pl.BlockSpec((seq_len, lanes), lambda s, g, n: (s, g)),
                pl.BlockSpec((1, 1, group, seq_len), lambda s, g, n: (s, g, 0, 0)),
            ],
        ),
        out_shape=[
            jax.ShapeDtypeStruct((rows, heads * head_size), BF16),
            jax.ShapeDtypeStruct((seqs, groups, group, seq_len), F32),
        ],
        compiler_params=pltpu.CompilerParams(vmem_limit_bytes=40 << 20),
        cost_estimate=pl.CostEstimate(
            flops=4 * rows * seq_len * heads * head_size,
            bytes_accessed=8 * rows * heads * head_size,
            transcendentals=rows * seq_len * heads // 2,
        ),
    )(lengths, projected, projected, projected)


def attend_back_kernel(head_size, group, tile, len_ref, q_ref, k_ref, v_ref, o_ref, do_ref, lse_ref, out_ref, dk_acc, dv_acc):
    seq_len, lanes = q_ref.shape
    scale = head_size**-0.5
    limit = len_ref[pl.program_id(0)]
    keys = k_ref[...]
    values = v_ref[...]
    zero = jnp.zeros((), BF16)

    def place(kind):
        block = kind * pl.num_programs(1) + pl.program_id(1)
        return pl.ds(pl.multiple_of(block * lanes, lanes), lanes)

    key_place = lax.broadcasted_iota(jnp.int32, (seq_len, lanes), 0)
    lane = lax.broadcasted_iota(jnp.int32, (seq_len, lanes), 1)
    causal = lax.broadcasted_iota(jnp.int32, (tile, tile), 0) <= lax.broadcasted_iota(
        jnp.int32, (tile, tile), 1
    )
    lane_q = lax.broadcasted_iota(jnp.int32, (tile, lanes), 1)
    heads = []
    for a in range(group):
        mine = (lane >= a * head_size) & (lane < (a + 1) * head_size)
        spare = ((a + 1) % group) * head_size
        extra = jnp.where((lane == spare) & (key_place >= limit), MASKED, 0.0).astype(BF16)
        k_a = jnp.where(mine, keys, extra)
        ones = jnp.where((lane == spare) | (lane == spare + 1), 1.0, 0.0).astype(BF16)
        v_a = jnp.where(mine, values, ones)
        heads.append((k_a, v_a, spare))
    steps = seq_len // tile
    for i in reversed(range(steps)):
        end = (i + 1) * tile
        q = (q_ref[i * tile : end, :].astype(F32) * scale).astype(BF16)
        do = do_ref[i * tile : end, :]
        product = do.astype(F32) * o_ref[i * tile : end, :].astype(F32)
        dq = None
        dk = None
        dv = None
        for a in range(group):
            k_a, v_a, spare = heads[a]
            mine_q = (lane_q >= a * head_size) & (lane_q < (a + 1) * head_size)
            q_m = jnp.where(mine_q, q, zero)
            q_a = jnp.where(mine_q, q, jnp.where(lane_q == spare, 1.0, 0.0).astype(BF16))
            delta = -jnp.sum(jnp.where(mine_q, product, 0.0), axis=1, keepdims=True)
            high = delta.astype(BF16)
            low = (delta - high.astype(F32)).astype(BF16)
            do_m = jnp.where(mine_q, do, zero)
            do_a = jnp.where(lane_q == spare, high, jnp.where(lane_q == spare + 1, low, do_m))
            scores = dot(k_a[:end], q_a, ((1,), (1,)))
            last = jnp.where(causal, scores[i * tile :], MASKED)
            scores = jnp.concatenate([scores[: i * tile], last], axis=0) if i else last
            probs = jnp.exp(scores - lse_ref[0, 0, a : a + 1, i * tile : end])
            grad = dot(v_a[:end], do_a, ((1,), (1,)))
            grad = (probs * grad).astype(BF16)
            term_v = dot(probs.astype(BF16), do_m, ((1,), (0,)))
            term_k = dot(grad, q_m, ((1,), (0,)))
            term_q = dot(k_a[:end], grad, ((0,), (0,)))
            dv = term_v if dv is None else dv + term_v
            dk = term_k if dk is None else dk + term_k
            if dq is None:
                dq = term_q
            else:
                tall = lax.broadcasted_iota(jnp.int32, (lanes, tile), 0)
                dq = jnp.where((tall >= a * head_size) & (tall < (a + 1) * head_size), term_q, dq)
        out_ref[i * tile : end, place(0)] = (dq.T * scale).astype(BF16)
        if i == steps - 1:
            dk_acc[...] = dk
            dv_acc[...] = dv
        else:
            dk_acc[:end, :] += dk
            dv_acc[:end, :] += dv
    out_ref[:, place(1)] = dk_acc[...].astype(BF16)
    out_ref[:, place(2)] = dv_acc[...].astype(BF16)


def attend_back(projected, attended, grad_attended, lse, lengths, seqs, heads, head_size):
    rows = projected.shape[0]
    seq_len = rows // seqs
    group = 2
    lanes = group * head_size
    groups = heads // group
    tile = 256
    spec = pl.BlockSpec((seq_len, lanes), lambda s, g, n: (s, g))
    return pl.pallas_call(
        functools.partial(attend_back_kernel, head_size, group, tile),
        grid_spec=pltpu.PrefetchScalarGridSpec(
            num_scalar_prefetch=1,
            grid=(seqs, groups),
            in_specs=[
                spec,
                pl.BlockSpec((seq_len, lanes), lambda s, g, n: (s, groups + g)),
                pl.BlockSpec((seq_len, lanes), lambda s, g, n: (s, 2 * groups + g)),
                spec,
                spec,
                pl.BlockSpec((1, 1, group, seq_len), lambda s, g, n: (s, g, 0, 0)),
            ],
            out_specs=pl.BlockSpec((seq_len, 3 * groups * lanes), lambda s, g, n: (s, 0)),
            scratch_shapes=[pltpu.VMEM((seq_len, lanes), F32), pltpu.VMEM((seq_len, lanes), F32)],
        ),
        out_shape=jax.ShapeDtypeStruct((rows, 3 * heads * head_size), BF16),
        compiler_params=pltpu.CompilerParams(vmem_limit_bytes=48 << 20),
        cost_estimate=pl.CostEstimate(
            flops=10 * rows * seq_len * heads * head_size,
            bytes_accessed=16 * rows * heads * head_size,
            transcendentals=rows * seq_len * heads // 2,
        ),
    )(lengths, projected, projected, projected, attended, grad_attended, lse)


def place_kernel(order_ref, out_ref):
    count = out_ref.shape[1]
    tile = order_ref.shape[0]
    step = pl.program_id(0)
    token = lax.broadcasted_iota(jnp.int32, (tile, count), 1)
    index = lax.broadcasted_iota(jnp.int32, (tile, 1), 0) + step * tile
    hit = jnp.sum(jnp.where(order_ref[...] == token, index, 0), axis=0, keepdims=True)

    @pl.when(step == 0)
    def _():
        out_ref[...] = hit

    @pl.when(step > 0)
    def _():
        out_ref[...] += hit


def rank_kernel(key_ref, keys_ref, out_ref):
    step = pl.program_id(0)
    keys = keys_ref[...]
    base = jnp.bitwise_and(keys, -4096)
    key = key_ref[...]
    hit = jnp.sum(jnp.where((key < keys) & (key >= base), 1, 0), axis=0, keepdims=True)

    @pl.when(step == 0)
    def _():
        out_ref[...] = hit

    @pl.when(step > 0)
    def _():
        out_ref[...] += hit


def tall_reduce(kernel, column, rows, count):
    tile = 512
    specs = [pl.BlockSpec((tile, 1), lambda i: (i, 0))]
    specs += [pl.BlockSpec((1, count), lambda i: (0, 0)) for _ in rows]
    return pl.pallas_call(
        kernel,
        grid=(count // tile,),
        in_specs=specs,
        out_specs=pl.BlockSpec((1, count), lambda i: (0, 0)),
        out_shape=jax.ShapeDtypeStruct((1, count), jnp.int32),
        cost_estimate=pl.CostEstimate(
            flops=4 * count * count, bytes_accessed=600 * count, transcendentals=0
        ),
    )(column, *rows)


def token_slots(routes, order, lengths, seq_len, capacity, padded, none):
    count = routes.shape[0]
    places = jnp.arange(count, dtype=jnp.int32)[None]
    limits = jnp.repeat(lengths, seq_len, total_repeat_length=count)[None]
    valid = places % seq_len < limits
    turn = tall_reduce(place_kernel, order.reshape(count, 1), [], count)
    route = routes.reshape(1, count)
    keys = jnp.where(valid, route * 4096 + turn, 1 << 20)
    rank = tall_reduce(rank_kernel, keys.reshape(count, 1), [keys], count)
    return jnp.where(valid & (rank < capacity), route * padded + rank, none)


def pick_kernel(share, experts_step, padded, first_ref, slots_ref, rows_ref, out_ref):
    step = pl.program_id(0)
    start = first_ref[0] + step * experts_step * padded
    count = rows_ref.shape[0]
    slot = lax.broadcasted_iota(jnp.int32, (share, count), 0) + start
    chosen = jnp.where(slots_ref[...] == slot, 1.0, 0.0).astype(BF16)
    out_ref[...] = dot(chosen, rows_ref[...], ((1,), (0,))).astype(BF16)


def pick_rows(rows, slots, first, blocks, share, step, padded):
    count, width = rows.shape
    return pl.pallas_call(
        functools.partial(pick_kernel, share, step, padded),
        grid_spec=pltpu.PrefetchScalarGridSpec(
            num_scalar_prefetch=1,
            grid=(blocks,),
            in_specs=[
                pl.BlockSpec((1, count), lambda i, n: (0, 0)),
                pl.BlockSpec((count, width), lambda i, n: (0, 0)),
            ],
            out_specs=pl.BlockSpec((share, width), lambda i, n: (i, 0)),
        ),
        out_shape=jax.ShapeDtypeStruct((blocks * share, width), BF16),
        compiler_params=pltpu.CompilerParams(vmem_limit_bytes=40 << 20),
        cost_estimate=pl.CostEstimate(
            flops=2 * blocks * share * count * width,
            bytes_accessed=2 * (count + blocks * share) * width,
            transcendentals=0,
        ),
    )(first, slots, rows)


def out_project_kernel(count, first_ref, *refs):
    piece_refs, w_ref, x_ref, out_ref, wide = refs[:count], *refs[count:]
    for i, piece in enumerate(piece_refs):
        width = piece.shape[1]
        start = pl.multiple_of(first_ref[i] * width, width)
        wide[:, pl.ds(start, width)] = piece[...]
    out_ref[...] = (x_ref[...].astype(F32) + dot(wide[...], w_ref[...], ((1,), (0,)))).astype(BF16)


def out_project(pieces, first, weight, tokens):
    rows, width = tokens.shape
    inner = weight.shape[0]
    count = len(pieces)
    tile = 512
    return pl.pallas_call(
        functools.partial(out_project_kernel, count),
        grid_spec=pltpu.PrefetchScalarGridSpec(
            num_scalar_prefetch=1,
            grid=(rows // tile,),
            in_specs=[pl.BlockSpec((tile, p.shape[1]), lambda i, n: (i, 0)) for p in pieces]
            + [
                pl.BlockSpec((inner, width), lambda i, n: (0, 0)),
                pl.BlockSpec((tile, width), lambda i, n: (i, 0)),
            ],
            out_specs=pl.BlockSpec((tile, width), lambda i, n: (i, 0)),
            scratch_shapes=[pltpu.VMEM((tile, inner), BF16)],
        ),
        out_shape=jax.ShapeDtypeStruct((rows, width), BF16),
        compiler_params=pltpu.CompilerParams(vmem_limit_bytes=40 << 20),
        cost_estimate=pl.CostEstimate(
            flops=2 * rows * width * inner,
            bytes_accessed=2 * (3 * rows * width + inner * width),
            transcendentals=0,
        ),
    )(first, *pieces, weight, tokens)


def spread(count, first_ref, place_ref, piece_refs):
    place = place_ref[...]
    total = None
    for i in range(count):
        rows = piece_refs[i].shape[0]
        index = lax.broadcasted_iota(jnp.int32, (place.shape[0], rows), 1) + first_ref[i]
        chosen = jnp.where(place == index, 1.0, 0.0).astype(BF16)
        term = dot(chosen, piece_refs[i][...], ((1,), (0,)))
        total = term if total is None else total + term
    return total


def combine_kernel(count, first_ref, place_ref, base_ref, *refs):
    total = spread(count, first_ref, place_ref, refs[:count])
    refs[count][...] = (base_ref[...].astype(F32) + total).astype(BF16)


def combine_project_kernel(count, first_ref, place_ref, base_ref, *refs):
    total = spread(count, first_ref, place_ref, refs[:count])
    w_ref, out_ref, back_ref = refs[count:]
    out = (base_ref[...].astype(F32) + total).astype(BF16)
    out_ref[...] = out
    back_ref[...] = dot(out, w_ref[...], ((1,), (1,))).astype(BF16)


def combine(pieces, first, place, base, weight=None):
    rows, width = base.shape
    count = len(pieces)
    tile = 256
    block = pl.BlockSpec((tile, width), lambda i, n: (i, 0))
    in_specs = [pl.BlockSpec((tile, 1), lambda i, n: (i, 0)), block]
    in_specs += [pl.BlockSpec(p.shape, lambda i, n: (0, 0), pipeline_mode=pl.Buffered(1)) for p in pieces]
    args = [place, base, *pieces]
    out_specs, out_shape = [block], [jax.ShapeDtypeStruct((rows, width), BF16)]
    kernel = combine_kernel
    table = sum(p.shape[0] for p in pieces)
    flops = 2 * rows * width * table
    if weight is not None:
        inner = weight.shape[0]
        in_specs.append(pl.BlockSpec((inner, width), lambda i, n: (0, 0)))
        args.append(weight)
        out_specs.append(pl.BlockSpec((tile, inner), lambda i, n: (i, 0)))
        out_shape.append(jax.ShapeDtypeStruct((rows, inner), BF16))
        kernel = combine_project_kernel
        flops += 2 * rows * width * inner
    return pl.pallas_call(
        functools.partial(kernel, count),
        grid_spec=pltpu.PrefetchScalarGridSpec(
            num_scalar_prefetch=1, grid=(rows // tile,), in_specs=in_specs, out_specs=out_specs
        ),
        out_shape=out_shape,
        compiler_params=pltpu.CompilerParams(vmem_limit_bytes=48 << 20),
        cost_estimate=pl.CostEstimate(
            flops=flops, bytes_accessed=2 * (2 * rows + table) * width, transcendentals=0
        ),
    )(first, *args)


class Grid:
    def __init__(self, shards, experts):
        self.size = shards
        self.experts = experts
        self.depth = experts // CORES

    def over_core(self, value):
        return lax.ppermute(value, "dp", [(d, d ^ 1) for d in range(self.experts)])

    def over_tensor(self, value, other):
        return lax.ppermute(value, "tensor", [(t, t ^ other) for t in range(self.size)])

    def sum_all(self, value):
        step = 1
        while step < self.size:
            value = value + self.over_tensor(value, step)
            step *= 2
        step = 1
        while step < self.experts:
            pairs = [(d, d ^ step) for d in range(self.experts)]
            value = value + lax.ppermute(value, "dp", pairs)
            step *= 2
        return value

    def exchange_depth(self, value):
        groups = [[CORES * z + c for z in range(self.depth)] for c in range(CORES)]
        return lax.all_to_all(
            value, "dp", split_axis=0, concat_axis=0, axis_index_groups=groups, tiled=True
        )


def slice_half(value, half, axis):
    width = value.shape[axis] // 2
    return lax.dynamic_slice_in_dim(value, half * width, width, axis)


def owner_pairs(grid, flip, back=False):
    pairs = []
    for z in range(grid.depth):
        for core in range(CORES):
            for y in range(2):
                for x in range(2):
                    here = (CORES * z + core) * 4 + 2 * y + x
                    there = (CORES * z + (x ^ flip)) * 4 + 2 * y + core
                    pairs.append((there, here) if back else (here, there))
    return pairs


def fetch_halves(grid, weight, axis):
    core = lax.axis_index("dp") % CORES
    me = lax.axis_index("tensor")
    if grid.size == 4:
        near = [
            lax.ppermute(
                slice_half(weight, jnp.bitwise_xor(me % 2, flip), axis),
                ("dp", "tensor"),
                owner_pairs(grid, flip),
            )
            for flip in range(2)
        ]
        return near + [grid.over_tensor(piece, 2) for piece in near]
    every = lax.all_gather(weight, "tensor", axis=0, tiled=False)
    chosen = jnp.where(me % 2 == core, every, grid.over_core(every))
    return [slice_half(chosen[t], core, axis) for t in range(grid.size)]


def return_halves(grid, pieces, axis):
    core = lax.axis_index("dp") % CORES
    me = lax.axis_index("tensor")
    if grid.size == 4:
        halves = []
        for flip in range(2):
            far = grid.over_tensor(pieces[2 + flip].astype(BF16), 2)
            total = pieces[flip] + far.astype(F32)
            halves.append(
                lax.ppermute(total.astype(BF16), ("dp", "tensor"), owner_pairs(grid, flip, True))
            )
        swapped = me % 2 == 1
    else:
        stacked = jnp.stack(pieces).astype(BF16)
        wide = jnp.stack([jnp.where(me % 2 == p, stacked, jnp.zeros_like(stacked)) for p in range(2)])
        mine = lax.psum_scatter(wide, "tensor", scatter_dimension=1, tiled=False)
        halves = [
            jnp.where(core == 0, mine[0], mine[1]),
            grid.over_core(jnp.where(core == 0, mine[1], mine[0])),
        ]
        swapped = core == 1
    halves = [half.astype(F32) for half in halves]
    return jnp.where(swapped, jnp.concatenate(halves[::-1], axis), jnp.concatenate(halves, axis))


def gather_pieces(grid, value, balanced):
    if grid.size != 4:
        every = lax.all_gather(value, "tensor", axis=0, tiled=True)
        return [every], [jnp.int32(0)], [0]
    me = lax.axis_index("tensor")
    if not balanced:
        from_y = grid.over_tensor(value, 2)
        from_x = grid.over_tensor(value, 1)
        from_xy = grid.over_tensor(from_y, 1)
        return [value, from_x, from_y, from_xy], [jnp.bitwise_xor(me, o) for o in range(4)], [0] * 4
    half = value.shape[0] // 2
    first, second = value[:half], value[half:]
    first_x = grid.over_tensor(first, 1)
    second_y = grid.over_tensor(second, 2)
    first_y = grid.over_tensor(first, 2)
    second_x = grid.over_tensor(second, 1)
    first_xy = grid.over_tensor(first_x, 2)
    second_xy = grid.over_tensor(second_y, 1)
    pieces = [value, first_x, second_x, first_y, second_y, first_xy, second_xy]
    devices = [jnp.bitwise_xor(me, o) for o in (0, 1, 1, 2, 2, 3, 3)]
    return pieces, devices, [0, 0, half, 0, half, 0, half]


def gather_rows(grid, value, balanced=True):
    pieces, devices, starts = gather_pieces(grid, value, balanced)
    if len(pieces) == 1:
        return pieces[0]
    rows, width = value.shape
    out = jnp.zeros((grid.size * rows, width), value.dtype)
    for piece, device, start in zip(pieces, devices, starts):
        out = lax.dynamic_update_slice(out, piece, (device * rows + start, 0))
    return out


def scatter_rows(grid, term):
    size, rows, width = term.shape
    if size != 4:
        return lax.psum_scatter(term.astype(BF16), "tensor", scatter_dimension=0, tiled=False).astype(F32)
    me = lax.axis_index("tensor")
    half = width // 2

    def pick(other, low):
        place = jnp.bitwise_xor(me, other)
        return lax.dynamic_slice(term, (place, 0, low), (1, rows, half))[0]

    totals = []
    for low, near, far in ((0, 1, 2), (half, 2, 1)):
        got_far = grid.over_tensor(pick(3, low).astype(BF16), near)
        got_own = grid.over_tensor(pick(near, low).astype(BF16), near)
        onward = pick(far, low).astype(F32) + got_far.astype(F32)
        got = grid.over_tensor(onward.astype(BF16), far)
        totals.append(pick(0, low).astype(F32) + got_own.astype(F32) + got.astype(F32))
    return jnp.concatenate(totals, axis=1)


def gelu_pair(pre):
    cdf = 0.5 * (1.0 + lax.erf(pre * (2.0**-0.5)))
    density = jnp.exp(-0.5 * pre * pre) * ((2.0 * math.pi) ** -0.5)
    return (pre * cdf).astype(BF16), (cdf + pre * density).astype(BF16)


def body(
    tokens,
    lengths,
    routes,
    fill_order,
    norm_gain,
    norm_bias,
    qkv_weight,
    out_weight,
    centroids,
    expert_in,
    expert_out,
    cotangent,
):
    tok_count, model_width = tokens.shape
    seq_count = lengths.shape[0]
    seq_len = tok_count // seq_count
    heads_here = qkv_weight.shape[1]
    head_size = out_weight.shape[1]
    experts = lax.axis_size("dp")
    shards = lax.axis_size("tensor")
    grid = Grid(shards, experts)
    me = lax.axis_index("tensor")
    parity, part = me % 2, me // 2
    core = lax.axis_index("dp") % CORES
    depth = experts // CORES
    row_parts = shards // 2
    capacity = (9 * tok_count + 8 * experts - 1) // (8 * experts)
    share = 16 * -(-capacity // (16 * row_parts))
    padded = share * row_parts
    own_rows = depth * share
    tok_rows = tok_count // shards

    win, wout = [], []
    for k in range(2):
        win.append(fetch_halves(grid, expert_in[0, k], 1))
        wout.append(fetch_halves(grid, expert_out[0, k], 0))
    out_flat = out_weight.reshape(heads_here * head_size, model_width)
    out_all = gather_rows(grid, out_flat, False)
    centroid = jnp.where(parity == core, centroids[0], grid.over_core(centroids[0]))

    slots = token_slots(
        routes, fill_order, lengths, seq_len, capacity, padded, experts * padded
    )
    slot = slots.reshape(tok_count, 1)
    rank = slot % padded
    slot_device = (rank // share) * 2 + (slot // padded) % 2
    slot_place = (slot_device * depth + slot // (2 * padded)) * share + rank % share
    place = jnp.where(slot < experts * padded, slot_place, -1)
    own_first = (parity * padded + part * share).astype(jnp.int32).reshape(1)

    def to_experts(rows):
        picked = pick_rows(rows, slots, own_first, depth, share, CORES, padded)
        return grid.exchange_depth(picked.reshape(depth, share, model_width)).reshape(own_rows, model_width)

    def from_experts(rows, balanced):
        moved = grid.exchange_depth(rows.reshape(depth, share, model_width))
        pieces, devices, starts = gather_pieces(grid, moved.reshape(own_rows, model_width), balanced)
        first = [device * own_rows + start for device, start in zip(devices, starts)]
        return pieces, jnp.stack(first).astype(jnp.int32)

    grad_ret = to_experts(cotangent).astype(F32)
    heads = heads_here + heads_here % 2
    fused = qkv_weight.reshape(model_width, heads_here, 3, head_size)
    fused = jnp.swapaxes(fused, 1, 2)
    fused = jnp.pad(fused, ((0, 0), (0, 0), (0, heads - heads_here), (0, 0)))
    fused = fused.reshape(model_width, 3 * heads * head_size)
    inner = heads_here * head_size
    ln_in, projected = norm_project(tokens, norm_gain, norm_bias, fused)
    attended, log_total = attend(projected, lengths, seq_count, heads, head_size)
    if shards == 4:
        pieces, devices, unused = gather_pieces(grid, attended, False)
        first = jnp.stack(devices).astype(jnp.int32)
    else:
        every = lax.all_gather(attended[:, :inner], "tensor", axis=1, tiled=True)
        pieces, first = [every], jnp.zeros((1,), jnp.int32)
    sent = out_project(pieces, first, out_all, tokens)

    def both_cores(value):
        return jnp.concatenate([value, grid.over_core(value)], axis=0)

    def sum_cores(total):
        return total[:own_rows] + grid.over_core(total[own_rows:].astype(BF16)).astype(F32)

    expert_rows = to_experts(sent)
    gate = jax.nn.sigmoid(jnp.dot(expert_rows, centroid, preferred_element_type=F32))[:, None]
    current = expert_rows.astype(F32)
    saved = []
    for k in range(2):
        rows_in = both_cores(current.astype(BF16))
        acts, slopes = [], []
        total = None
        for w_in, w_out in zip(win[k], wout[k]):
            act, slope = gelu_pair(dot(rows_in, w_in, ((1,), (0,))))
            term = dot(act, w_out, ((1,), (0,)))
            total = term if total is None else total + term
            acts.append(act)
            slopes.append(slope)
        current = current + sum_cores(total)
        saved.append((rows_in, acts, slopes))
    pieces, first = from_experts((gate * current).astype(BF16), False)
    output = combine(pieces, first, place, sent)[0]

    grad_gate = jnp.sum(grad_ret * current, axis=1, keepdims=True)
    grad_logit = grad_gate * gate * (1.0 - gate)
    grad_current = gate * grad_ret
    grads_in = [None, None]
    grads_back = [None, None]
    for k in (1, 0):
        rows_in, acts, slopes = saved[k]
        branch = both_cores(grad_current.astype(BF16))
        total = None
        in_parts, out_parts = [], []
        for w_in, w_out, act, slope in zip(win[k], wout[k], acts, slopes):
            grad_pre = (dot(branch, w_out, ((1,), (1,))) * slope.astype(F32)).astype(BF16)
            term = dot(grad_pre, w_in, ((1,), (1,)))
            total = term if total is None else total + term
            out_parts.append(dot(act, branch, ((0,), (0,))))
            in_parts.append(dot(rows_in, grad_pre, ((0,), (0,))))
        grad_current = grad_current + sum_cores(total)
        grads_in[k] = return_halves(grid, in_parts, 1)
        grads_back[k] = return_halves(grid, out_parts, 0)
    grad_rows = (grad_current + grad_logit * centroid.astype(F32)[None, :]).astype(BF16)
    centroid_part = jnp.sum(grad_logit * expert_rows.astype(F32), axis=0, keepdims=True)
    centroid_parts = lax.psum(
        jnp.concatenate([jnp.where(parity == p, centroid_part, 0.0) for p in range(2)], axis=0), "tensor"
    )
    centroid_parts = centroid_parts + grid.over_core(centroid_parts)
    grad_centroid = lax.dynamic_slice_in_dim(centroid_parts, core, 1, 0)
    pieces, first = from_experts(grad_rows, True)
    out_padded = jnp.pad(out_flat, ((0, heads * head_size - inner), (0, 0)))
    grad_mixed, grad_attended = combine(pieces, first, place, cotangent, out_padded)
    grad_out_local = dot(attended[:, :inner], grad_mixed, ((0,), (0,))).reshape(
        heads_here, head_size, model_width
    )
    grad_projected = attend_back(
        projected, attended, grad_attended, log_total, lengths, seq_count, heads, head_size
    )
    grad_qkv_local = dot(ln_in, grad_projected, ((0,), (0,)))
    grad_ln_part = dot(grad_projected, fused, ((1,), (1,))).astype(BF16)
    grad_ln = scatter_rows(grid, grad_ln_part.reshape(shards, tok_rows, model_width))

    def own(rows):
        return lax.dynamic_slice_in_dim(rows, me * tok_rows, tok_rows, 0)

    own_tokens = own(tokens).astype(F32)
    centre = own_tokens - jnp.mean(own_tokens, axis=1, keepdims=True)
    own_scale = lax.rsqrt(jnp.mean(centre * centre, axis=1, keepdims=True) + EPSILON)
    own_normed = centre * own_scale
    grad_normed = grad_ln * norm_gain
    mean_plain = jnp.mean(grad_normed, axis=1, keepdims=True)
    mean_cross = jnp.mean(grad_normed * own_normed, axis=1, keepdims=True)
    grad_input = own(grad_mixed).astype(F32) + own_scale * (
        grad_normed - mean_plain - own_normed * mean_cross
    )
    grad_tokens = gather_rows(grid, grad_input.astype(BF16))
    norm_total = jnp.stack([jnp.sum(grad_ln * own_normed, axis=0), jnp.sum(grad_ln, axis=0)])
    norm_total = grid.sum_all(norm_total)
    norm_total = lax.dynamic_slice_in_dim(
        norm_total, me * (model_width // shards), model_width // shards, 1
    )
    grad_qkv, grad_out_weight = lax.psum(
        (grad_qkv_local.astype(BF16), grad_out_local.astype(BF16)), "dp"
    )
    grad_qkv = grad_qkv.astype(F32).reshape(model_width, 3, heads, head_size)[:, :, :heads_here]
    grad_qkv_weight = jnp.swapaxes(grad_qkv, 1, 2).reshape(model_width, heads_here, 3 * head_size)
    return (
        output,
        grad_tokens,
        norm_total[0],
        norm_total[1],
        grad_qkv_weight,
        grad_out_weight.astype(F32),
        grad_centroid,
        jnp.stack(grads_in)[None],
        jnp.stack(grads_back)[None],
    )


def solution(mesh):
    return jax.shard_map(
        body,
        mesh=mesh,
        in_specs=(
            P("dp", None),
            P("dp"),
            P("dp", None),
            P("dp", None),
            P(),
            P(),
            P(None, "tensor", None),
            P("tensor", None, None),
            P("dp", None),
            P("dp", None, None, "tensor"),
            P("dp", None, "tensor", None),
            P("dp", None),
        ),
        out_specs=(
            P("dp", None),
            P("dp", None),
            P("tensor"),
            P("tensor"),
            P(None, "tensor", None),
            P("tensor", None, None),
            P("dp", None),
            P("dp", None, None, "tensor"),
            P("dp", None, "tensor", None),
        ),
        check_vma=False,
    )
```

time: 1450 us -> 1210 us (0.83)
  local copies, waits for them, and re-layouts: 272 us -> 62.3 us
  Pallas kernels: 0 us -> 174 us
  matrix products: 411 us -> 297 us
  blocking collectives: 110 us -> 8.54 us
  waiting for transfers between devices: 330 us -> 418 us
  other arithmetic: 174 us -> 90.8 us
    pallas_call x0 -> x10, Pallas kernels: none -> 174 us  [the longest x2 68.8 us: combine(): pl.pallas_call(functools.partial(kernel, count), grid_spec=pltpu.Prefetch...]
    dot_general x7 -> x0, matrix products: 130 us -> none  [the longest x1 36.9 us: body(): jnp.einsum('sqhd,skhd->shqk', grad_attended, values, preferred_element_ty...]
    ppermute x43 -> x45, waiting for transfers between devices: 244 us -> 359 us  [over_tensor(): lax.ppermute(value, 'tensor', [(t, t ^ other) for t in range(self.size)])]
    gather x6 -> x1, local copies, waits for them, and re-layouts: 94.9 us -> 0.59 us  [token_slots(): limits = jnp.repeat(lengths, seq_len, total_repeat_length=count)[None]]
    psum x1 -> x0, blocking collectives: 47.8 us -> none  [body(): lax.psum(norm_parts, ('dp', 'tensor'))]
    all_to_all x1 -> x0, blocking collectives: 45.4 us -> none  [exchange_depth(): lax.all_to_all(value, 'dp', split_axis=0, concat_axis=0, axis_index_group...]
    convert_element_type x3 -> x1, other arithmetic: 45.3 us -> 1.09 us  [body(): grad_out_weight.astype(F32)]
    ppermute x8, waiting for transfers between devices: 35.7 us -> 0.02 us  [fetch_halves(): lax.ppermute(slice_half(weight, jnp.bitwise_xor(me % 2, flip), axis), ('d...]
  transfers between devices with their start and end apart: 73 -> 79, of which waited for: 23 -> 28; matrix products, arithmetic and copies ran while one was open for 46% -> 34% of each run, Pallas kernels for 0% -> 10%
where the time goes in v3:
time: 1210 us; the launch traced here: 1200 us
  waiting for transfers between devices  418 us (35%)
  matrix products  297 us (25%)
  Pallas kernels  174 us (14%)
  starting transfers between devices  133 us (11%)
  other arithmetic  90.8 us (8%)
  local copies, waits for them, and re-layouts  62.3 us (5%)
  between operations  16 us (1%)
    ppermute x45, waiting for transfers between devices, over_tensor(): lax.ppermute(value, 'tensor', [(t, t ^ other) for t in range(self.size)])  359 us
    dot_general x51, matrix products, dot(): lax.dot_general(a, b, (contract, ((), ())), preferred_element_type=F32)  296 us
    pallas_call x2, Pallas kernels, combine(): pl.pallas_call(functools.partial(kernel, count), grid_spec=pltpu.Prefetch...  68.8 us
    all_to_all x4, waiting for transfers between devices, exchange_depth(): lax.all_to_all(value, 'dp', split_axis=0, concat_axis=0, axis_index_group...  41.9 us
    ppermute x45, starting transfers between devices, over_tensor(): lax.ppermute(value, 'tensor', [(t, t ^ other) for t in range(self.size)])  40.5 us
    ppermute x8, starting transfers between devices, fetch_halves(): lax.ppermute(slice_half(weight, jnp.bitwise_xor(me % 2, flip), axis), ('d...  39.9 us
    pallas_call x1, Pallas kernels, attend_back(): pl.pallas_call(functools.partial(attend_back_kernel, head_size, group, ti...  26.8 us
    ppermute x8, starting transfers between devices, return_halves(): lax.ppermute(total.astype(BF16), ('dp', 'tensor'), owner_pairs(grid, flip...  26.1 us
  transfers between devices with their start and end apart: 79, of which 28 were waited for; matrix products, arithmetic and copies ran while one was open for 34% of the time, Pallas kernels for 10%

profile of v3, /device:TPU:0, one launch (start us, length us, event | category | flops | bytes accessed | tf_op | source)
XLA Modules:
  0.0 1199.8 jit_solution(16166185753544044774)
XLA Ops:
  9.9 10.6 shard_map.189
  20.6 24.6 %shard_map.190 = (bf16[3072,256]{1,0:T(8,128)(2,1)S(1)}, f32[3,2,2,1024]{3,2,1,0:T(2,128)S(1)}) custom-call(s32[3]{0:T(128)S(1)} %copy-done.6, bf16[3072,768]{1,0:T(8,128)(2,1)S(1)} %get-tuple-element.27.q_ref.k_ref.v_ref, bf16[3072,768]{1,0:T(8,128)(2,1)S(1)} %get-tuple-element.27.q_ref.k_ref.v_ref, bf16[3072,768]{1,0:T(8,128)(2,1)S(1)} %get-tuple-element.27.q_ref.k_ref.v_ref), custom_call_target="tpu_custom_call" | custom-call | flops 3221225472 | bytes 6291456 | tf_op jit(solution)/shard_map/pallas_call | solution.py:113
  63.0 20.7 %collective-permute-done.1.refs_2_ = bf16[3072,256]{1,0:T(8,128)(2,1)} collective-permute-done((bf16[3072,256]{1,0:T(8,128)(2,1)S(1)}, bf16[3072,256]{1,0:T(8,128)(2,1)}, u32[]{:S(2)}, u32[]{:S(2)}) %collective-permute-start.1) | collective-permute-done | bytes 1572896 | tf_op jit(solution)/shard_map/ppermute | solution.py:446
  101.6 38.9 %collective-permute-done.5 = bf16[256,1024]{1,0:T(8,128)(2,1)} collective-permute-done((bf16[256,1024]{1,0:T(8,128)(2,1)S(1)}, bf16[256,1024]{1,0:T(8,128)(2,1)}, u32[]{:S(2)}, u32[]{:S(2)}) %collective-permute-start.5) | collective-permute-done | bytes 524320 | tf_op jit(solution)/shard_map/ppermute | solution.py:446
  141.6 12.4 %shard_map.191.rows_ref.base_ref = bf16[3072,1024]{1,0:T(8,128)(2,1)} custom-call(s32[4]{0:T(128)S(1)} %pad_add_fusion.1.first_ref, bf16[3072,256]{1,0:T(8,128)(2,1)S(1)} %get-tuple-element.28.refs_0_.o_ref, bf16[3072,256]{1,0:T(8,128)(2,1)} %collective-permute-done.refs_1_, bf16[3072,256]{1,0:T(8,128)(2,1)} %collective-permute-done.1.refs_2_, ...), custom_call_target="tpu_custom_call" | custom-call | flops 6442450944 | bytes 20971520 | tf_op jit(solution)/shard_map/pallas_call | solution.py:355
  169.0 41.4 %all-to-all-done = bf16[4,224,1024]{2,1,0:T(8,128)(2,1)S(1)} async-done(((bf16[4,224,1024]{2,1,0:T(8,128)(2,1)}), bf16[4,224,1024]{2,1,0:T(8,128)(2,1)S(1)}, u32[]{:S(2)}, u32[]{:S(2)}) %all-to-all-start) | async-done | bytes 1835040 | tf_op jit(solution)/shard_map/all_to_all | solution.py:462
  216.5 10.4 collective-permute-start.8
  270.6 11.6 collective-permute-done.12
  297.3 29.8 %collective-permute-done.13 = bf16[512,1024]{1,0:T(8,128)(2,1)S(1)} collective-permute-done((bf16[512,1024]{1,0:T(8,128)(2,1)}, bf16[512,1024]{1,0:T(8,128)(2,1)S(1)}, u32[]{:S(2)}, u32[]{:S(2)}) %collective-permute-start.13) | collective-permute-done | bytes 1048608 | tf_op jit(solution)/shard_map/ppermute | solution.py:446
  424.8 47.5 %collective-permute-done.22 = bf16[1024,512]{1,0:T(8,128)(2,1)S(1)} collective-permute-done((bf16[1024,512]{1,0:T(8,128)(2,1)}, bf16[1024,512]{1,0:T(8,128)(2,1)S(1)}, u32[]{:S(2)}, u32[]{:S(2)}) %collective-permute-start.22) | collective-permute-done | bytes 1048608 | tf_op jit(solution)/shard_map/ppermute | solution.py:446
  559.1 9.9 add_add_fusion.2
  608.3 15.7 %collective-permute-done.72 = bf16[512,1024]{1,0:T(8,128)(2,1)} collective-permute-done((bf16[512,1024]{1,0:T(8,128)(2,1)}, bf16[512,1024]{1,0:T(8,128)(2,1)}, u32[]{:S(2)}, u32[]{:S(2)}) %collective-permute-start.72) | collective-permute-done | bytes 1048608 | tf_op jit(solution)/shard_map/ppermute | solution.py:446
  791.0 25.6 %collective-permute-done.58 = bf16[1024,512]{1,0:T(8,128)(2,1)} collective-permute-done((bf16[1024,512]{1,0:T(8,128)(2,1)}, bf16[1024,512]{1,0:T(8,128)(2,1)}, u32[]{:S(2)}, u32[]{:S(2)}) %collective-permute-start.58) | collective-permute-done | bytes 1048608 | tf_op jit(solution)/shard_map/ppermute | solution.py:446
  828.7 10.3 collective-permute-done.68
  841.1 40.1 %collective-permute-done.37.refs_4_ = bf16[448,1024]{1,0:T(8,128)(2,1)} collective-permute-done((bf16[448,1024]{1,0:T(8,128)(2,1)}, bf16[448,1024]{1,0:T(8,128)(2,1)}, u32[]{:S(2)}, u32[]{:S(2)}) %collective-permute-start.37) | collective-permute-done | bytes 917536 | tf_op jit(solution)/shard_map/ppermute | solution.py:446
  900.8 11.8 collective-permute-done.38.refs_5_
  915.5 35.8 %shard_map.195 = (bf16[3072,1024]{1,0:T(8,128)(2,1)}, bf16[3072,256]{1,0:T(8,128)(2,1)}) custom-call(s32[7]{0:T(128)S(1)} %stack.78.first_ref, s32[3072,1]{1,0:T(8,128)} %fusion.66.place_ref, bf16[3072,1024]{1,0:T(8,128)(2,1)} %base_ref.1, bf16[896,1024]{1,0:T(8,128)(2,1)} %bitcast.47.refs_0_, bf16[448,1024]{1,0:T(8,128)(2,1)} %collective-permute-done.34.refs_1_, ...), custom_call_target="tpu_custom_call" | custom-call | flops 24159191040 | bytes 19922944 | tf_op jit(solution)/shard_map/pallas_call | solution.py:423
  952.7 26.8 %shard_map.196 = bf16[3072,768]{1,0:T(8,128)(2,1)} custom-call(s32[3]{0:T(128)S(1)} %copy-done.7, bf16[3072,768]{1,0:T(8,128)(2,1)} %copy-done, bf16[3072,768]{1,0:T(8,128)(2,1)} %copy-done, bf16[3072,768]{1,0:T(8,128)(2,1)} %copy-done, bf16[3072,256]{1,0:T(8,128)(2,1)S(1)} %get-tuple-element.28.refs_0_.o_ref, bf16[3072,256]{1,0:T(8,128)(2,1)S(1)} %copy-done.11, ...), custom_call_target="tpu_custom_call" | custom-call | flops 8053063680 | bytes 12582912 | tf_op jit(solution)/shard_map/pallas_call | solution.py:222
  995.4 14.0 %collective-permute-done.41 = bf16[768,512]{1,0:T(8,128)(2,1)S(1)} collective-permute-done((bf16[768,512]{1,0:T(8,128)(2,1)S(1)}, bf16[768,512]{1,0:T(8,128)(2,1)S(1)}, u32[]{:S(2)}, u32[]{:S(2)}) %collective-permute-start.41) | collective-permute-done | bytes 786464 | tf_op jit(solution)/shard_map/ppermute | solution.py:446
  1049.4 21.8 %collective-permute-done.28.refs_2_ = bf16[896,1024]{1,0:T(8,128)(2,1)} collective-permute-done((bf16[896,1024]{1,0:T(8,128)(2,1)S(1)}, bf16[896,1024]{1,0:T(8,128)(2,1)}, u32[]{:S(2)}, u32[]{:S(2)}) %collective-permute-start.28) | collective-permute-done | bytes 1835040 | tf_op jit(solution)/shard_map/ppermute | solution.py:446
  1071.8 16.2 %collective-permute-done.43 = bf16[768,512]{1,0:T(8,128)(2,1)} collective-permute-done((bf16[768,512]{1,0:T(8,128)(2,1)}, bf16[768,512]{1,0:T(8,128)(2,1)}, u32[]{:S(2)}, u32[]{:S(2)}) %collective-permute-start.43) | collective-permute-done | bytes 786464 | tf_op jit(solution)/shard_map/ppermute | solution.py:446
  1098.9 16.8 %all-reduce.3.cloned.1.call-done = (bf16[1024,4,192]{0,2,1:T(8,128)(2,1)}, bf16[4,64,1024]{2,1,0:T(8,128)(2,1)}) async-done(((bf16[1024,4,192]{0,2,1:T(8,128)(2,1)}, bf16[4,64,1024]{2,1,0:T(8,128)(2,1)}), (bf16[1024,4,192]{0,2,1:T(8,128)(2,1)}, bf16[4,64,1024]{2,1,0:T(8,128)(2,1)})) %all-reduce.3.cloned.1.call-update) | async-done | bytes 2097168 | tf_op jit(solution)/shard_map/psum | solution.py:749
  1138.0 33.0 %shard_map.193 = bf16[3072,1024]{1,0:T(8,128)(2,1)} custom-call(s32[4]{0:T(128)S(1)} %pad_add_fusion.first_ref, s32[3072,1]{1,0:T(8,128)S(1)} %copy-done.1, bf16[3072,1024]{1,0:T(8,128)(2,1)} %shard_map.191.rows_ref.base_ref, bf16[896,1024]{1,0:T(8,128)(2,1)S(1)} %bitcast.213, bf16[896,1024]{1,0:T(8,128)(2,1)} %collective-permute-done.27.refs_1_, ...), custom_call_target="tpu_custom_call" | custom-call | flops 22548578304 | bytes 19922944 | tf_op jit(solution)/shard_map/pallas_call | solution.py:423
  1173.9 15.3 %collective-permute-done.50 = bf16[384,1024]{1,0:T(8,128)(2,1)S(1)} collective-permute-done((bf16[384,1024]{1,0:T(8,128)(2,1)S(1)}, bf16[384,1024]{1,0:T(8,128)(2,1)S(1)}, u32[]{:S(2)}, u32[]{:S(2)}) %collective-permute-start.50) | collective-permute-done | bytes 786464 | tf_op jit(solution)/shard_map/ppermute | solution.py:446
  (500 shorter events, 642.7 us)
Async XLA Ops:
  50.3 91.2 %collective-permute-start = (bf16[3072,256]{1,0:T(8,128)(2,1)S(1)}, bf16[3072,256]{1,0:T(8,128)(2,1)}, u32[]{:S(2)}, u32[]{:S(2)}) collective-permute-start(bf16[3072,256]{1,0:T(8,128)(2,1)S(1)} %get-tuple-element.28.refs_0_.o_ref), channel_id=1, source_target_pairs={{0,1},{1,0},{2,3},{3,2},{4,5},{5,4},{6,7},{7,6},{8,9},{9,8},{10,11... | collective-permute-start | bytes 4718600 | tf_op jit(solution)/shard_map/ppermute | solution.py:446
  246.8 145.5 %all-to-all-start.2 = ((bf16[4,224,1024]{2,1,0:T(8,128)(2,1)}), bf16[4,224,1024]{2,1,0:T(8,128)(2,1)}, u32[]{:S(2)}, u32[]{:S(2)}) async-start(bf16[4,224,1024]{2,1,0:T(8,128)(2,1)} %bitcast.43), calls=%async_computation.2 | async-start | bytes 3670016 | tf_op jit(solution)/shard_map/all_to_all | solution.py:462
  256.0 138.3 %collective-permute-start.20 = (bf16[1024,512]{1,0:T(8,128)(2,1)}, bf16[1024,512]{1,0:T(8,128)(2,1)}, u32[]{:S(2)}, u32[]{:S(2)}) collective-permute-start(bf16[1024,512]{1,0:T(8,128)(2,1)} %get-tuple-element.60), channel_id=1, source_target_pairs={{0,4},{1,0},{2,6},{3,2},{4,5},{5,1},{6,7},{7,3},{8,12},{9,8},{10,1... | collective-permute-start | bytes 3145736 | tf_op jit(solution)/shard_map/ppermute | solution.py:489
  262.1 129.0 %collective-permute-start.6 = (bf16[1024]{0:T(1024)(128)(2,1)S(1)}, bf16[1024]{0:T(1024)(128)(2,1)S(1)}, u32[]{:S(2)}, u32[]{:S(2)}) collective-permute-start(bf16[1024]{0:T(1024)(128)(2,1)S(1)} %reduce.4), channel_id=1, source_target_pairs={{0,4},{4,0},{8,12},{12,8},{16,20},{20,16},{24,28},{28,24},{1,5},{5... | collective-permute-start | bytes 6152 | tf_op jit(solution)/shard_map/ppermute | solution.py:443
  327.1 74.0 %collective-permute-start.21 = (bf16[512,1024]{1,0:T(8,128)(2,1)}, bf16[512,1024]{1,0:T(8,128)(2,1)}, u32[]{:S(2)}, u32[]{:S(2)}) collective-permute-start(bf16[512,1024]{1,0:T(8,128)(2,1)} %get-tuple-element.58), channel_id=1, source_target_pairs={{0,4},{1,0},{2,6},{3,2},{4,5},{5,1},{6,7},{7,3},{8,12},{9,8},{10,1... | collective-permute-start | bytes 3145736 | tf_op jit(solution)/shard_map/ppermute | solution.py:489
  332.7 68.9 %collective-permute-start.18 = (bf16[1024,512]{1,0:T(8,128)(2,1)}, bf16[1024,512]{1,0:T(8,128)(2,1)}, u32[]{:S(2)}, u32[]{:S(2)}) collective-permute-start(bf16[1024,512]{1,0:T(8,128)(2,1)} %get-tuple-element.59), channel_id=1, source_target_pairs={{0,0},{1,4},{2,2},{3,6},{4,1},{5,5},{6,3},{7,7},{8,8},{9,12},{10,1... | collective-permute-start | bytes 3145736 | tf_op jit(solution)/shard_map/ppermute | solution.py:489
  401.2 114.3 %collective-permute-start.24 = (bf16[1024,512]{1,0:T(8,128)(2,1)}, bf16[1024,512]{1,0:T(8,128)(2,1)S(1)}, u32[]{:S(2)}, u32[]{:S(2)}) collective-permute-start(bf16[1024,512]{1,0:T(8,128)(2,1)} %collective-permute-done.20), channel_id=1, source_target_pairs={{0,2},{1,3},{2,0},{3,1},{4,6},{5,7},{6,4},{7,5},{8,10},{9,11},{10,... | collective-permute-start | bytes 3145736 | tf_op jit(solution)/shard_map/ppermute | solution.py:446
  401.6 120.1 %collective-permute-start.25 = (bf16[512,1024]{1,0:T(8,128)(2,1)}, bf16[512,1024]{1,0:T(8,128)(2,1)S(1)}, u32[]{:S(2)}, u32[]{:S(2)}) collective-permute-start(bf16[512,1024]{1,0:T(8,128)(2,1)} %collective-permute-done.21), channel_id=1, source_target_pairs={{0,2},{1,3},{2,0},{3,1},{4,6},{5,7},{6,4},{7,5},{8,10},{9,11},{10,... | collective-permute-start | bytes 3145736 | tf_op jit(solution)/shard_map/ppermute | solution.py:446
  403.2 69.1 %collective-permute-start.22 = (bf16[1024,512]{1,0:T(8,128)(2,1)}, bf16[1024,512]{1,0:T(8,128)(2,1)S(1)}, u32[]{:S(2)}, u32[]{:S(2)}) collective-permute-start(bf16[1024,512]{1,0:T(8,128)(2,1)} %collective-permute-done.18), channel_id=1, source_target_pairs={{0,2},{1,3},{2,0},{3,1},{4,6},{5,7},{6,4},{7,5},{8,10},{9,11},{10,... | collective-permute-start | bytes 3145736 | tf_op jit(solution)/shard_map/ppermute | solution.py:446
  403.6 90.6 %collective-permute-start.23 = (bf16[512,1024]{1,0:T(8,128)(2,1)}, bf16[512,1024]{1,0:T(8,128)(2,1)S(1)}, u32[]{:S(2)}, u32[]{:S(2)}) collective-permute-start(bf16[512,1024]{1,0:T(8,128)(2,1)} %collective-permute-done.19), channel_id=1, source_target_pairs={{0,2},{1,3},{2,0},{3,1},{4,6},{5,7},{6,4},{7,5},{8,10},{9,11},{10,... | collective-permute-start | bytes 3145736 | tf_op jit(solution)/shard_map/ppermute | solution.py:446
  591.8 123.3 %collective-permute-start.64 = (bf16[1024,512]{1,0:T(8,128)(2,1)}, bf16[1024,512]{1,0:T(8,128)(2,1)}, u32[]{:S(2)}, u32[]{:S(2)}) collective-permute-start(bf16[1024,512]{1,0:T(8,128)(2,1)} %convolution_convert_fusion.6), channel_id=1, source_target_pairs={{0,2},{1,3},{2,0},{3,1},{4,6},{5,7},{6,4},{7,5},{8,10},{9,11},{10,... | collective-permute-start | bytes 3145736 | tf_op jit(solution)/shard_map/ppermute | solution.py:446
  607.6 123.7 %collective-permute-start.71 = (bf16[512,1024]{1,0:T(8,128)(2,1)}, bf16[512,1024]{1,0:T(8,128)(2,1)}, u32[]{:S(2)}, u32[]{:S(2)}) collective-permute-start(bf16[512,1024]{1,0:T(8,128)(2,1)} %add_convert_fusion.1), channel_id=1, source_target_pairs={{4,0},{0,1},{6,2},{2,3},{5,4},{1,5},{7,6},{3,7},{12,8},{8,9},{14,1... | collective-permute-start | bytes 3145736 | tf_op jit(solution)/shard_map/ppermute | solution.py:511
  628.4 105.9 %collective-permute-start.73 = (bf16[512,1024]{1,0:T(8,128)(2,1)}, bf16[512,1024]{1,0:T(8,128)(2,1)}, u32[]{:S(2)}, u32[]{:S(2)}) collective-permute-start(bf16[512,1024]{1,0:T(8,128)(2,1)} %add_convert_fusion), channel_id=1, source_target_pairs={{0,0},{4,1},{2,2},{6,3},{1,4},{5,5},{3,6},{7,7},{8,8},{12,9},{10,1... | collective-permute-start | bytes 3145736 | tf_op jit(solution)/shard_map/ppermute | solution.py:511
  652.0 85.3 %collective-permute-start.63 = (bf16[1024,512]{1,0:T(8,128)(2,1)}, bf16[1024,512]{1,0:T(8,128)(2,1)}, u32[]{:S(2)}, u32[]{:S(2)}) collective-permute-start(bf16[1024,512]{1,0:T(8,128)(2,1)} %add_convert_fusion.5), channel_id=1, source_target_pairs={{4,0},{0,1},{6,2},{2,3},{5,4},{1,5},{7,6},{3,7},{12,8},{8,9},{14,1... | collective-permute-start | bytes 3145736 | tf_op jit(solution)/shard_map/ppermute | solution.py:511
  785.5 101.1 %collective-permute-start.60 = (bf16[1024,512]{1,0:T(8,128)(2,1)}, bf16[1024,512]{1,0:T(8,128)(2,1)}, u32[]{:S(2)}, u32[]{:S(2)}) collective-permute-start(bf16[1024,512]{1,0:T(8,128)(2,1)} %convolution_convert_fusion.8), channel_id=1, source_target_pairs={{0,2},{1,3},{2,0},{3,1},{4,6},{5,7},{6,4},{7,5},{8,10},{9,11},{10,... | collective-permute-start | bytes 3145736 | tf_op jit(solution)/shard_map/ppermute | solution.py:446
  828.6 70.1 %collective-permute-start.35 = (bf16[448,1024]{1,0:T(8,128)(2,1)}, bf16[448,1024]{1,0:T(8,128)(2,1)}, u32[]{:S(2)}, u32[]{:S(2)}) collective-permute-start(bf16[448,1024]{1,0:T(8,128)(2,1)} %bitcast.49), channel_id=1, source_target_pairs={{0,1},{1,0},{2,3},{3,2},{4,5},{5,4},{6,7},{7,6},{8,9},{9,8},{10,11... | collective-permute-start | bytes 2752520 | tf_op jit(solution)/shard_map/ppermute | solution.py:446
  840.5 72.1 %collective-permute-start.38 = (bf16[448,1024]{1,0:T(8,128)(2,1)}, bf16[448,1024]{1,0:T(8,128)(2,1)}, u32[]{:S(2)}, u32[]{:S(2)}) collective-permute-start(bf16[448,1024]{1,0:T(8,128)(2,1)} %collective-permute-done.34.refs_1_), channel_id=1, source_target_pairs={{0,2},{1,3},{2,0},{3,1},{4,6},{5,7},{6,4},{7,5},{8,10},{9,11},{10,... | collective-permute-start | bytes 2752520 | tf_op jit(solution)/shard_map/ppermute | solution.py:446
  886.6 102.4 %collective-permute-start.67 = (bf16[512,1024]{1,0:T(8,128)(2,1)}, bf16[512,1024]{1,0:T(8,128)(2,1)}, u32[]{:S(2)}, u32[]{:S(2)}) collective-permute-start(bf16[512,1024]{1,0:T(8,128)(2,1)} %add_convert_fusion.3), channel_id=1, source_target_pairs={{4,0},{0,1},{6,2},{2,3},{5,4},{1,5},{7,6},{3,7},{12,8},{8,9},{14,1... | collective-permute-start | bytes 3145736 | tf_op jit(solution)/shard_map/ppermute | solution.py:511
  893.5 126.2 %all-to-all-start.1 = ((bf16[4,224,1024]{2,1,0:T(8,128)(2,1)}), bf16[4,224,1024]{2,1,0:T(8,128)(2,1)S(1)}, u32[]{:S(2)}, u32[]{:S(2)}) async-start(bf16[4,224,1024]{2,1,0:T(8,128)(2,1)} %bitcast.236), calls=%async_computation.1 | async-start | bytes 3670016 | tf_op jit(solution)/shard_map/all_to_all | solution.py:462
  898.6 217.1 %all-reduce.3.cloned.1.call-start = ((), (), s32[]{:S(2)}) async-start(), calls=%async_computation.4 | async-start | bytes 4194304 | tf_op jit(solution)/shard_map/psum | solution.py:749
  898.6 92.7 %collective-permute-start.69 = (bf16[512,1024]{1,0:T(8,128)(2,1)}, bf16[512,1024]{1,0:T(8,128)(2,1)S(1)}, u32[]{:S(2)}, u32[]{:S(2)}) collective-permute-start(bf16[512,1024]{1,0:T(8,128)(2,1)} %add_convert_fusion.2), channel_id=1, source_target_pairs={{0,0},{4,1},{2,2},{6,3},{1,4},{5,5},{3,6},{7,7},{8,8},{12,9},{10,1... | collective-permute-start | bytes 3145736 | tf_op jit(solution)/shard_map/ppermute | solution.py:511
  900.8 90.7 %collective-permute-start.59 = (bf16[1024,512]{1,0:T(8,128)(2,1)}, bf16[1024,512]{1,0:T(8,128)(2,1)}, u32[]{:S(2)}, u32[]{:S(2)}) collective-permute-start(bf16[1024,512]{1,0:T(8,128)(2,1)} %add_convert_fusion.7), channel_id=1, source_target_pairs={{4,0},{0,1},{6,2},{2,3},{5,4},{1,5},{7,6},{3,7},{12,8},{8,9},{14,1... | collective-permute-start | bytes 3145736 | tf_op jit(solution)/shard_map/ppermute | solution.py:511
  912.6 98.8 %collective-permute-start.61 = (bf16[1024,512]{1,0:T(8,128)(2,1)}, bf16[1024,512]{1,0:T(8,128)(2,1)S(1)}, u32[]{:S(2)}, u32[]{:S(2)}) collective-permute-start(bf16[1024,512]{1,0:T(8,128)(2,1)} %add_convert_fusion.6), channel_id=1, source_target_pairs={{0,0},{4,1},{2,2},{6,3},{1,4},{5,5},{3,6},{7,7},{8,8},{12,9},{10,1... | collective-permute-start | bytes 3145736 | tf_op jit(solution)/shard_map/ppermute | solution.py:511
  1021.0 113.2 %collective-permute-start.27 = (bf16[896,1024]{1,0:T(8,128)(2,1)S(1)}, bf16[896,1024]{1,0:T(8,128)(2,1)}, u32[]{:S(2)}, u32[]{:S(2)}) collective-permute-start(bf16[896,1024]{1,0:T(8,128)(2,1)S(1)} %bitcast.212), channel_id=1, source_target_pairs={{0,1},{1,0},{2,3},{3,2},{4,5},{5,4},{6,7},{7,6},{8,9},{9,8},{10,11... | collective-permute-start | bytes 5505032 | tf_op jit(solution)/shard_map/ppermute | solution.py:446
  (157 other events, 3957.2 us)
Sparse Core Ops, SparseCore 0:
  1049.5 66.1 all-reduce.2

commit v4 on v3

--- a/solution.py
+++ b/solution.py
@@ -403,7 +403,7 @@
 def combine(pieces, first, place, base, weight=None):
     rows, width = base.shape
     count = len(pieces)
-    tile = 256
+    tile = 512
     block = pl.BlockSpec((tile, width), lambda i, n: (i, 0))
     in_specs = [pl.BlockSpec((tile, 1), lambda i, n: (i, 0)), block]
     in_specs += [pl.BlockSpec(p.shape, lambda i, n: (0, 0), pipeline_mode=pl.Buffered(1)) for p in pieces]
@@ -433,6 +433,172 @@
     )(first, *args)
 
 
+def gelu_pair(pre):
+    cdf = 0.5 + 0.5 * lax.erf(pre * (2.0**-0.5))
+    density = jnp.exp(-0.5 * pre * pre) * ((2.0 * math.pi) ** -0.5)
+    return (pre * cdf).astype(BF16), (cdf + pre * density).astype(BF16)
+
+
+def without_base(kernel, count):
+    def wrapped(*refs):
+        kernel(*refs[:count], None, *refs[count:])
+
+    return wrapped
+
+
+def expert_forward_kernel(count, x_ref, base_ref, *refs):
+    w_in, w_out = refs[:count], refs[count : 2 * count]
+    act_ref, slope_ref, out_ref = refs[2 * count :]
+    x = x_ref[...]
+    total = base_ref[...] if base_ref is not None else None
+    width = w_in[0].shape[1]
+    chunk = min(width, 1024)
+    blocks = [(i, c) for i in range(count) for c in range(0, width, chunk)]
+
+    def into(i, c):
+        return dot(x, w_in[i][:, c : c + chunk], ((1,), (0,)))
+
+    ahead = into(*blocks[0])
+    for n, (i, c) in enumerate(blocks):
+        pre = ahead
+        if n + 1 < len(blocks):
+            ahead = into(*blocks[n + 1])
+        act, slope = gelu_pair(pre)
+        act_ref[:, i * width + c : i * width + c + chunk] = act
+        slope_ref[:, i * width + c : i * width + c + chunk] = slope
+        term = dot(act, w_out[i][c : c + chunk, :], ((1,), (0,)))
+        total = term if total is None else total + term
+    out_ref[...] = total.astype(out_ref.dtype)
+
+
+def expert_forward(x, w_in, w_out, base=None):
+    rows, width = x.shape
+    count = len(w_in)
+    hidden = sum(w.shape[1] for w in w_in)
+    tile = rows // 2
+
+    def row(n):
+        return pl.BlockSpec((tile, n), lambda i: (i, 0))
+
+    specs = [row(width)]
+    args = [x]
+    kernel = functools.partial(expert_forward_kernel, count)
+    if base is not None:
+        specs.append(row(width))
+        args.append(base)
+    else:
+        kernel = without_base(kernel, 1)
+    specs += [pl.BlockSpec(w.shape, lambda i: (0, 0), pipeline_mode=pl.Buffered(1)) for w in (*w_in, *w_out)]
+    return pl.pallas_call(
+        kernel,
+        grid=(rows // tile,),
+        in_specs=specs,
+        out_specs=[row(hidden), row(hidden), row(width)],
+        out_shape=[
+            jax.ShapeDtypeStruct((rows, hidden), BF16),
+            jax.ShapeDtypeStruct((rows, hidden), BF16),
+            jax.ShapeDtypeStruct((rows, width), BF16 if base is None else F32),
+        ],
+        compiler_params=pltpu.CompilerParams(vmem_limit_bytes=48 << 20),
+        cost_estimate=pl.CostEstimate(
+            flops=4 * rows * width * hidden,
+            bytes_accessed=4 * width * hidden + 4 * rows * hidden + 6 * rows * width,
+            transcendentals=2 * rows * hidden,
+        ),
+    )(*args, *w_in, *w_out)
+
+
+def expert_backward_kernel(count, g_ref, slope_ref, base_ref, *refs):
+    w_in, w_out = refs[:count], refs[count : 2 * count]
+    pre_ref, out_ref = refs[2 * count :]
+    g = g_ref[...]
+    total = base_ref[...] if base_ref is not None else None
+    width = w_in[0].shape[1]
+    chunk = min(width, 1024)
+    blocks = [(i, c) for i in range(count) for c in range(0, width, chunk)]
+
+    def into(i, c):
+        return dot(g, w_out[i][c : c + chunk, :], ((1,), (1,)))
+
+    ahead = into(*blocks[0])
+    for n, (i, c) in enumerate(blocks):
+        back = ahead
+        if n + 1 < len(blocks):
+            ahead = into(*blocks[n + 1])
+        place = slice(i * width + c, i * width + c + chunk)
+        pre = (back * slope_ref[:, place].astype(F32)).astype(BF16)
+        pre_ref[:, place] = pre
+        term = dot(pre, w_in[i][:, c : c + chunk], ((1,), (1,)))
+        total = term if total is None else total + term
+    out_ref[...] = total.astype(out_ref.dtype)
+
+
+def expert_backward(g, slope, w_in, w_out, base=None):
+    rows, width = g.shape
+    count = len(w_in)
+    hidden = slope.shape[1]
+    tile = rows // 2
+
+    def row(n):
+        return pl.BlockSpec((tile, n), lambda i: (i, 0))
+
+    specs = [row(width), row(hidden)]
+    args = [g, slope]
+    kernel = functools.partial(expert_backward_kernel, count)
+    if base is not None:
+        specs.append(row(width))
+        args.append(base)
+    else:
+        kernel = without_base(kernel, 2)
+    specs += [pl.BlockSpec(w.shape, lambda i: (0, 0), pipeline_mode=pl.Buffered(1)) for w in (*w_in, *w_out)]
+    return pl.pallas_call(
+        kernel,
+        grid=(rows // tile,),
+        in_specs=specs,
+        out_specs=[row(hidden), row(width)],
+        out_shape=[
+            jax.ShapeDtypeStruct((rows, hidden), BF16),
+            jax.ShapeDtypeStruct((rows, width), BF16 if base is None else F32),
+        ],
+        compiler_params=pltpu.CompilerParams(vmem_limit_bytes=48 << 20),
+        cost_estimate=pl.CostEstimate(
+            flops=4 * rows * width * hidden,
+            bytes_accessed=4 * width * hidden + 4 * rows * hidden + 6 * rows * width,
+            transcendentals=0,
+        ),
+    )(*args, *w_in, *w_out)
+
+
+def outer_kernel(count, *refs):
+    lefts, rights, out_ref = refs[:count], refs[count : 2 * count], refs[-1]
+    total = None
+    for a, b in zip(lefts, rights):
+        term = dot(a[...], b[...], ((0,), (0,)))
+        total = term if total is None else total + term
+    out_ref[...] = total.astype(out_ref.dtype)
+
+
+def outer(lefts, rights, left_block, right_block, left_width, right_width):
+    rows = lefts[0].shape[0]
+    count = len(lefts)
+    tile = min(256, left_width)
+    steps = left_width // tile
+    return pl.pallas_call(
+        functools.partial(outer_kernel, count),
+        grid=(steps,),
+        in_specs=[pl.BlockSpec((rows, tile), lambda i: (0, left_block * steps + i))] * count
+        + [pl.BlockSpec((rows, right_width), lambda i: (0, right_block))] * count,
+        out_specs=pl.BlockSpec((tile, right_width), lambda i: (i, 0)),
+        out_shape=jax.ShapeDtypeStruct((left_width, right_width), BF16),
+        compiler_params=pltpu.CompilerParams(vmem_limit_bytes=48 << 20),
+        cost_estimate=pl.CostEstimate(
+            flops=2 * count * rows * left_width * right_width,
+            bytes_accessed=2 * (count * rows * (left_width + right_width) + left_width * right_width),
+            transcendentals=0,
+        ),
+    )(*lefts, *rights)
+
+
 class Grid:
     def __init__(self, shards, experts):
         self.size = shards
@@ -464,64 +630,44 @@
         )
 
 
-def slice_half(value, half, axis):
-    width = value.shape[axis] // 2
-    return lax.dynamic_slice_in_dim(value, half * width, width, axis)
-
-
-def owner_pairs(grid, flip, back=False):
+def owner_pairs(grid, back=False):
     pairs = []
     for z in range(grid.depth):
         for core in range(CORES):
             for y in range(2):
                 for x in range(2):
                     here = (CORES * z + core) * 4 + 2 * y + x
-                    there = (CORES * z + (x ^ flip)) * 4 + 2 * y + core
+                    there = (CORES * z + x) * 4 + 2 * y + core
                     pairs.append((there, here) if back else (here, there))
     return pairs
 
 
-def fetch_halves(grid, weight, axis):
+def fetch_hidden(grid, weight):
+    if grid.size == 4:
+        near = lax.ppermute(weight, ("dp", "tensor"), owner_pairs(grid))
+        return [near, grid.over_tensor(near, 2)]
+    core = lax.axis_index("dp") % CORES
+    every = lax.all_gather(weight, "tensor", axis=0, tiled=False)
+    chosen = jnp.where(lax.axis_index("tensor") % 2 == core, every, grid.over_core(every))
+    return [jnp.where(core == 0, chosen[t], chosen[t + 1]) for t in range(0, grid.size, 2)]
+
+
+def return_hidden(grid, pieces):
+    if grid.size == 4:
+        total = pieces[0].astype(F32) + grid.over_tensor(pieces[1], 2).astype(F32)
+        return lax.ppermute(total.astype(BF16), ("dp", "tensor"), owner_pairs(grid, True)).astype(F32)
     core = lax.axis_index("dp") % CORES
     me = lax.axis_index("tensor")
-    if grid.size == 4:
-        near = [
-            lax.ppermute(
-                slice_half(weight, jnp.bitwise_xor(me % 2, flip), axis),
-                ("dp", "tensor"),
-                owner_pairs(grid, flip),
-            )
-            for flip in range(2)
-        ]
-        return near + [grid.over_tensor(piece, 2) for piece in near]
-    every = lax.all_gather(weight, "tensor", axis=0, tiled=False)
-    chosen = jnp.where(me % 2 == core, every, grid.over_core(every))
-    return [slice_half(chosen[t], core, axis) for t in range(grid.size)]
-
-
-def return_halves(grid, pieces, axis):
-    core = lax.axis_index("dp") % CORES
-    me = lax.axis_index("tensor")
-    if grid.size == 4:
-        halves = []
-        for flip in range(2):
-            far = grid.over_tensor(pieces[2 + flip].astype(BF16), 2)
-            total = pieces[flip] + far.astype(F32)
-            halves.append(
-                lax.ppermute(total.astype(BF16), ("dp", "tensor"), owner_pairs(grid, flip, True))
-            )
-        swapped = me % 2 == 1
-    else:
-        stacked = jnp.stack(pieces).astype(BF16)
-        wide = jnp.stack([jnp.where(me % 2 == p, stacked, jnp.zeros_like(stacked)) for p in range(2)])
-        mine = lax.psum_scatter(wide, "tensor", scatter_dimension=1, tiled=False)
-        halves = [
-            jnp.where(core == 0, mine[0], mine[1]),
-            grid.over_core(jnp.where(core == 0, mine[1], mine[0])),
-        ]
-        swapped = core == 1
-    halves = [half.astype(F32) for half in halves]
-    return jnp.where(swapped, jnp.concatenate(halves[::-1], axis), jnp.concatenate(halves, axis))
+    zero = jnp.zeros_like(pieces[0])
+    wide = []
+    for parity in range(2):
+        row = []
+        for piece in pieces:
+            row += [jnp.where((me % 2 == parity) & (core == c), piece, zero) for c in range(CORES)]
+        wide.append(jnp.stack(row))
+    mine = lax.psum_scatter(jnp.stack(wide), "tensor", scatter_dimension=1, tiled=False)
+    other = grid.over_core(jnp.where(core == 0, mine[1], mine[0]))
+    return jnp.where(core == 0, mine[0], mine[1]).astype(F32) + other.astype(F32)
 
 
 def gather_pieces(grid, value, balanced):
@@ -577,12 +723,6 @@
         got = grid.over_tensor(onward.astype(BF16), far)
         totals.append(pick(0, low).astype(F32) + got_own.astype(F32) + got.astype(F32))
     return jnp.concatenate(totals, axis=1)
-
-
-def gelu_pair(pre):
-    cdf = 0.5 * (1.0 + lax.erf(pre * (2.0**-0.5)))
-    density = jnp.exp(-0.5 * pre * pre) * ((2.0 * math.pi) ** -0.5)
-    return (pre * cdf).astype(BF16), (cdf + pre * density).astype(BF16)
 
 
 def body(
@@ -620,8 +760,8 @@
 
     win, wout = [], []
     for k in range(2):
-        win.append(fetch_halves(grid, expert_in[0, k], 1))
-        wout.append(fetch_halves(grid, expert_out[0, k], 0))
+        win.append(fetch_hidden(grid, expert_in[0, k]))
+        wout.append(fetch_hidden(grid, expert_out[0, k]))
     out_flat = out_weight.reshape(heads_here * head_size, model_width)
     out_all = gather_rows(grid, out_flat, False)
     centroid = jnp.where(parity == core, centroids[0], grid.over_core(centroids[0]))
@@ -663,50 +803,32 @@
         pieces, first = [every], jnp.zeros((1,), jnp.int32)
     sent = out_project(pieces, first, out_all, tokens)
 
-    def both_cores(value):
-        return jnp.concatenate([value, grid.over_core(value)], axis=0)
-
-    def sum_cores(total):
-        return total[:own_rows] + grid.over_core(total[own_rows:].astype(BF16)).astype(F32)
-
     expert_rows = to_experts(sent)
     gate = jax.nn.sigmoid(jnp.dot(expert_rows, centroid, preferred_element_type=F32))[:, None]
     current = expert_rows.astype(F32)
     saved = []
     for k in range(2):
-        rows_in = both_cores(current.astype(BF16))
-        acts, slopes = [], []
-        total = None
-        for w_in, w_out in zip(win[k], wout[k]):
-            act, slope = gelu_pair(dot(rows_in, w_in, ((1,), (0,))))
-            term = dot(act, w_out, ((1,), (0,)))
-            total = term if total is None else total + term
-            acts.append(act)
-            slopes.append(slope)
-        current = current + sum_cores(total)
-        saved.append((rows_in, acts, slopes))
+        here = current.astype(BF16)
+        there = grid.over_core(here)
+        act, slope, total = expert_forward(here, win[k], wout[k], current)
+        act_there, slope_there, part = expert_forward(there, win[k], wout[k])
+        current = total + grid.over_core(part).astype(F32)
+        saved.append(([here, there], [act, act_there], [slope, slope_there]))
     pieces, first = from_experts((gate * current).astype(BF16), False)
     output = combine(pieces, first, place, sent)[0]
 
     grad_gate = jnp.sum(grad_ret * current, axis=1, keepdims=True)
     grad_logit = grad_gate * gate * (1.0 - gate)
     grad_current = gate * grad_ret
-    grads_in = [None, None]
-    grads_back = [None, None]
+    branches = [None, None]
     for k in (1, 0):
-        rows_in, acts, slopes = saved[k]
-        branch = both_cores(grad_current.astype(BF16))
-        total = None
-        in_parts, out_parts = [], []
-        for w_in, w_out, act, slope in zip(win[k], wout[k], acts, slopes):
-            grad_pre = (dot(branch, w_out, ((1,), (1,))) * slope.astype(F32)).astype(BF16)
-            term = dot(grad_pre, w_in, ((1,), (1,)))
-            total = term if total is None else total + term
-            out_parts.append(dot(act, branch, ((0,), (0,))))
-            in_parts.append(dot(rows_in, grad_pre, ((0,), (0,))))
-        grad_current = grad_current + sum_cores(total)
-        grads_in[k] = return_halves(grid, in_parts, 1)
-        grads_back[k] = return_halves(grid, out_parts, 0)
+        slopes = saved[k][2]
+        here = grad_current.astype(BF16)
+        there = grid.over_core(here)
+        grad_pre, total = expert_backward(here, slopes[0], win[k], wout[k], grad_current)
+        grad_pre_there, part = expert_backward(there, slopes[1], win[k], wout[k])
+        grad_current = total + grid.over_core(part).astype(F32)
+        branches[k] = ([here, there], [grad_pre, grad_pre_there])
     grad_rows = (grad_current + grad_logit * centroid.astype(F32)[None, :]).astype(BF16)
     centroid_part = jnp.sum(grad_logit * expert_rows.astype(F32), axis=0, keepdims=True)
     centroid_parts = lax.psum(
@@ -715,6 +837,18 @@
     centroid_parts = centroid_parts + grid.over_core(centroid_parts)
     grad_centroid = lax.dynamic_slice_in_dim(centroid_parts, core, 1, 0)
     pieces, first = from_experts(grad_rows, True)
+    hidden = expert_in.shape[3]
+    grads_in, grads_back = [None, None], [None, None]
+    for k in (1, 0):
+        rows_in, acts, unused = saved[k]
+        branch, grad_pres = branches[k]
+        blocks = range(len(win[k]))
+        grads_back[k] = return_hidden(
+            grid, [outer(acts, branch, j, 0, hidden, model_width) for j in blocks]
+        )
+        grads_in[k] = return_hidden(
+            grid, [outer(rows_in, grad_pres, 0, j, model_width, hidden) for j in blocks]
+        )
     out_padded = jnp.pad(out_flat, ((0, heads * head_size - inner), (0, 0)))
     grad_mixed, grad_attended = combine(pieces, first, place, cotangent, out_padded)
     grad_out_local = dot(attended[:, :inner], grad_mixed, ((0,), (0,))).reshape(

time: 1210 us -> 1060 us (0.88)
  matrix products: 297 us -> 16.2 us
  Pallas kernels: 174 us -> 337 us
  waiting for transfers between devices: 418 us -> 369 us
  starting transfers between devices: 133 us -> 157 us
    dot_general x51 -> x3, matrix products: 296 us -> 15.6 us  [dot(): lax.dot_general(a, b, (contract, ((), ())), preferred_element_type=F32)]
    pallas_call x0 -> x16, Pallas kernels: none -> 167 us  [the longest x8 59.7 us: outer(): pl.pallas_call(functools.partial(outer_kernel, count), grid=(steps,), in_...]
    ppermute x45 -> x37, waiting for transfers between devices: 359 us -> 312 us  [over_tensor(): lax.ppermute(value, 'tensor', [(t, t ^ other) for t in range(self.size)])]
    ppermute x10, starting transfers between devices: 1.8 us -> 29.4 us  [over_core(): return lax.ppermute(value, 'dp', [(d, d ^ 1) for d in range(self.experts)])]
    convert_element_type x2 -> x7, other arithmetic: 6.82 us -> 29.8 us  [the longest x4 16.6 us: return_hidden(): total.astype(BF16)]
    psum x1, waiting for transfers between devices: 16.8 us -> 0.01 us  [body(): lax.psum((grad_qkv_local.astype(BF16), grad_out_local.astype(BF16)), 'dp')]
    concatenate x8 -> x0, other arithmetic: 14.7 us -> none  [return_halves(): jnp.concatenate(halves[::-1], axis)]
    select_n x4 -> x0, other arithmetic: 13.6 us -> none  [return_halves(): jnp.where(swapped, jnp.concatenate(halves[::-1], axis), jnp.concatenate(h...]
  transfers between devices with their start and end apart: 79 -> 63, of which waited for: 28 -> 21; matrix products, arithmetic and copies ran while one was open for 34% -> 12% of each run, Pallas kernels for 10% -> 25%
where the time goes in v4:
time: 1060 us; the launch traced here: 1040 us
  waiting for transfers between devices  369 us (35%)
  Pallas kernels  337 us (32%)
  starting transfers between devices  157 us (15%)
  other arithmetic  85.7 us (8%)
  local copies, waits for them, and re-layouts  56.2 us (5%)
  matrix products  16.2 us (2%)
  between operations  15.5 us (1%)
    ppermute x37, waiting for transfers between devices, over_tensor(): lax.ppermute(value, 'tensor', [(t, t ^ other) for t in range(self.size)])  312 us
    pallas_call x2, Pallas kernels, combine(): pl.pallas_call(functools.partial(kernel, count), grid_spec=pltpu.Prefetch...  65.5 us
    pallas_call x8, Pallas kernels, outer(): pl.pallas_call(functools.partial(outer_kernel, count), grid=(steps,), in_...  59.7 us
    pallas_call x4, Pallas kernels, expert_forward(): pl.pallas_call(kernel, grid=(rows // tile,), in_specs=specs, out_specs=[r...  54 us
    pallas_call x4, Pallas kernels, expert_backward(): pl.pallas_call(kernel, grid=(rows // tile,), in_specs=specs, out_specs=[r...  53.1 us
    all_to_all x4, waiting for transfers between devices, exchange_depth(): lax.all_to_all(value, 'dp', split_axis=0, concat_axis=0, axis_index_group...  45.5 us
    ppermute x37, starting transfers between devices, over_tensor(): lax.ppermute(value, 'tensor', [(t, t ^ other) for t in range(self.size)])  41.9 us
    ppermute x4, starting transfers between devices, fetch_hidden(): near = lax.ppermute(weight, ('dp', 'tensor'), owner_pairs(grid))  38.3 us
  transfers between devices with their start and end apart: 63, of which 21 were waited for; matrix products, arithmetic and copies ran while one was open for 12% of the time, Pallas kernels for 25%

profile of v4, /device:TPU:0, one launch (start us, length us, event | category | flops | bytes accessed | tf_op | source)
XLA Modules:
  0.0 1043.1 jit_solution(13967299547642575129)
XLA Ops:
  22.2 24.6 %shard_map.190 = (bf16[3072,256]{1,0:T(8,128)(2,1)S(1)}, f32[3,2,2,1024]{3,2,1,0:T(2,128)S(1)}) custom-call(s32[3]{0:T(128)S(1)} %copy-done.17, bf16[3072,768]{1,0:T(8,128)(2,1)S(1)} %get-tuple-element.47.q_ref.k_ref.v_ref, bf16[3072,768]{1,0:T(8,128)(2,1)S(1)} %get-tuple-element.47.q_ref.k_ref.v_ref, bf16[3072,768]{1,0:T(8,128)(2,1)S(1)} %get-tuple-element.47.q_ref.k_ref.v_ref), custom_call_target="tpu_custom_call" | custom-call | flops 3221225472 | bytes 6291456 | tf_op jit(solution)/shard_map/pallas_call | solution.py:113
  64.6 20.7 %collective-permute-done.1.refs_2_ = bf16[3072,256]{1,0:T(8,128)(2,1)} collective-permute-done((bf16[3072,256]{1,0:T(8,128)(2,1)S(1)}, bf16[3072,256]{1,0:T(8,128)(2,1)}, u32[]{:S(2)}, u32[]{:S(2)}) %collective-permute-start.1) | collective-permute-done | bytes 1572896 | tf_op jit(solution)/shard_map/ppermute | solution.py:612
  104.2 37.9 %collective-permute-done.5 = bf16[256,1024]{1,0:T(8,128)(2,1)} collective-permute-done((bf16[256,1024]{1,0:T(8,128)(2,1)S(1)}, bf16[256,1024]{1,0:T(8,128)(2,1)}, u32[]{:S(2)}, u32[]{:S(2)}) %collective-permute-start.5) | collective-permute-done | bytes 524320 | tf_op jit(solution)/shard_map/ppermute | solution.py:612
  182.9 29.5 %all-to-all-done = bf16[4,224,1024]{2,1,0:T(8,128)(2,1)S(1)} async-done(((bf16[4,224,1024]{2,1,0:T(8,128)(2,1)}), bf16[4,224,1024]{2,1,0:T(8,128)(2,1)S(1)}, u32[]{:S(2)}, u32[]{:S(2)}) %all-to-all-start) | async-done | bytes 1835040 | tf_op jit(solution)/shard_map/all_to_all | solution.py:628
  212.5 13.1 %collective-permute-start.11 = (bf16[896,1024]{1,0:T(8,128)(2,1)S(1)}, bf16[896,1024]{1,0:T(8,128)(2,1)S(1)}, u32[]{:S(2)}, u32[]{:S(2)}) collective-permute-start(bf16[896,1024]{1,0:T(8,128)(2,1)S(1)} %bitcast.120), channel_id=1, source_target_pairs={{0,4},{4,0},{8,12},{12,8},{16,20},{20,16},{24,28},{28,24},{1,5},{5... | collective-permute-start | bytes 5505032 | tf_op jit(solution)/shard_map/ppermute | solution.py:609
  225.5 17.2 %collective-permute-start.13 = (bf16[1024,1024]{1,0:T(8,128)(2,1)}, bf16[1024,1024]{1,0:T(8,128)(2,1)}, u32[]{:S(2)}, u32[]{:S(2)}) collective-permute-start(bf16[1024,1024]{1,0:T(8,128)(2,1)} %get-tuple-element.99), channel_id=1, source_target_pairs={{0,0},{1,4},{2,2},{3,6},{4,1},{5,5},{6,3},{7,7},{8,8},{9,12},{10,1... | collective-permute-start | bytes 6291464 | tf_op jit(solution)/shard_map/ppermute | solution.py:647
  242.7 17.2 %collective-permute-start.15 = (bf16[1024,1024]{1,0:T(8,128)(2,1)}, bf16[1024,1024]{1,0:T(8,128)(2,1)}, u32[]{:S(2)}, u32[]{:S(2)}) collective-permute-start(bf16[1024,1024]{1,0:T(8,128)(2,1)} %get-tuple-element.97), channel_id=1, source_target_pairs={{0,0},{1,4},{2,2},{3,6},{4,1},{5,5},{6,3},{7,7},{8,8},{9,12},{10,1... | collective-permute-start | bytes 6291464 | tf_op jit(solution)/shard_map/ppermute | solution.py:647
  273.0 14.5 %collective-permute-start.12 = (bf16[896,1024]{1,0:T(8,128)(2,1)S(1)}, bf16[896,1024]{1,0:T(8,128)(2,1)}, u32[]{:S(2)}, u32[]{:S(2)}) collective-permute-start(bf16[896,1024]{1,0:T(8,128)(2,1)S(1)} %get-tuple-element.50), channel_id=1, source_target_pairs={{0,4},{4,0},{8,12},{12,8},{16,20},{20,16},{24,28},{28,24},{1,5},{5... | collective-permute-start | bytes 5505032 | tf_op jit(solution)/shard_map/ppermute | solution.py:609
  292.0 13.9 %shard_map.193 = (bf16[896,2048]{1,0:T(8,128)(2,1)}, bf16[896,2048]{1,0:T(8,128)(2,1)}, f32[896,1024]{1,0:T(8,128)}) custom-call(bf16[896,1024]{1,0:T(8,128)(2,1)S(1)} %bitcast.121, f32[896,1024]{1,0:T(8,128)} %bitcast_convert_fusion.base_ref, bf16[1024,1024]{1,0:T(8,128)(2,1)} %collective-permute-done.7.refs_0_.refs_1_.refs_2_, ...), custom_call_target="tpu_custom_call" | custom-call | flops 7516192768 | bytes 21233664 | tf_op jit(solution)/shard_map/pallas_call | solution.py:492
  336.4 44.1 %collective-permute-done.16.refs_3_.refs_4_.refs_5_ = bf16[1024,1024]{1,0:T(8,128)(2,1)} collective-permute-done((bf16[1024,1024]{1,0:T(8,128)(2,1)}, bf16[1024,1024]{1,0:T(8,128)(2,1)}, u32[]{:S(2)}, u32[]{:S(2)}) %collective-permute-start.16) | collective-permute-done | bytes 2097184 | tf_op jit(solution)/shard_map/ppermute | solution.py:612
  397.5 14.1 %shard_map.195 = (bf16[896,2048]{1,0:T(8,128)(2,1)}, bf16[896,2048]{1,0:T(8,128)(2,1)}, f32[896,1024]{1,0:T(8,128)}) custom-call(bf16[896,1024]{1,0:T(8,128)(2,1)} %get-tuple-element.85.x_ref.refs_0_, f32[896,1024]{1,0:T(8,128)} %get-tuple-element.86.base_ref, bf16[1024,1024]{1,0:T(8,128)(2,1)} %collective-permute-done.13.refs_0_.refs_1_.refs_2_, ...), custom_call_target="tpu_custom_call" | custom-call | flops 7516192768 | bytes 21233664 | tf_op jit(solution)/shard_map/pallas_call | solution.py:492
  435.1 13.9 %shard_map.199 = (bf16[896,2048]{1,0:T(8,128)(2,1)}, f32[896,1024]{1,0:T(8,128)}) custom-call(bf16[896,1024]{1,0:T(8,128)(2,1)S(1)} %get-tuple-element.101.g_ref.refs_2_, bf16[896,2048]{1,0:T(8,128)(2,1)} %get-tuple-element.53.slope_ref, f32[896,1024]{1,0:T(8,128)} %get-tuple-element.102.base_ref, ...), custom_call_target="tpu_custom_call" | custom-call | flops 7516192768 | bytes 21233664 | tf_op jit(solution)/shard_map/pallas_call | solution.py:554
  470.8 13.8 %shard_map.201 = (bf16[896,2048]{1,0:T(8,128)(2,1)}, f32[896,1024]{1,0:T(8,128)}) custom-call(bf16[896,1024]{1,0:T(8,128)(2,1)S(1)} %get-tuple-element.83.g_ref.refs_2_, bf16[896,2048]{1,0:T(8,128)(2,1)} %get-tuple-element.57.slope_ref, f32[896,1024]{1,0:T(8,128)} %get-tuple-element.84.base_ref, ...), custom_call_target="tpu_custom_call" | custom-call | flops 7516192768 | bytes 21233664 | tf_op jit(solution)/shard_map/pallas_call | solution.py:554
  521.2 15.9 %all-to-all-done.3 = bf16[4,224,1024]{2,1,0:T(8,128)(2,1)} async-done(((bf16[4,224,1024]{2,1,0:T(8,128)(2,1)}), bf16[4,224,1024]{2,1,0:T(8,128)(2,1)}, u32[]{:S(2)}, u32[]{:S(2)}) %all-to-all-start.3) | async-done | bytes 1835040 | tf_op jit(solution)/shard_map/all_to_all | solution.py:628
  598.4 34.4 %collective-permute-done.28.refs_3_ = bf16[448,1024]{1,0:T(8,128)(2,1)} collective-permute-done((bf16[448,1024]{1,0:T(8,128)(2,1)}, bf16[448,1024]{1,0:T(8,128)(2,1)}, u32[]{:S(2)}, u32[]{:S(2)}) %collective-permute-start.28) | collective-permute-done | bytes 917536 | tf_op jit(solution)/shard_map/ppermute | solution.py:612
  633.2 19.2 %collective-permute-done.30.refs_5_ = bf16[448,1024]{1,0:T(8,128)(2,1)} collective-permute-done((bf16[448,1024]{1,0:T(8,128)(2,1)S(1)}, bf16[448,1024]{1,0:T(8,128)(2,1)}, u32[]{:S(2)}, u32[]{:S(2)}) %collective-permute-start.30) | collective-permute-done | bytes 917536 | tf_op jit(solution)/shard_map/ppermute | solution.py:612
  654.1 33.8 %shard_map.203 = (bf16[3072,1024]{1,0:T(8,128)(2,1)}, bf16[3072,256]{1,0:T(8,128)(2,1)}) custom-call(s32[7]{0:T(128)S(1)} %stack.92.first_ref, s32[3072,1]{1,0:T(8,128)} %fusion.21.place_ref, bf16[3072,1024]{1,0:T(8,128)(2,1)} %base_ref.1, bf16[896,1024]{1,0:T(8,128)(2,1)} %bitcast.43.refs_0_, bf16[448,1024]{1,0:T(8,128)(2,1)S(1)} %collective-permute-done.26.refs_1_, ...), custom_call_target="tpu_custom_call" | custom-call | flops 24159191040 | bytes 19922944 | tf_op jit(solution)/shard_map/pallas_call | solution.py:423
  689.3 27.0 %shard_map.204 = bf16[3072,768]{1,0:T(8,128)(2,1)} custom-call(s32[3]{0:T(128)S(1)} %copy-done.18, bf16[3072,768]{1,0:T(8,128)(2,1)} %copy-done, bf16[3072,768]{1,0:T(8,128)(2,1)} %copy-done, bf16[3072,768]{1,0:T(8,128)(2,1)} %copy-done, bf16[3072,256]{1,0:T(8,128)(2,1)S(1)} %copy-done.2, bf16[3072,256]{1,0:T(8,128)(2,1)S(1)} %copy-done.32, ...), custom_call_target="tpu_custom_call" | custom-call | flops 8053063680 | bytes 12582912 | tf_op jit(solution)/shard_map/pallas_call | solution.py:222
  764.9 22.4 %collective-permute-done.50 = bf16[1024,1024]{1,0:T(8,128)(2,1)} collective-permute-done((bf16[1024,1024]{1,0:T(8,128)(2,1)}, bf16[1024,1024]{1,0:T(8,128)(2,1)}, u32[]{:S(2)}, u32[]{:S(2)}) %collective-permute-start.50) | collective-permute-done | bytes 2097184 | tf_op jit(solution)/shard_map/ppermute | solution.py:612
  793.2 17.2 %collective-permute-start.57 = (bf16[1024,1024]{1,0:T(8,128)(2,1)}, bf16[1024,1024]{1,0:T(8,128)(2,1)}, u32[]{:S(2)}, u32[]{:S(2)}) collective-permute-start(bf16[1024,1024]{1,0:T(8,128)(2,1)} %add_convert_fusion), channel_id=1, source_target_pairs={{0,0},{4,1},{2,2},{6,3},{1,4},{5,5},{3,6},{7,7},{8,8},{12,9},{10,1... | collective-permute-start | bytes 6291464 | tf_op jit(solution)/shard_map/ppermute | solution.py:658
  836.5 23.7 %collective-permute-done.20.refs_2_ = bf16[896,1024]{1,0:T(8,128)(2,1)} collective-permute-done((bf16[896,1024]{1,0:T(8,128)(2,1)}, bf16[896,1024]{1,0:T(8,128)(2,1)}, u32[]{:S(2)}, u32[]{:S(2)}) %collective-permute-start.20) | collective-permute-done | bytes 1835040 | tf_op jit(solution)/shard_map/ppermute | solution.py:612
  882.6 45.3 %collective-permute-done.44 = f32[2,1024]{1,0:T(2,128)S(1)} collective-permute-done((f32[2,1024]{1,0:T(2,128)S(1)}, f32[2,1024]{1,0:T(2,128)S(1)}, u32[]{:S(2)}, u32[]{:S(2)}) %collective-permute-start.44) | collective-permute-done | bytes 8224 | tf_op jit(solution)/shard_map/ppermute | solution.py:612
  942.3 31.7 %shard_map.197 = bf16[3072,1024]{1,0:T(8,128)(2,1)} custom-call(s32[4]{0:T(128)S(1)} %pad_add_fusion.first_ref, s32[3072,1]{1,0:T(8,128)S(1)} %copy-done.12, bf16[3072,1024]{1,0:T(8,128)(2,1)} %shard_map.191.rows_ref.base_ref, bf16[896,1024]{1,0:T(8,128)(2,1)} %bitcast.35.refs_0_, bf16[896,1024]{1,0:T(8,128)(2,1)S(1)} %collective-permute-done.19.refs_1_, ...), custom_call_target="tpu_custom_call" | custom-call | flops 22548578304 | bytes 19922944 | tf_op jit(solution)/shard_map/pallas_call | solution.py:423
  994.8 14.8 %collective-permute-done.38 = bf16[384,1024]{1,0:T(8,128)(2,1)S(1)} collective-permute-done((bf16[384,1024]{1,0:T(8,128)(2,1)}, bf16[384,1024]{1,0:T(8,128)(2,1)S(1)}, u32[]{:S(2)}, u32[]{:S(2)}) %collective-permute-start.38) | collective-permute-done | bytes 786464 | tf_op jit(solution)/shard_map/ppermute | solution.py:612
  (334 shorter events, 467.8 us)
Async XLA Ops:
  51.9 91.2 %collective-permute-start = (bf16[3072,256]{1,0:T(8,128)(2,1)S(1)}, bf16[3072,256]{1,0:T(8,128)(2,1)}, u32[]{:S(2)}, u32[]{:S(2)}) collective-permute-start(bf16[3072,256]{1,0:T(8,128)(2,1)S(1)} %get-tuple-element.48.refs_0_.o_ref), channel_id=1, source_target_pairs={{0,1},{1,0},{2,3},{3,2},{4,5},{5,4},{6,7},{7,6},{8,9},{9,8},{10,11... | collective-permute-start | bytes 4718600 | tf_op jit(solution)/shard_map/ppermute | solution.py:612
  180.9 79.0 %collective-permute-start.10 = (bf16[1024,1024]{1,0:T(8,128)(2,1)}, bf16[1024,1024]{1,0:T(8,128)(2,1)}, u32[]{:S(2)}, u32[]{:S(2)}) collective-permute-start(bf16[1024,1024]{1,0:T(8,128)(2,1)} %collective-permute-done.9.refs_2_.refs_3_.refs_4_), channel_id=1, source_target_pairs={{0,2},{1,3},{2,0},{3,1},{4,6},{5,7},{6,4},{7,5},{8,10},{9,11},{10,... | collective-permute-start | bytes 6291464 | tf_op jit(solution)/shard_map/ppermute | solution.py:612
  181.4 78.5 %collective-permute-start.8 = (bf16[1024,1024]{1,0:T(8,128)(2,1)}, bf16[1024,1024]{1,0:T(8,128)(2,1)}, u32[]{:S(2)}, u32[]{:S(2)}) collective-permute-start(bf16[1024,1024]{1,0:T(8,128)(2,1)} %collective-permute-done.7.refs_0_.refs_1_.refs_2_), channel_id=1, source_target_pairs={{0,2},{1,3},{2,0},{3,1},{4,6},{5,7},{6,4},{7,5},{8,10},{9,11},{10,... | collective-permute-start | bytes 6291464 | tf_op jit(solution)/shard_map/ppermute | solution.py:612
  288.1 92.4 %collective-permute-start.16 = (bf16[1024,1024]{1,0:T(8,128)(2,1)}, bf16[1024,1024]{1,0:T(8,128)(2,1)}, u32[]{:S(2)}, u32[]{:S(2)}) collective-permute-start(bf16[1024,1024]{1,0:T(8,128)(2,1)} %collective-permute-done.15.refs_2_.refs_3_.refs_4_), channel_id=1, source_target_pairs={{0,2},{1,3},{2,0},{3,1},{4,6},{5,7},{6,4},{7,5},{8,10},{9,11},{10,... | collective-permute-start | bytes 6291464 | tf_op jit(solution)/shard_map/ppermute | solution.py:612
  311.9 68.6 %collective-permute-start.17 = (bf16[896,1024]{1,0:T(8,128)(2,1)}, bf16[896,1024]{1,0:T(8,128)(2,1)}, u32[]{:S(2)}, u32[]{:S(2)}) collective-permute-start(bf16[896,1024]{1,0:T(8,128)(2,1)} %get-tuple-element.85.x_ref.refs_0_), channel_id=1, source_target_pairs={{0,4},{4,0},{8,12},{12,8},{16,20},{20,16},{24,28},{28,24},{1,5},{5... | collective-permute-start | bytes 5505032 | tf_op jit(solution)/shard_map/ppermute | solution.py:609
  319.5 92.1 %all-to-all-start.2 = ((bf16[4,224,1024]{2,1,0:T(8,128)(2,1)}), bf16[4,224,1024]{2,1,0:T(8,128)(2,1)}, u32[]{:S(2)}, u32[]{:S(2)}) async-start(bf16[4,224,1024]{2,1,0:T(8,128)(2,1)} %bitcast.125), calls=%async_computation.2 | async-start | bytes 3670016 | tf_op jit(solution)/shard_map/all_to_all | solution.py:628
  537.1 221.5 %all-to-all-start.1 = ((bf16[4,224,1024]{2,1,0:T(8,128)(2,1)}), bf16[4,224,1024]{2,1,0:T(8,128)(2,1)}, u32[]{:S(2)}, u32[]{:S(2)}) async-start(bf16[4,224,1024]{2,1,0:T(8,128)(2,1)} %bitcast.139), calls=%async_computation.1 | async-start | bytes 3670016 | tf_op jit(solution)/shard_map/all_to_all | solution.py:628
  541.5 448.7 %all-reduce.3.cloned.1.call-start = ((), (), s32[]{:S(2)}) async-start(), calls=%async_computation.4 | async-start | bytes 4194304 | tf_op jit(solution)/shard_map/psum | solution.py:883
  552.2 177.1 %collective-permute-start.56 = (bf16[1024,1024]{1,0:T(8,128)(2,1)}, bf16[1024,1024]{1,0:T(8,128)(2,1)}, u32[]{:S(2)}, u32[]{:S(2)}) collective-permute-start(bf16[1024,1024]{1,0:T(8,128)(2,1)} %shard_map.212), channel_id=1, source_target_pairs={{0,2},{1,3},{2,0},{3,1},{4,6},{5,7},{6,4},{7,5},{8,10},{9,11},{10,... | collective-permute-start | bytes 6291464 | tf_op jit(solution)/shard_map/ppermute | solution.py:612
  569.8 63.0 %collective-permute-start.28 = (bf16[448,1024]{1,0:T(8,128)(2,1)}, bf16[448,1024]{1,0:T(8,128)(2,1)}, u32[]{:S(2)}, u32[]{:S(2)}) collective-permute-start(bf16[448,1024]{1,0:T(8,128)(2,1)} %bitcast.44), channel_id=1, source_target_pairs={{0,2},{1,3},{2,0},{3,1},{4,6},{5,7},{6,4},{7,5},{8,10},{9,11},{10,... | collective-permute-start | bytes 2752520 | tf_op jit(solution)/shard_map/ppermute | solution.py:612
  570.3 82.2 %collective-permute-start.30 = (bf16[448,1024]{1,0:T(8,128)(2,1)S(1)}, bf16[448,1024]{1,0:T(8,128)(2,1)}, u32[]{:S(2)}, u32[]{:S(2)}) collective-permute-start(bf16[448,1024]{1,0:T(8,128)(2,1)S(1)} %collective-permute-done.26.refs_1_), channel_id=1, source_target_pairs={{0,2},{1,3},{2,0},{3,1},{4,6},{5,7},{6,4},{7,5},{8,10},{9,11},{10,... | collective-permute-start | bytes 2752520 | tf_op jit(solution)/shard_map/ppermute | solution.py:612
  571.8 81.1 %collective-permute-start.31 = (bf16[448,1024]{1,0:T(8,128)(2,1)S(1)}, bf16[448,1024]{1,0:T(8,128)(2,1)}, u32[]{:S(2)}, u32[]{:S(2)}) collective-permute-start(bf16[448,1024]{1,0:T(8,128)(2,1)S(1)} %collective-permute-done.29.refs_4_), channel_id=1, source_target_pairs={{0,1},{1,0},{2,3},{3,2},{4,5},{5,4},{6,7},{7,6},{8,9},{9,8},{10,11... | collective-permute-start | bytes 2752520 | tf_op jit(solution)/shard_map/ppermute | solution.py:612
  597.9 135.4 %collective-permute-start.52 = (bf16[1024,1024]{1,0:T(8,128)(2,1)}, bf16[1024,1024]{1,0:T(8,128)(2,1)}, u32[]{:S(2)}, u32[]{:S(2)}) collective-permute-start(bf16[1024,1024]{1,0:T(8,128)(2,1)} %shard_map.208), channel_id=1, source_target_pairs={{0,2},{1,3},{2,0},{3,1},{4,6},{5,7},{6,4},{7,5},{8,10},{9,11},{10,... | collective-permute-start | bytes 6291464 | tf_op jit(solution)/shard_map/ppermute | solution.py:612
  632.8 125.8 %collective-permute-start.54 = (bf16[1024,1024]{1,0:T(8,128)(2,1)}, bf16[1024,1024]{1,0:T(8,128)(2,1)}, u32[]{:S(2)}, u32[]{:S(2)}) collective-permute-start(bf16[1024,1024]{1,0:T(8,128)(2,1)} %shard_map.210), channel_id=1, source_target_pairs={{0,2},{1,3},{2,0},{3,1},{4,6},{5,7},{6,4},{7,5},{8,10},{9,11},{10,... | collective-permute-start | bytes 6291464 | tf_op jit(solution)/shard_map/ppermute | solution.py:612
  652.4 134.8 %collective-permute-start.50 = (bf16[1024,1024]{1,0:T(8,128)(2,1)}, bf16[1024,1024]{1,0:T(8,128)(2,1)}, u32[]{:S(2)}, u32[]{:S(2)}) collective-permute-start(bf16[1024,1024]{1,0:T(8,128)(2,1)} %shard_map.206), channel_id=1, source_target_pairs={{0,2},{1,3},{2,0},{3,1},{4,6},{5,7},{6,4},{7,5},{8,10},{9,11},{10,... | collective-permute-start | bytes 6291464 | tf_op jit(solution)/shard_map/ppermute | solution.py:612
  745.0 65.4 %collective-permute-start.36 = (bf16[768,512]{1,0:T(8,128)(2,1)}, bf16[768,512]{1,0:T(8,128)(2,1)}, u32[]{:S(2)}, u32[]{:S(2)}) collective-permute-start(bf16[768,512]{1,0:T(8,128)(2,1)} %get-tuple-element.92), channel_id=1, source_target_pairs={{0,2},{1,3},{2,0},{3,1},{4,6},{5,7},{6,4},{7,5},{8,10},{9,11},{10,... | collective-permute-start | bytes 2359304 | tf_op jit(solution)/shard_map/ppermute | solution.py:612
  748.8 72.1 %collective-permute-start.34 = (bf16[768,512]{1,0:T(8,128)(2,1)}, bf16[768,512]{1,0:T(8,128)(2,1)}, u32[]{:S(2)}, u32[]{:S(2)}) collective-permute-start(bf16[768,512]{1,0:T(8,128)(2,1)} %fusion.25), channel_id=1, source_target_pairs={{0,2},{1,3},{2,0},{3,1},{4,6},{5,7},{6,4},{7,5},{8,10},{9,11},{10,... | collective-permute-start | bytes 2359304 | tf_op jit(solution)/shard_map/ppermute | solution.py:612
  758.6 101.7 %collective-permute-start.20 = (bf16[896,1024]{1,0:T(8,128)(2,1)}, bf16[896,1024]{1,0:T(8,128)(2,1)}, u32[]{:S(2)}, u32[]{:S(2)}) collective-permute-start(bf16[896,1024]{1,0:T(8,128)(2,1)} %bitcast.35.refs_0_), channel_id=1, source_target_pairs={{0,2},{1,3},{2,0},{3,1},{4,6},{5,7},{6,4},{7,5},{8,10},{9,11},{10,... | collective-permute-start | bytes 5505032 | tf_op jit(solution)/shard_map/ppermute | solution.py:612
  787.2 146.4 %collective-permute-start.19 = (bf16[896,1024]{1,0:T(8,128)(2,1)}, bf16[896,1024]{1,0:T(8,128)(2,1)S(1)}, u32[]{:S(2)}, u32[]{:S(2)}) collective-permute-start(bf16[896,1024]{1,0:T(8,128)(2,1)} %bitcast.35.refs_0_), channel_id=1, source_target_pairs={{0,1},{1,0},{2,3},{3,2},{4,5},{5,4},{6,7},{7,6},{8,9},{9,8},{10,11... | collective-permute-start | bytes 5505032 | tf_op jit(solution)/shard_map/ppermute | solution.py:612
  793.2 144.2 %collective-permute-start.57 = (bf16[1024,1024]{1,0:T(8,128)(2,1)}, bf16[1024,1024]{1,0:T(8,128)(2,1)}, u32[]{:S(2)}, u32[]{:S(2)}) collective-permute-start(bf16[1024,1024]{1,0:T(8,128)(2,1)} %add_convert_fusion), channel_id=1, source_target_pairs={{0,0},{4,1},{2,2},{6,3},{1,4},{5,5},{3,6},{7,7},{8,8},{12,9},{10,1... | collective-permute-start | bytes 6291464 | tf_op jit(solution)/shard_map/ppermute | solution.py:658
  810.4 64.9 %collective-permute-start.35 = (bf16[768,512]{1,0:T(8,128)(2,1)}, bf16[768,512]{1,0:T(8,128)(2,1)}, u32[]{:S(2)}, u32[]{:S(2)}) collective-permute-start(bf16[768,512]{1,0:T(8,128)(2,1)} %get-tuple-element.93), channel_id=1, source_target_pairs={{0,2},{1,3},{2,0},{3,1},{4,6},{5,7},{6,4},{7,5},{8,10},{9,11},{10,... | collective-permute-start | bytes 2359304 | tf_op jit(solution)/shard_map/ppermute | solution.py:612
  860.3 123.1 %collective-permute-start.53 = (bf16[1024,1024]{1,0:T(8,128)(2,1)}, bf16[1024,1024]{1,0:T(8,128)(2,1)S(1)}, u32[]{:S(2)}, u32[]{:S(2)}) collective-permute-start(bf16[1024,1024]{1,0:T(8,128)(2,1)} %add_convert_fusion.2), channel_id=1, source_target_pairs={{0,0},{4,1},{2,2},{6,3},{1,4},{5,5},{3,6},{7,7},{8,8},{12,9},{10,1... | collective-permute-start | bytes 6291464 | tf_op jit(solution)/shard_map/ppermute | solution.py:658
  938.2 71.4 %collective-permute-start.38 = (bf16[384,1024]{1,0:T(8,128)(2,1)}, bf16[384,1024]{1,0:T(8,128)(2,1)S(1)}, u32[]{:S(2)}, u32[]{:S(2)}) collective-permute-start(bf16[384,1024]{1,0:T(8,128)(2,1)} %get-tuple-element.106), channel_id=1, source_target_pairs={{0,1},{1,0},{2,3},{3,2},{4,5},{5,4},{6,7},{7,6},{8,9},{9,8},{10,11... | collective-permute-start | bytes 2359304 | tf_op jit(solution)/shard_map/ppermute | solution.py:612
  940.8 70.4 %collective-permute-start.41 = (bf16[384,1024]{1,0:T(8,128)(2,1)}, bf16[384,1024]{1,0:T(8,128)(2,1)S(1)}, u32[]{:S(2)}, u32[]{:S(2)}) collective-permute-start(bf16[384,1024]{1,0:T(8,128)(2,1)} %get-tuple-element.105), channel_id=1, source_target_pairs={{0,2},{1,3},{2,0},{3,1},{4,6},{5,7},{6,4},{7,5},{8,10},{9,11},{10,... | collective-permute-start | bytes 2359304 | tf_op jit(solution)/shard_map/ppermute | solution.py:612
  (97 other events, 2335.4 us)
Sparse Core Ops, SparseCore 0:
  836.6 64.3 all-reduce.2

commit v5 on v4

--- a/solution.py
+++ b/solution.py
@@ -13,6 +13,10 @@
 F32 = jnp.float32
 BF16 = jnp.bfloat16
 CORES = 2
+
+
+def after(value, *others):
+    return lax.optimization_barrier((value, *others))[0]
 
 
 def dot(a, b, contract):
@@ -473,8 +477,8 @@
 
 def expert_forward(x, w_in, w_out, base=None):
     rows, width = x.shape
-    count = len(w_in)
-    hidden = sum(w.shape[1] for w in w_in)
+    count, unused, inner = w_in.shape
+    hidden = count * inner
     tile = rows // 2
 
     def row(n):
@@ -488,7 +492,13 @@
         args.append(base)
     else:
         kernel = without_base(kernel, 1)
-    specs += [pl.BlockSpec(w.shape, lambda i: (0, 0), pipeline_mode=pl.Buffered(1)) for w in (*w_in, *w_out)]
+    specs += [
+        pl.BlockSpec(
+            (None, *w.shape[1:]), functools.partial(lambda j, i: (j, 0, 0), j), pipeline_mode=pl.Buffered(1)
+        )
+        for w in (w_in, w_out)
+        for j in range(count)
+    ]
     return pl.pallas_call(
         kernel,
         grid=(rows // tile,),
@@ -505,7 +515,7 @@
             bytes_accessed=4 * width * hidden + 4 * rows * hidden + 6 * rows * width,
             transcendentals=2 * rows * hidden,
         ),
-    )(*args, *w_in, *w_out)
+    )(*args, *[w_in] * count, *[w_out] * count)
 
 
 def expert_backward_kernel(count, g_ref, slope_ref, base_ref, *refs):
@@ -535,7 +545,7 @@
 
 def expert_backward(g, slope, w_in, w_out, base=None):
     rows, width = g.shape
-    count = len(w_in)
+    count, unused, inner = w_in.shape
     hidden = slope.shape[1]
     tile = rows // 2
 
@@ -550,7 +560,13 @@
         args.append(base)
     else:
         kernel = without_base(kernel, 2)
-    specs += [pl.BlockSpec(w.shape, lambda i: (0, 0), pipeline_mode=pl.Buffered(1)) for w in (*w_in, *w_out)]
+    specs += [
+        pl.BlockSpec(
+            (None, *w.shape[1:]), functools.partial(lambda j, i: (j, 0, 0), j), pipeline_mode=pl.Buffered(1)
+        )
+        for w in (w_in, w_out)
+        for j in range(count)
+    ]
     return pl.pallas_call(
         kernel,
         grid=(rows // tile,),
@@ -566,7 +582,7 @@
             bytes_accessed=4 * width * hidden + 4 * rows * hidden + 6 * rows * width,
             transcendentals=0,
         ),
-    )(*args, *w_in, *w_out)
+    )(*args, *[w_in] * count, *[w_out] * count)
 
 
 def outer_kernel(count, *refs):
@@ -578,22 +594,31 @@
     out_ref[...] = total.astype(out_ref.dtype)
 
 
-def outer(lefts, rights, left_block, right_block, left_width, right_width):
+def outer(lefts, rights, blocks):
     rows = lefts[0].shape[0]
     count = len(lefts)
+    left_blocks = blocks if lefts[0].shape[1] > rights[0].shape[1] else 1
+    right_blocks = blocks // left_blocks
+    left_width = lefts[0].shape[1] // left_blocks
+    right_width = rights[0].shape[1] // right_blocks
     tile = min(256, left_width)
     steps = left_width // tile
+    if left_blocks > 1:
+        left_spec = pl.BlockSpec((rows, tile), lambda j, i: (0, j * steps + i))
+        right_spec = pl.BlockSpec((rows, right_width), lambda j, i: (0, 0))
+    else:
+        left_spec = pl.BlockSpec((rows, tile), lambda j, i: (0, i))
+        right_spec = pl.BlockSpec((rows, right_width), lambda j, i: (0, j))
     return pl.pallas_call(
         functools.partial(outer_kernel, count),
-        grid=(steps,),
-        in_specs=[pl.BlockSpec((rows, tile), lambda i: (0, left_block * steps + i))] * count
-        + [pl.BlockSpec((rows, right_width), lambda i: (0, right_block))] * count,
-        out_specs=pl.BlockSpec((tile, right_width), lambda i: (i, 0)),
-        out_shape=jax.ShapeDtypeStruct((left_width, right_width), BF16),
+        grid=(blocks, steps),
+        in_specs=[left_spec] * count + [right_spec] * count,
+        out_specs=pl.BlockSpec((None, tile, right_width), lambda j, i: (j, i, 0)),
+        out_shape=jax.ShapeDtypeStruct((blocks, left_width, right_width), BF16),
         compiler_params=pltpu.CompilerParams(vmem_limit_bytes=48 << 20),
         cost_estimate=pl.CostEstimate(
-            flops=2 * count * rows * left_width * right_width,
-            bytes_accessed=2 * (count * rows * (left_width + right_width) + left_width * right_width),
+            flops=2 * count * blocks * rows * left_width * right_width,
+            bytes_accessed=2 * blocks * (count * rows * (left_width + right_width) + left_width * right_width),
             transcendentals=0,
         ),
     )(*lefts, *rights)
@@ -611,11 +636,15 @@
     def over_tensor(self, value, other):
         return lax.ppermute(value, "tensor", [(t, t ^ other) for t in range(self.size)])
 
-    def sum_all(self, value):
+    def sum_tensor(self, value):
         step = 1
         while step < self.size:
             value = value + self.over_tensor(value, step)
             step *= 2
+        return value
+
+    def sum_all(self, value):
+        value = self.sum_tensor(value)
         step = 1
         while step < self.experts:
             pairs = [(d, d ^ step) for d in range(self.experts)]
@@ -628,6 +657,9 @@
         return lax.all_to_all(
             value, "dp", split_axis=0, concat_axis=0, axis_index_groups=groups, tiled=True
         )
+
+
+ROWS_OF_CHIPS = [[0, 2], [1, 3]]
 
 
 def owner_pairs(grid, back=False):
@@ -637,50 +669,82 @@
             for y in range(2):
                 for x in range(2):
                     here = (CORES * z + core) * 4 + 2 * y + x
-                    there = (CORES * z + x) * 4 + 2 * y + core
+                    there = (CORES * z + 1 - x) * 4 + 2 * y + core
                     pairs.append((there, here) if back else (here, there))
     return pairs
 
 
+def fetch_near(grid, weight):
+    return lax.ppermute(weight, ("dp", "tensor"), owner_pairs(grid)) if grid.size == 4 else weight
+
+
 def fetch_hidden(grid, weight):
     if grid.size == 4:
-        near = lax.ppermute(weight, ("dp", "tensor"), owner_pairs(grid))
-        return [near, grid.over_tensor(near, 2)]
+        return lax.all_gather(weight, "tensor", axis=0, axis_index_groups=ROWS_OF_CHIPS, tiled=False)
     core = lax.axis_index("dp") % CORES
     every = lax.all_gather(weight, "tensor", axis=0, tiled=False)
     chosen = jnp.where(lax.axis_index("tensor") % 2 == core, every, grid.over_core(every))
-    return [jnp.where(core == 0, chosen[t], chosen[t + 1]) for t in range(0, grid.size, 2)]
+    chosen = chosen.reshape(grid.size // 2, 2, *weight.shape)
+    return jnp.where(core == 0, chosen[:, 0], chosen[:, 1])
+
+
+def sum_hidden(grid, pieces):
+    if grid.size != 4:
+        return pieces
+    return lax.psum_scatter(
+        pieces, "tensor", scatter_dimension=0, axis_index_groups=ROWS_OF_CHIPS, tiled=False
+    )
 
 
 def return_hidden(grid, pieces):
     if grid.size == 4:
-        total = pieces[0].astype(F32) + grid.over_tensor(pieces[1], 2).astype(F32)
-        return lax.ppermute(total.astype(BF16), ("dp", "tensor"), owner_pairs(grid, True)).astype(F32)
+        return lax.ppermute(pieces, ("dp", "tensor"), owner_pairs(grid, True))
     core = lax.axis_index("dp") % CORES
     me = lax.axis_index("tensor")
-    zero = jnp.zeros_like(pieces[0])
-    wide = []
-    for parity in range(2):
-        row = []
-        for piece in pieces:
-            row += [jnp.where((me % 2 == parity) & (core == c), piece, zero) for c in range(CORES)]
-        wide.append(jnp.stack(row))
-    mine = lax.psum_scatter(jnp.stack(wide), "tensor", scatter_dimension=1, tiled=False)
+    zero = jnp.zeros_like(pieces)
+    row = jnp.stack([jnp.where(core == c, pieces, zero) for c in range(CORES)], axis=1)
+    row = row.reshape(grid.size, *pieces.shape[1:])
+    wide = jnp.stack([jnp.where(me % 2 == parity, row, jnp.zeros_like(row)) for parity in range(2)])
+    mine = lax.psum_scatter(wide, "tensor", scatter_dimension=1, tiled=False)
     other = grid.over_core(jnp.where(core == 0, mine[1], mine[0]))
-    return jnp.where(core == 0, mine[0], mine[1]).astype(F32) + other.astype(F32)
-
-
-def gather_pieces(grid, value, balanced):
+    total = jnp.where(core == 0, mine[0], mine[1]).astype(F32) + other.astype(F32)
+    return total.astype(BF16)
+
+
+class Gather:
+    def __init__(self, grid, value):
+        self.grid = grid
+        if grid.size != 4:
+            self.pieces = [lax.all_gather(value, "tensor", axis=0, tiled=True)]
+            self.devices = [jnp.int32(0)]
+            return
+        me = lax.axis_index("tensor")
+        self.pieces = [value, grid.over_tensor(value, 1), grid.over_tensor(value, 2)]
+        self.devices = [jnp.bitwise_xor(me, other) for other in range(4)]
+
+    def ready(self):
+        return self.pieces[1:3]
+
+    def joined(self):
+        if self.grid.size != 4:
+            return self.pieces[0]
+        rows, width = self.pieces[0].shape
+        out = jnp.zeros((4 * rows, width), self.pieces[0].dtype)
+        for piece, device in zip(self.pieces, self.devices):
+            out = lax.dynamic_update_slice(out, piece, (device * rows, 0))
+        return out
+
+    def finish(self, *others, over=1):
+        if self.grid.size == 4:
+            self.pieces.append(self.grid.over_tensor(after(self.pieces[3 - over], *others), over))
+        return self.pieces
+
+
+def gather_rows(grid, value):
     if grid.size != 4:
-        every = lax.all_gather(value, "tensor", axis=0, tiled=True)
-        return [every], [jnp.int32(0)], [0]
-    me = lax.axis_index("tensor")
-    if not balanced:
-        from_y = grid.over_tensor(value, 2)
-        from_x = grid.over_tensor(value, 1)
-        from_xy = grid.over_tensor(from_y, 1)
-        return [value, from_x, from_y, from_xy], [jnp.bitwise_xor(me, o) for o in range(4)], [0] * 4
-    half = value.shape[0] // 2
+        return lax.all_gather(value, "tensor", axis=0, tiled=True)
+    rows, width = value.shape
+    half = rows // 2
     first, second = value[:half], value[half:]
     first_x = grid.over_tensor(first, 1)
     second_y = grid.over_tensor(second, 2)
@@ -688,26 +752,21 @@
     second_x = grid.over_tensor(second, 1)
     first_xy = grid.over_tensor(first_x, 2)
     second_xy = grid.over_tensor(second_y, 1)
-    pieces = [value, first_x, second_x, first_y, second_y, first_xy, second_xy]
-    devices = [jnp.bitwise_xor(me, o) for o in (0, 1, 1, 2, 2, 3, 3)]
-    return pieces, devices, [0, 0, half, 0, half, 0, half]
-
-
-def gather_rows(grid, value, balanced=True):
-    pieces, devices, starts = gather_pieces(grid, value, balanced)
-    if len(pieces) == 1:
-        return pieces[0]
-    rows, width = value.shape
-    out = jnp.zeros((grid.size * rows, width), value.dtype)
-    for piece, device, start in zip(pieces, devices, starts):
-        out = lax.dynamic_update_slice(out, piece, (device * rows + start, 0))
+    me = lax.axis_index("tensor")
+    out = jnp.zeros((4 * rows, width), value.dtype)
+    out = lax.dynamic_update_slice(out, value, (me * rows, 0))
+    for other, top, bottom in ((1, first_x, second_x), (2, first_y, second_y), (3, first_xy, second_xy)):
+        place = jnp.bitwise_xor(me, other) * rows
+        out = lax.dynamic_update_slice(out, top, (place, 0))
+        out = lax.dynamic_update_slice(out, bottom, (place + half, 0))
     return out
 
 
 def scatter_rows(grid, term):
     size, rows, width = term.shape
     if size != 4:
-        return lax.psum_scatter(term.astype(BF16), "tensor", scatter_dimension=0, tiled=False).astype(F32)
+        total = lax.psum_scatter(term.astype(BF16), "tensor", scatter_dimension=0, tiled=False)
+        return total.astype(F32), []
     me = lax.axis_index("tensor")
     half = width // 2
 
@@ -715,14 +774,15 @@
         place = jnp.bitwise_xor(me, other)
         return lax.dynamic_slice(term, (place, 0, low), (1, rows, half))[0]
 
-    totals = []
+    totals, arrived = [], []
     for low, near, far in ((0, 1, 2), (half, 2, 1)):
         got_far = grid.over_tensor(pick(3, low).astype(BF16), near)
         got_own = grid.over_tensor(pick(near, low).astype(BF16), near)
         onward = pick(far, low).astype(F32) + got_far.astype(F32)
         got = grid.over_tensor(onward.astype(BF16), far)
+        arrived.append(got)
         totals.append(pick(0, low).astype(F32) + got_own.astype(F32) + got.astype(F32))
-    return jnp.concatenate(totals, axis=1)
+    return jnp.concatenate(totals, axis=1), arrived
 
 
 def body(
@@ -758,12 +818,11 @@
     own_rows = depth * share
     tok_rows = tok_count // shards
 
-    win, wout = [], []
-    for k in range(2):
-        win.append(fetch_hidden(grid, expert_in[0, k]))
-        wout.append(fetch_hidden(grid, expert_out[0, k]))
+    near = [fetch_near(grid, w[0, k]) for k in range(2) for w in (expert_in, expert_out)]
     out_flat = out_weight.reshape(heads_here * head_size, model_width)
-    out_all = gather_rows(grid, out_flat, False)
+    out_gather = Gather(grid, out_flat)
+    out_gather.finish(over=2)
+    out_all = out_gather.joined()
     centroid = jnp.where(parity == core, centroids[0], grid.over_core(centroids[0]))
 
     slots = token_slots(
@@ -780,11 +839,11 @@
         picked = pick_rows(rows, slots, own_first, depth, share, CORES, padded)
         return grid.exchange_depth(picked.reshape(depth, share, model_width)).reshape(own_rows, model_width)
 
-    def from_experts(rows, balanced):
-        moved = grid.exchange_depth(rows.reshape(depth, share, model_width))
-        pieces, devices, starts = gather_pieces(grid, moved.reshape(own_rows, model_width), balanced)
-        first = [device * own_rows + start for device, start in zip(devices, starts)]
-        return pieces, jnp.stack(first).astype(jnp.int32)
+    def leave_experts(rows):
+        return grid.exchange_depth(rows.reshape(depth, share, model_width))
+
+    def row_starts(gathered):
+        return jnp.stack([device * own_rows for device in gathered.devices]).astype(jnp.int32)
 
     grad_ret = to_experts(cotangent).astype(F32)
     heads = heads_here + heads_here % 2
@@ -794,10 +853,14 @@
     fused = fused.reshape(model_width, 3 * heads * head_size)
     inner = heads_here * head_size
     ln_in, projected = norm_project(tokens, norm_gain, norm_bias, fused)
+    near[0] = after(near[0], projected)
     attended, log_total = attend(projected, lengths, seq_count, heads, head_size)
+    near[1:] = [after(piece, attended) for piece in near[1:]]
+    win, wout = [fetch_hidden(grid, w) for w in near[::2]], [fetch_hidden(grid, w) for w in near[1::2]]
     if shards == 4:
-        pieces, devices, unused = gather_pieces(grid, attended, False)
-        first = jnp.stack(devices).astype(jnp.int32)
+        gathered = Gather(grid, attended)
+        pieces = gathered.finish()
+        first = jnp.stack(gathered.devices).astype(jnp.int32)
     else:
         every = lax.all_gather(attended[:, :inner], "tensor", axis=1, tiled=True)
         pieces, first = [every], jnp.zeros((1,), jnp.int32)
@@ -814,8 +877,7 @@
         act_there, slope_there, part = expert_forward(there, win[k], wout[k])
         current = total + grid.over_core(part).astype(F32)
         saved.append(([here, there], [act, act_there], [slope, slope_there]))
-    pieces, first = from_experts((gate * current).astype(BF16), False)
-    output = combine(pieces, first, place, sent)[0]
+    returned = leave_experts((gate * current).astype(BF16))
 
     grad_gate = jnp.sum(grad_ret * current, axis=1, keepdims=True)
     grad_logit = grad_gate * gate * (1.0 - gate)
@@ -831,35 +893,45 @@
         branches[k] = ([here, there], [grad_pre, grad_pre_there])
     grad_rows = (grad_current + grad_logit * centroid.astype(F32)[None, :]).astype(BF16)
     centroid_part = jnp.sum(grad_logit * expert_rows.astype(F32), axis=0, keepdims=True)
-    centroid_parts = lax.psum(
-        jnp.concatenate([jnp.where(parity == p, centroid_part, 0.0) for p in range(2)], axis=0), "tensor"
-    )
-    centroid_parts = centroid_parts + grid.over_core(centroid_parts)
-    grad_centroid = lax.dynamic_slice_in_dim(centroid_parts, core, 1, 0)
-    pieces, first = from_experts(grad_rows, True)
-    hidden = expert_in.shape[3]
-    grads_in, grads_back = [None, None], [None, None]
+    centroid_parts = jnp.concatenate(
+        [jnp.where(parity == p, centroid_part, 0.0) for p in range(2)], axis=0
+    )
+
+    moved = leave_experts(grad_rows)
+    outers, sums = [], []
     for k in (1, 0):
         rows_in, acts, unused = saved[k]
         branch, grad_pres = branches[k]
-        blocks = range(len(win[k]))
-        grads_back[k] = return_hidden(
-            grid, [outer(acts, branch, j, 0, hidden, model_width) for j in blocks]
-        )
-        grads_in[k] = return_hidden(
-            grid, [outer(rows_in, grad_pres, 0, j, model_width, hidden) for j in blocks]
-        )
+        blocks = win[k].shape[0]
+        outers += [outer(rows_in, grad_pres, blocks), outer(acts, branch, blocks)]
+    sums_in2, sums_back2, sums_in1, sums_back1 = [sum_hidden(grid, pieces) for pieces in outers]
+    moved = after(moved, *outers)
+    grad_gather = Gather(grid, moved.reshape(own_rows, model_width))
+    pieces = grad_gather.finish()
+    first = row_starts(grad_gather)
     out_padded = jnp.pad(out_flat, ((0, heads * head_size - inner), (0, 0)))
     grad_mixed, grad_attended = combine(pieces, first, place, cotangent, out_padded)
+    out_gather = Gather(grid, after(returned, *pieces[1:]).reshape(own_rows, model_width))
+    out_first = row_starts(out_gather)
+    back_in2 = return_hidden(grid, after(sums_in2, *pieces[1:]))
+    back_out2 = return_hidden(grid, after(sums_back2, *pieces[1:]))
+    grad_projected = attend_back(
+        projected, attended, grad_attended, log_total, lengths, seq_count, heads, head_size
+    )
+    grad_projected = after(grad_projected, back_in2, back_out2, *out_gather.ready())
+    out_pieces = out_gather.finish()
     grad_out_local = dot(attended[:, :inner], grad_mixed, ((0,), (0,))).reshape(
         heads_here, head_size, model_width
     )
-    grad_projected = attend_back(
-        projected, attended, grad_attended, log_total, lengths, seq_count, heads, head_size
-    )
     grad_qkv_local = dot(ln_in, grad_projected, ((0,), (0,)))
     grad_ln_part = dot(grad_projected, fused, ((1,), (1,))).astype(BF16)
-    grad_ln = scatter_rows(grid, grad_ln_part.reshape(shards, tok_rows, model_width))
+    grad_ln, scattered = scatter_rows(grid, grad_ln_part.reshape(shards, tok_rows, model_width))
+    scattered = scattered + [grad_projected]
+    back_in1 = return_hidden(grid, after(sums_in1, *scattered))
+    back_out1 = return_hidden(grid, after(sums_back1, *scattered))
+    centroid_parts = grid.sum_tensor(after(centroid_parts, *scattered))
+    centroid_parts = centroid_parts + grid.over_core(centroid_parts)
+    grad_centroid = lax.dynamic_slice_in_dim(centroid_parts, core, 1, 0)
 
     def own(rows):
         return lax.dynamic_slice_in_dim(rows, me * tok_rows, tok_rows, 0)
@@ -875,6 +947,7 @@
         grad_normed - mean_plain - own_normed * mean_cross
     )
     grad_tokens = gather_rows(grid, grad_input.astype(BF16))
+    output = combine(out_pieces, out_first, place, after(sent, *scattered))[0]
     norm_total = jnp.stack([jnp.sum(grad_ln * own_normed, axis=0), jnp.sum(grad_ln, axis=0)])
     norm_total = grid.sum_all(norm_total)
     norm_total = lax.dynamic_slice_in_dim(
@@ -893,8 +966,8 @@
         grad_qkv_weight,
         grad_out_weight.astype(F32),
         grad_centroid,
-        jnp.stack(grads_in)[None],
-        jnp.stack(grads_back)[None],
+        jnp.stack([back_in1, back_in2])[None].astype(F32),
+        jnp.stack([back_out1, back_out2])[None].astype(F32),
     )
 
 

time: 1060 us -> 991 us (0.935); the launches traced: 1040 us -> 986 us
  starting transfers between devices: 157 us -> 58.7 us
  waiting for transfers between devices: 369 us -> 420 us
  other arithmetic: 85.7 us -> 71 us
    ppermute x37 -> x28, waiting for transfers between devices: 312 us -> 250 us  [over_tensor(): lax.ppermute(value, 'tensor', [(t, t ^ other) for t in range(self.size)])]
    ppermute x8, starting transfers between devices: 60.5 us -> 1.5 us  [the longest x4 1.02 us: return_hidden(): return lax.ppermute(pieces, ('dp', 'tensor'), owner_pairs(grid, True))]
    reduce_scatter x0 -> x4, waiting for transfers between devices: none -> 55.7 us  [sum_hidden(): lax.psum_scatter(pieces, 'tensor', scatter_dimension=0, axis_index_groups...]
    ppermute x10, starting transfers between devices: 29.4 us -> 2.67 us  [over_core(): return lax.ppermute(value, 'dp', [(d, d ^ 1) for d in range(self.experts)])]
    all_gather x0 -> x4, waiting for transfers between devices: none -> 23.6 us  [fetch_hidden(): lax.all_gather(weight, 'tensor', axis=0, axis_index_groups=ROWS_OF_CHIPS,...]
    ppermute x8, waiting for transfers between devices: 0.02 us -> 22.7 us  [the longest x4 12.3 us: return_hidden(): return lax.ppermute(pieces, ('dp', 'tensor'), owner_pairs(grid, True))]
    ppermute x37 -> x28, starting transfers between devices: 41.9 us -> 31.6 us  [over_tensor(): lax.ppermute(value, 'tensor', [(t, t ^ other) for t in range(self.size)])]
    unnamed x117 -> x89, local copies, waits for them, and re-layouts: 17.4 us -> 26.4 us
  transfers between devices with their start and end apart: 63 -> 62, of which waited for: 21 -> 27; matrix products, arithmetic and copies ran while one was open for 12% -> 11% of each run, Pallas kernels for 25% -> 31%
where the time goes in v5:
time: 991 us; the launch traced here: 986 us
  waiting for transfers between devices  420 us (42%)
  Pallas kernels  336 us (34%)
  other arithmetic  71 us (7%)
  local copies, waits for them, and re-layouts  64.2 us (6%)
  starting transfers between devices  58.7 us (6%)
  matrix products  20.7 us (2%)
  between operations  14.9 us (2%)
    ppermute x28, waiting for transfers between devices, over_tensor(): lax.ppermute(value, 'tensor', [(t, t ^ other) for t in range(self.size)])  250 us
    pallas_call x2, Pallas kernels, combine(): pl.pallas_call(functools.partial(kernel, count), grid_spec=pltpu.Prefetch...  66.9 us
    pallas_call x4, Pallas kernels, expert_backward(): pl.pallas_call(kernel, grid=(rows // tile,), in_specs=specs, out_specs=[r...  56.4 us
    reduce_scatter x4, waiting for transfers between devices, sum_hidden(): lax.psum_scatter(pieces, 'tensor', scatter_dimension=0, axis_index_groups...  55.7 us
    pallas_call x4, Pallas kernels, outer(): pl.pallas_call(functools.partial(outer_kernel, count), grid=(blocks, step...  55.5 us
    pallas_call x4, Pallas kernels, expert_forward(): pl.pallas_call(kernel, grid=(rows // tile,), in_specs=specs, out_specs=[r...  53.1 us
    all_to_all x4, waiting for transfers between devices, exchange_depth(): lax.all_to_all(value, 'dp', split_axis=0, concat_axis=0, axis_index_group...  51.7 us
    ppermute x28, starting transfers between devices, over_tensor(): lax.ppermute(value, 'tensor', [(t, t ^ other) for t in range(self.size)])  31.6 us
  transfers between devices with their start and end apart: 62, of which 27 were waited for; matrix products, arithmetic and copies ran while one was open for 11% of the time, Pallas kernels for 31%

profile of v5, /device:TPU:0, one launch (start us, length us, event | category | flops | bytes accessed | tf_op | source)
XLA Modules:
  0.0 986.0 jit_solution(14832666842080494748)
XLA Ops:
  43.7 24.6 %shard_map.190 = (bf16[3072,256]{1,0:T(8,128)(2,1)S(1)}, f32[3,2,2,1024]{3,2,1,0:T(2,128)S(1)}) custom-call(s32[3]{0:T(128)S(1)} %copy-done.15, bf16[3072,768]{1,0:T(8,128)(2,1)S(1)} %copy-done.1, bf16[3072,768]{1,0:T(8,128)(2,1)S(1)} %copy-done.1, bf16[3072,768]{1,0:T(8,128)(2,1)S(1)} %copy-done.1), custom_call_target="tpu_custom_call" | custom-call | flops 3221225472 | bytes 6291456 | tf_op jit(solution)/shard_map/pallas_call | solution.py:117
  86.6 44.2 %collective-permute-done.1.refs_2_ = bf16[3072,256]{1,0:T(8,128)(2,1)} collective-permute-done((bf16[3072,256]{1,0:T(8,128)(2,1)S(1)}, bf16[3072,256]{1,0:T(8,128)(2,1)}, u32[]{:S(2)}, u32[]{:S(2)}) %collective-permute-start.1) | collective-permute-done | bytes 1572896 | tf_op jit(solution)/shard_map/ppermute | solution.py:637
  149.5 23.1 %collective-permute-done.5 = bf16[256,1024]{1,0:T(8,128)(2,1)} collective-permute-done((bf16[256,1024]{1,0:T(8,128)(2,1)S(1)}, bf16[256,1024]{1,0:T(8,128)(2,1)}, u32[]{:S(2)}, u32[]{:S(2)}) %collective-permute-start.5) | collective-permute-done | bytes 524320 | tf_op jit(solution)/shard_map/ppermute | solution.py:637
  203.0 39.5 %all-to-all-done = bf16[4,224,1024]{2,1,0:T(8,128)(2,1)S(1)} async-done(((bf16[4,224,1024]{2,1,0:T(8,128)(2,1)}), bf16[4,224,1024]{2,1,0:T(8,128)(2,1)S(1)}, u32[]{:S(2)}, u32[]{:S(2)}) %all-to-all-start) | async-done | bytes 1835040 | tf_op jit(solution)/shard_map/all_to_all | solution.py:657
  261.5 13.7 %shard_map.194 = (bf16[896,2048]{1,0:T(8,128)(2,1)S(1)}, bf16[896,2048]{1,0:T(8,128)(2,1)}, f32[896,1024]{1,0:T(8,128)}) custom-call(bf16[896,1024]{1,0:T(8,128)(2,1)S(1)} %bitcast.114, f32[896,1024]{1,0:T(8,128)} %bitcast_convert_fusion.base_ref, bf16[2,1024,1024]{2,1,0:T(8,128)(2,1)} %bitcast.159, bf16[2,1024,1024]{2,1,0:T(8,128)(2,1)} %bitcast.160, ...), custom_call_target="tpu_custom_call" | custom-call | flops 7516192768 | bytes 21233664 | tf_op jit(solution)/shard_map/pallas_call | solution.py:502
  295.1 23.6 %all-gather.15.cloned.1.call-done = bf16[2048,1024]{1,0:T(8,128)(2,1)} async-done(((bf16[1024,1024]{1,0:T(8,128)(2,1)}), bf16[2048,1024]{1,0:T(8,128)(2,1)}) %all-gather.15.cloned.1.call-update) | async-done | bytes 4194320 | tf_op jit(solution)/shard_map/all_gather | solution.py:683
  318.7 13.0 %shard_map.198 = (bf16[896,2048]{1,0:T(8,128)(2,1)}, bf16[896,2048]{1,0:T(8,128)(2,1)}, bf16[896,1024]{1,0:T(8,128)(2,1)}) custom-call(bf16[896,1024]{1,0:T(8,128)(2,1)} %collective-permute-done.14.refs_0_.refs_1_, bf16[2,1024,1024]{2,1,0:T(8,128)(2,1)} %bitcast.173, bf16[2,1024,1024]{2,1,0:T(8,128)(2,1)} %bitcast.174, bf16[2,1024,1024]{2,1,0:T(8,128)(2,1)} %bitcast.181, ...), custom_call_target="tpu_custom_call" | custom-call | flops 7516192768 | bytes 21233664 | tf_op jit(solution)/shard_map/pallas_call | solution.py:502
  335.8 13.8 %shard_map.196 = (bf16[896,2048]{1,0:T(8,128)(2,1)S(1)}, bf16[896,2048]{1,0:T(8,128)(2,1)}, f32[896,1024]{1,0:T(8,128)}) custom-call(bf16[896,1024]{1,0:T(8,128)(2,1)} %get-tuple-element.111.x_ref.refs_0_, f32[896,1024]{1,0:T(8,128)} %get-tuple-element.112.base_ref, bf16[2,1024,1024]{2,1,0:T(8,128)(2,1)} %bitcast.175, bf16[2,1024,1024]{2,1,0:T(8,128)(2,1)} %bitcast.176, ...), custom_call_target="tpu_custom_call" | custom-call | flops 7516192768 | bytes 21233664 | tf_op jit(solution)/shard_map/pallas_call | solution.py:502
  358.5 14.1 %shard_map.197 = (bf16[896,2048]{1,0:T(8,128)(2,1)S(1)}, f32[896,1024]{1,0:T(8,128)}) custom-call(bf16[896,1024]{1,0:T(8,128)(2,1)S(1)} %get-tuple-element.129.g_ref.refs_2_, bf16[896,2048]{1,0:T(8,128)(2,1)} %get-tuple-element.68.slope_ref, f32[896,1024]{1,0:T(8,128)} %get-tuple-element.130.base_ref, bf16[2,1024,1024]{2,1,0:T(8,128)(2,1)} %bitcast.177, ...), custom_call_target="tpu_custom_call" | custom-call | flops 7516192768 | bytes 21233664 | tf_op jit(solution)/shard_map/pallas_call | solution.py:570
  372.6 14.0 %shard_map.199 = (bf16[896,2048]{1,0:T(8,128)(2,1)}, bf16[896,1024]{1,0:T(8,128)(2,1)S(1)}) custom-call(bf16[896,1024]{1,0:T(8,128)(2,1)S(1)} %collective-permute-done.13.refs_0_.refs_3_, bf16[896,2048]{1,0:T(8,128)(2,1)} %get-tuple-element.70.refs_1_, bf16[2,1024,1024]{2,1,0:T(8,128)(2,1)} %bitcast.179, bf16[2,1024,1024]{2,1,0:T(8,128)(2,1)} %bitcast.180, ...), custom_call_target="tpu_custom_call" | custom-call | flops 7516192768 | bytes 21233664 | tf_op jit(solution)/shard_map/pallas_call | solution.py:570
  387.9 15.1 %shard_map.202 = bf16[2,1024,1024]{2,1,0:T(8,128)(2,1)} custom-call(bf16[896,1024]{1,0:T(8,128)(2,1)} %get-tuple-element.111.x_ref.refs_0_, bf16[896,1024]{1,0:T(8,128)(2,1)} %collective-permute-done.14.refs_0_.refs_1_, bf16[896,2048]{1,0:T(8,128)(2,1)} %copy-done.24, bf16[896,2048]{1,0:T(8,128)(2,1)} %get-tuple-element.79.refs_3_), custom_call_target="tpu_custom_call" | custom-call | flops 7516192768 | bytes 18874368 | tf_op jit(solution)/shard_map/pallas_call | solution.py:612
  415.8 14.5 %shard_map.201 = (bf16[896,2048]{1,0:T(8,128)(2,1)}, bf16[896,1024]{1,0:T(8,128)(2,1)}) custom-call(bf16[896,1024]{1,0:T(8,128)(2,1)S(1)} %collective-permute-done.16.refs_0_.refs_3_, bf16[896,2048]{1,0:T(8,128)(2,1)} %get-tuple-element.74.refs_1_, bf16[2,1024,1024]{2,1,0:T(8,128)(2,1)} %bitcast.161, bf16[2,1024,1024]{2,1,0:T(8,128)(2,1)} %bitcast.162, ...), custom_call_target="tpu_custom_call" | custom-call | flops 7516192768 | bytes 21233664 | tf_op jit(solution)/shard_map/pallas_call | solution.py:570
  444.9 13.8 %shard_map.200 = (bf16[896,2048]{1,0:T(8,128)(2,1)S(1)}, f32[896,1024]{1,0:T(8,128)}) custom-call(bf16[896,1024]{1,0:T(8,128)(2,1)S(1)} %copy-done.9, bf16[896,2048]{1,0:T(8,128)(2,1)} %get-tuple-element.72.slope_ref, f32[896,1024]{1,0:T(8,128)} %get-tuple-element.110.base_ref, bf16[2,1024,1024]{2,1,0:T(8,128)(2,1)} %bitcast.163, ...), custom_call_target="tpu_custom_call" | custom-call | flops 7516192768 | bytes 21233664 | tf_op jit(solution)/shard_map/pallas_call | solution.py:570
  469.0 15.1 %shard_map.204 = bf16[2,1024,1024]{2,1,0:T(8,128)(2,1)} custom-call(bf16[896,1024]{1,0:T(8,128)(2,1)S(1)} %bitcast.116, bf16[896,1024]{1,0:T(8,128)(2,1)} %collective-permute-done.9.refs_0_.refs_1_, bf16[896,2048]{1,0:T(8,128)(2,1)} %copy-done.23, bf16[896,2048]{1,0:T(8,128)(2,1)} %get-tuple-element.83.refs_3_), custom_call_target="tpu_custom_call" | custom-call | flops 7516192768 | bytes 18874368 | tf_op jit(solution)/shard_map/pallas_call | solution.py:612
  518.6 34.9 %collective-permute-done.20.refs_2_ = bf16[896,1024]{1,0:T(8,128)(2,1)} collective-permute-done((bf16[896,1024]{1,0:T(8,128)(2,1)}, bf16[896,1024]{1,0:T(8,128)(2,1)}, u32[]{:S(2)}, u32[]{:S(2)}) %collective-permute-start.20) | collective-permute-done | bytes 1835040 | tf_op jit(solution)/shard_map/ppermute | solution.py:637
  569.5 27.8 %collective-permute-done.21.refs_3_ = bf16[896,1024]{1,0:T(8,128)(2,1)} collective-permute-done((bf16[896,1024]{1,0:T(8,128)(2,1)}, bf16[896,1024]{1,0:T(8,128)(2,1)}, u32[]{:S(2)}, u32[]{:S(2)}) %collective-permute-start.21) | collective-permute-done | bytes 1835040 | tf_op jit(solution)/shard_map/ppermute | solution.py:637
  602.3 34.6 %shard_map.206 = (bf16[3072,1024]{1,0:T(8,128)(2,1)}, bf16[3072,256]{1,0:T(8,128)(2,1)S(1)}) custom-call(s32[4]{0:T(128)S(1)} %pad_add_fusion.first_ref, s32[3072,1]{1,0:T(8,128)S(1)} %fusion.19.place_ref, bf16[3072,1024]{1,0:T(8,128)(2,1)} %base_ref.1, bf16[896,1024]{1,0:T(8,128)(2,1)} %bitcast.42.refs_0_, ...), custom_call_target="tpu_custom_call" | custom-call | flops 24159191040 | bytes 19922944 | tf_op jit(solution)/shard_map/pallas_call | solution.py:427
  642.5 26.9 %shard_map.207 = bf16[3072,768]{1,0:T(8,128)(2,1)} custom-call(s32[3]{0:T(128)S(1)} %copy-done.16, bf16[3072,768]{1,0:T(8,128)(2,1)} %copy-done, bf16[3072,768]{1,0:T(8,128)(2,1)} %copy-done, bf16[3072,768]{1,0:T(8,128)(2,1)} %copy-done, bf16[3072,256]{1,0:T(8,128)(2,1)S(1)} %copy-done.3, bf16[3072,256]{1,0:T(8,128)(2,1)S(1)} %get-tuple-element.87.do_ref, ...), custom_call_target="tpu_custom_call" | custom-call | flops 8053063680 | bytes 12582912 | tf_op jit(solution)/shard_map/pallas_call | solution.py:226
  709.1 14.3 %collective-permute-done.28 = bf16[768,512]{1,0:T(8,128)(2,1)} collective-permute-done((bf16[768,512]{1,0:T(8,128)(2,1)}, bf16[768,512]{1,0:T(8,128)(2,1)}, u32[]{:S(2)}, u32[]{:S(2)}) %collective-permute-start.28) | collective-permute-done | bytes 786464 | tf_op jit(solution)/shard_map/ppermute | solution.py:637
  742.1 14.7 %collective-permute-done.27 = bf16[768,512]{1,0:T(8,128)(2,1)} collective-permute-done((bf16[768,512]{1,0:T(8,128)(2,1)}, bf16[768,512]{1,0:T(8,128)(2,1)}, u32[]{:S(2)}, u32[]{:S(2)}) %collective-permute-start.27) | collective-permute-done | bytes 786464 | tf_op jit(solution)/shard_map/ppermute | solution.py:637
  774.8 39.7 %collective-permute-done.39 = f32[2,1024]{1,0:T(2,128)S(1)} collective-permute-done((f32[2,1024]{1,0:T(2,128)S(1)}, f32[2,1024]{1,0:T(2,128)S(1)}, u32[]{:S(2)}, u32[]{:S(2)}) %collective-permute-start.39) | collective-permute-done | bytes 8224 | tf_op jit(solution)/shard_map/ppermute | solution.py:637
  831.2 55.7 %reduce-scatter.11.cloned.1.call-done = bf16[1,1024,1024]{2,1,0:T(8,128)(2,1)} async-done(((bf16[2,1024,1024]{2,1,0:T(8,128)(2,1)}), bf16[1,1024,1024]{2,1,0:T(8,128)(2,1)}) %reduce-scatter.11.cloned.1.call-update) | async-done | bytes 2097168 | tf_op jit(solution)/shard_map/reduce_scatter | solution.py:694
  889.3 32.3 %shard_map.208 = bf16[3072,1024]{1,0:T(8,128)(2,1)} custom-call(s32[4]{0:T(128)S(1)} %pad_add_fusion.first_ref, s32[3072,1]{1,0:T(8,128)S(1)} %fusion.19.place_ref, bf16[3072,1024]{1,0:T(8,128)(2,1)} %shard_map.191.rows_ref.base_ref, bf16[896,1024]{1,0:T(8,128)(2,1)} %bitcast.46.refs_0_, bf16[896,1024]{1,0:T(8,128)(2,1)} %collective-permute-done.24.refs_1_, ...), custom_call_target="tpu_custom_call" | custom-call | flops 22548578304 | bytes 19922944 | tf_op jit(solution)/shard_map/pallas_call | solution.py:427
  943.3 23.9 %collective-permute-done.38 = bf16[384,1024]{1,0:T(8,128)(2,1)S(1)} collective-permute-done((bf16[384,1024]{1,0:T(8,128)(2,1)S(1)}, bf16[384,1024]{1,0:T(8,128)(2,1)S(1)}, u32[]{:S(2)}, u32[]{:S(2)}) %collective-permute-start.38) | collective-permute-done | bytes 786464 | tf_op jit(solution)/shard_map/ppermute | solution.py:637
  (300 shorter events, 384.3 us)
Async XLA Ops:
  7.2 235.3 %all-gather.9.cloned.1.call-start = ((), (), s32[]{:S(2)}) async-start(), calls=%async_computation.12 | async-start | bytes 6291456 | tf_op jit(solution)/shard_map/all_gather | solution.py:683
  39.3 203.2 %all-gather.11.cloned.1.call-start = ((), (), s32[]{:S(2)}) async-start(), calls=%async_computation.13 | async-start | bytes 6291456 | tf_op jit(solution)/shard_map/all_gather | solution.py:683
  70.6 103.2 %collective-permute-start = (bf16[3072,256]{1,0:T(8,128)(2,1)S(1)}, bf16[3072,256]{1,0:T(8,128)(2,1)}, u32[]{:S(2)}, u32[]{:S(2)}) collective-permute-start(bf16[3072,256]{1,0:T(8,128)(2,1)S(1)} %get-tuple-element.61.refs_0_.o_ref), channel_id=1, source_target_pairs={{0,1},{1,0},{2,3},{3,2},{4,5},{5,4},{6,7},{7,6},{8,9},{9,8},{10,11... | collective-permute-start | bytes 4718600 | tf_op jit(solution)/shard_map/ppermute | solution.py:637
  72.7 74.7 %collective-permute-start.3 = (bf16[256,1024]{1,0:T(8,128)(2,1)S(1)}, bf16[256,1024]{1,0:T(8,128)(2,1)S(1)}, u32[]{:S(2)}, u32[]{:S(2)}) collective-permute-start(bf16[256,1024]{1,0:T(8,128)(2,1)S(1)} %bitcast.119), channel_id=1, source_target_pairs={{0,1},{1,0},{2,3},{3,2},{4,5},{5,4},{6,7},{7,6},{8,9},{9,8},{10,11... | collective-permute-start | bytes 1572872 | tf_op jit(solution)/shard_map/ppermute | solution.py:637
  72.8 76.7 %collective-permute-start.4 = (bf16[256,1024]{1,0:T(8,128)(2,1)S(1)}, bf16[256,1024]{1,0:T(8,128)(2,1)S(1)}, u32[]{:S(2)}, u32[]{:S(2)}) collective-permute-start(bf16[256,1024]{1,0:T(8,128)(2,1)S(1)} %bitcast.120), channel_id=1, source_target_pairs={{0,2},{1,3},{2,0},{3,1},{4,6},{5,7},{6,4},{7,5},{8,10},{9,11},{10,... | collective-permute-start | bytes 1572872 | tf_op jit(solution)/shard_map/ppermute | solution.py:637
  74.1 127.7 %collective-permute-start.11 = (bf16[1024,1024]{1,0:T(8,128)(2,1)}, bf16[1024,1024]{1,0:T(8,128)(2,1)}, u32[]{:S(2)}, u32[]{:S(2)}) collective-permute-start(bf16[1024,1024]{1,0:T(8,128)(2,1)} %get-tuple-element.127), channel_id=1, source_target_pairs={{0,4},{1,0},{2,6},{3,2},{4,5},{5,1},{6,7},{7,3},{8,12},{9,8},{10,1... | collective-permute-start | bytes 6291464 | tf_op jit(solution)/shard_map/ppermute | solution.py:678
  201.8 93.3 %all-gather.13.cloned.1.call-start = ((), (), s32[]{:S(2)}) async-start(), calls=%async_computation.14 | async-start | bytes 6291456 | tf_op jit(solution)/shard_map/all_gather | solution.py:683
  202.5 116.2 %all-gather.15.cloned.1.call-start = ((), (), s32[]{:S(2)}) async-start(), calls=%async_computation.15 | async-start | bytes 6291456 | tf_op jit(solution)/shard_map/all_gather | solution.py:683
  294.9 305.6 %reduce-scatter.5.cloned.1.call-start = ((), (), s32[]{:S(2)}) async-start(), calls=%async_computation.8 | async-start | bytes 6291456 | tf_op jit(solution)/shard_map/reduce_scatter | solution.py:694
  403.0 198.1 %reduce-scatter.7.cloned.1.call-start = ((), (), s32[]{:S(2)}) async-start(), calls=%async_computation.9 | async-start | bytes 6291456 | tf_op jit(solution)/shard_map/reduce_scatter | solution.py:694
  516.8 309.5 %all-reduce.3.cloned.1.call-start = ((), (), s32[]{:S(2)}) async-start(), calls=%async_computation.16 | async-start | bytes 4194304 | tf_op jit(solution)/shard_map/psum | solution.py:956
  597.3 72.1 %collective-permute-start.24 = (bf16[896,1024]{1,0:T(8,128)(2,1)}, bf16[896,1024]{1,0:T(8,128)(2,1)}, u32[]{:S(2)}, u32[]{:S(2)}) collective-permute-start(bf16[896,1024]{1,0:T(8,128)(2,1)} %bitcast.46.refs_0_), channel_id=1, source_target_pairs={{0,1},{1,0},{2,3},{3,2},{4,5},{5,4},{6,7},{7,6},{8,9},{9,8},{10,11... | collective-permute-start | bytes 5505032 | tf_op jit(solution)/shard_map/ppermute | solution.py:637
  599.1 70.3 %collective-permute-start.25 = (bf16[896,1024]{1,0:T(8,128)(2,1)}, bf16[896,1024]{1,0:T(8,128)(2,1)}, u32[]{:S(2)}, u32[]{:S(2)}) collective-permute-start(bf16[896,1024]{1,0:T(8,128)(2,1)} %bitcast.46.refs_0_), channel_id=1, source_target_pairs={{0,2},{1,3},{2,0},{3,1},{4,6},{5,7},{6,4},{7,5},{8,10},{9,11},{10,... | collective-permute-start | bytes 5505032 | tf_op jit(solution)/shard_map/ppermute | solution.py:637
  600.5 69.0 %collective-permute-start.22 = (bf16[1024,1024]{1,0:T(8,128)(2,1)}, bf16[1024,1024]{1,0:T(8,128)(2,1)}, u32[]{:S(2)}, u32[]{:S(2)}) collective-permute-start(bf16[1024,1024]{1,0:T(8,128)(2,1)} %bitcast.191), channel_id=1, source_target_pairs={{4,0},{0,1},{6,2},{2,3},{5,4},{1,5},{7,6},{3,7},{12,8},{8,9},{14,1... | collective-permute-start | bytes 6291464 | tf_op jit(solution)/shard_map/ppermute | solution.py:701
  601.1 80.6 %collective-permute-start.23 = (bf16[1024,1024]{1,0:T(8,128)(2,1)}, bf16[1024,1024]{1,0:T(8,128)(2,1)}, u32[]{:S(2)}, u32[]{:S(2)}) collective-permute-start(bf16[1024,1024]{1,0:T(8,128)(2,1)} %bitcast.192), channel_id=1, source_target_pairs={{4,0},{0,1},{6,2},{2,3},{5,4},{1,5},{7,6},{3,7},{12,8},{8,9},{14,1... | collective-permute-start | bytes 6291464 | tf_op jit(solution)/shard_map/ppermute | solution.py:701
  690.2 141.0 %reduce-scatter.9.cloned.1.call-start = ((), (), s32[]{:S(2)}) async-start(), calls=%async_computation.10 | async-start | bytes 6291456 | tf_op jit(solution)/shard_map/reduce_scatter | solution.py:694
  690.9 196.0 %reduce-scatter.11.cloned.1.call-start = ((), (), s32[]{:S(2)}) async-start(), calls=%async_computation.11 | async-start | bytes 6291456 | tf_op jit(solution)/shard_map/reduce_scatter | solution.py:694
  734.1 152.9 %collective-permute-start.30 = (bf16[896,1024]{1,0:T(8,128)(2,1)}, bf16[896,1024]{1,0:T(8,128)(2,1)}, u32[]{:S(2)}, u32[]{:S(2)}) collective-permute-start(bf16[896,1024]{1,0:T(8,128)(2,1)} %collective-permute-done.25.refs_2_), channel_id=1, source_target_pairs={{0,1},{1,0},{2,3},{3,2},{4,5},{5,4},{6,7},{7,6},{8,9},{9,8},{10,11... | collective-permute-start | bytes 5505032 | tf_op jit(solution)/shard_map/ppermute | solution.py:637
  772.6 116.7 %collective-permute-start.33 = (bf16[384,1024]{1,0:T(8,128)(2,1)}, bf16[384,1024]{1,0:T(8,128)(2,1)}, u32[]{:S(2)}, u32[]{:S(2)}) collective-permute-start(bf16[384,1024]{1,0:T(8,128)(2,1)} %get-tuple-element.132), channel_id=1, source_target_pairs={{0,1},{1,0},{2,3},{3,2},{4,5},{5,4},{6,7},{7,6},{8,9},{9,8},{10,11... | collective-permute-start | bytes 2359304 | tf_op jit(solution)/shard_map/ppermute | solution.py:637
  822.3 66.1 %collective-permute-start.46 = (f32[2,1024]{1,0:T(2,128)S(1)}, f32[2,1024]{1,0:T(2,128)S(1)}, u32[]{:S(2)}, u32[]{:S(2)}) collective-permute-start(f32[2,1024]{1,0:T(2,128)S(1)} %add.387), channel_id=1, source_target_pairs={{0,4},{4,0},{8,12},{12,8},{16,20},{20,16},{24,28},{28,24},{1,5},{5... | collective-permute-start | bytes 24584 | tf_op jit(solution)/shard_map/ppermute | solution.py:634
  824.1 64.8 %collective-permute-start.43 = (f32[2,1024]{1,0:T(2,128)S(1)}, f32[2,1024]{1,0:T(2,128)S(1)}, u32[]{:S(2)}, u32[]{:S(2)}) collective-permute-start(f32[2,1024]{1,0:T(2,128)S(1)} %add.384), channel_id=1, source_target_pairs={{0,16},{4,20},{8,24},{12,28},{16,0},{20,4},{24,8},{28,12},{1,17},{... | collective-permute-start | bytes 24584 | tf_op jit(solution)/shard_map/ppermute | solution.py:651
  830.9 97.0 %collective-permute-start.35 = (bf16[384,1024]{1,0:T(8,128)(2,1)}, bf16[384,1024]{1,0:T(8,128)(2,1)}, u32[]{:S(2)}, u32[]{:S(2)}) collective-permute-start(bf16[384,1024]{1,0:T(8,128)(2,1)} %get-tuple-element.132), channel_id=1, source_target_pairs={{0,2},{1,3},{2,0},{3,1},{4,6},{5,7},{6,4},{7,5},{8,10},{9,11},{10,... | collective-permute-start | bytes 2359304 | tf_op jit(solution)/shard_map/ppermute | solution.py:637
  889.0 79.2 %collective-permute-start.47 = (bf16[1024,1024]{1,0:T(8,128)(2,1)}, bf16[1024,1024]{1,0:T(8,128)(2,1)S(1)}, u32[]{:S(2)}, u32[]{:S(2)}) collective-permute-start(bf16[1024,1024]{1,0:T(8,128)(2,1)} %bitcast.189), channel_id=1, source_target_pairs={{4,0},{0,1},{6,2},{2,3},{5,4},{1,5},{7,6},{3,7},{12,8},{8,9},{14,1... | collective-permute-start | bytes 6291464 | tf_op jit(solution)/shard_map/ppermute | solution.py:701
  889.3 84.4 %collective-permute-start.48 = (bf16[1024,1024]{1,0:T(8,128)(2,1)}, bf16[1024,1024]{1,0:T(8,128)(2,1)S(1)}, u32[]{:S(2)}, u32[]{:S(2)}) collective-permute-start(bf16[1024,1024]{1,0:T(8,128)(2,1)} %bitcast.190), channel_id=1, source_target_pairs={{4,0},{0,1},{6,2},{2,3},{5,4},{1,5},{7,6},{3,7},{12,8},{8,9},{14,1... | collective-permute-start | bytes 6291464 | tf_op jit(solution)/shard_map/ppermute | solution.py:701
  (82 other events, 1639.5 us)
Sparse Core Ops, SparseCore 0:
  39.4 82.9 all-gather.8
  124.0 74.1 all-gather.10
  204.2 56.3 all-gather.12
  261.9 56.7 all-gather.14
  403.1 54.3 reduce-scatter.4
  459.7 54.3 reduce-scatter.6
  690.3 67.1 all-reduce.2
  759.7 53.5 reduce-scatter.8
  815.7 71.1 reduce-scatter.10

commit v6 on v5

--- a/solution.py
+++ b/solution.py
@@ -17,6 +17,10 @@
 
 def after(value, *others):
     return lax.optimization_barrier((value, *others))[0]
+
+
+def together(*values):
+    return lax.optimization_barrier(values)
 
 
 def dot(a, b, contract):
@@ -643,8 +647,7 @@
             step *= 2
         return value
 
-    def sum_all(self, value):
-        value = self.sum_tensor(value)
+    def sum_dp(self, value):
         step = 1
         while step < self.experts:
             pairs = [(d, d ^ step) for d in range(self.experts)]
@@ -742,7 +745,7 @@
 
 def gather_rows(grid, value):
     if grid.size != 4:
-        return lax.all_gather(value, "tensor", axis=0, tiled=True)
+        return lax.all_gather(value, "tensor", axis=0, tiled=True), [], []
     rows, width = value.shape
     half = rows // 2
     first, second = value[:half], value[half:]
@@ -759,14 +762,14 @@
         place = jnp.bitwise_xor(me, other) * rows
         out = lax.dynamic_update_slice(out, top, (place, 0))
         out = lax.dynamic_update_slice(out, bottom, (place + half, 0))
-    return out
-
-
-def scatter_rows(grid, term):
+    return out, [first_x, second_y], [first_xy, second_xy]
+
+
+def scatter_rows(grid, term, beside):
     size, rows, width = term.shape
     if size != 4:
         total = lax.psum_scatter(term.astype(BF16), "tensor", scatter_dimension=0, tiled=False)
-        return total.astype(F32), []
+        return total.astype(F32), [], beside
     me = lax.axis_index("tensor")
     half = width // 2
 
@@ -774,15 +777,17 @@
         place = jnp.bitwise_xor(me, other)
         return lax.dynamic_slice(term, (place, 0, low), (1, rows, half))[0]
 
+    halves = ((0, 1, 2), (half, 2, 1))
+    got_far = [grid.over_tensor(pick(3, low).astype(BF16), near) for low, near, far in halves]
+    got_own = [grid.over_tensor(pick(near, low).astype(BF16), near) for low, near, far in halves]
+    first, second, *beside = together(*got_far, *beside)
     totals, arrived = [], []
-    for low, near, far in ((0, 1, 2), (half, 2, 1)):
-        got_far = grid.over_tensor(pick(3, low).astype(BF16), near)
-        got_own = grid.over_tensor(pick(near, low).astype(BF16), near)
-        onward = pick(far, low).astype(F32) + got_far.astype(F32)
+    for (low, near, far), far_term, own_term in zip(halves, (first, second), got_own):
+        onward = pick(far, low).astype(F32) + far_term.astype(F32)
         got = grid.over_tensor(onward.astype(BF16), far)
         arrived.append(got)
-        totals.append(pick(0, low).astype(F32) + got_own.astype(F32) + got.astype(F32))
-    return jnp.concatenate(totals, axis=1), arrived
+        totals.append(pick(0, low).astype(F32) + own_term.astype(F32) + got.astype(F32))
+    return jnp.concatenate(totals, axis=1), arrived, beside
 
 
 def body(
@@ -887,51 +892,63 @@
         slopes = saved[k][2]
         here = grad_current.astype(BF16)
         there = grid.over_core(here)
+        grad_pre_there, part = expert_backward(there, slopes[1], win[k], wout[k])
         grad_pre, total = expert_backward(here, slopes[0], win[k], wout[k], grad_current)
-        grad_pre_there, part = expert_backward(there, slopes[1], win[k], wout[k])
         grad_current = total + grid.over_core(part).astype(F32)
         branches[k] = ([here, there], [grad_pre, grad_pre_there])
     grad_rows = (grad_current + grad_logit * centroid.astype(F32)[None, :]).astype(BF16)
     centroid_part = jnp.sum(grad_logit * expert_rows.astype(F32), axis=0, keepdims=True)
-    centroid_parts = jnp.concatenate(
-        [jnp.where(parity == p, centroid_part, 0.0) for p in range(2)], axis=0
-    )
+    centroid_parts = grid.sum_tensor(
+        jnp.concatenate([jnp.where(parity == p, centroid_part, 0.0) for p in range(2)], axis=0)
+    )
+    centroid_other = grid.over_core(centroid_parts)
+    grad_centroid = lax.dynamic_slice_in_dim(centroid_parts + centroid_other, core, 1, 0)
 
     moved = leave_experts(grad_rows)
-    outers, sums = [], []
+    outers = []
     for k in (1, 0):
         rows_in, acts, unused = saved[k]
         branch, grad_pres = branches[k]
         blocks = win[k].shape[0]
         outers += [outer(rows_in, grad_pres, blocks), outer(acts, branch, blocks)]
-    sums_in2, sums_back2, sums_in1, sums_back1 = [sum_hidden(grid, pieces) for pieces in outers]
-    moved = after(moved, *outers)
+    sums_in2, sums_back2 = [sum_hidden(grid, pieces) for pieces in outers[:2]]
+    moved = after(moved, *outers, centroid_other)
     grad_gather = Gather(grid, moved.reshape(own_rows, model_width))
+    sums_in1, sums_back1 = [
+        sum_hidden(grid, after(pieces, *grad_gather.ready())) for pieces in outers[2:]
+    ]
     pieces = grad_gather.finish()
     first = row_starts(grad_gather)
     out_padded = jnp.pad(out_flat, ((0, heads * head_size - inner), (0, 0)))
     grad_mixed, grad_attended = combine(pieces, first, place, cotangent, out_padded)
-    out_gather = Gather(grid, after(returned, *pieces[1:]).reshape(own_rows, model_width))
-    out_first = row_starts(out_gather)
     back_in2 = return_hidden(grid, after(sums_in2, *pieces[1:]))
     back_out2 = return_hidden(grid, after(sums_back2, *pieces[1:]))
+    out_gather = Gather(grid, after(returned, *pieces[1:]).reshape(own_rows, model_width))
     grad_projected = attend_back(
-        projected, attended, grad_attended, log_total, lengths, seq_count, heads, head_size
-    )
-    grad_projected = after(grad_projected, back_in2, back_out2, *out_gather.ready())
-    out_pieces = out_gather.finish()
+        projected,
+        attended,
+        grad_attended,
+        log_total,
+        lengths,
+        seq_count,
+        heads,
+        head_size,
+    )
+    grad_ln_part = dot(grad_projected, fused, ((1,), (1,))).astype(BF16)
+    grad_ln_part, grad_mixed, grad_projected = together(
+        grad_ln_part, grad_mixed, grad_projected, back_in2, back_out2, sums_in1, sums_back1, *out_gather.ready()
+    )[:3]
     grad_out_local = dot(attended[:, :inner], grad_mixed, ((0,), (0,))).reshape(
         heads_here, head_size, model_width
     )
     grad_qkv_local = dot(ln_in, grad_projected, ((0,), (0,)))
-    grad_ln_part = dot(grad_projected, fused, ((1,), (1,))).astype(BF16)
-    grad_ln, scattered = scatter_rows(grid, grad_ln_part.reshape(shards, tok_rows, model_width))
+    grad_sums = (grad_qkv_local.astype(BF16), grad_out_local.astype(BF16))
+    grad_ln, scattered, grad_sums = scatter_rows(
+        grid, grad_ln_part.reshape(shards, tok_rows, model_width), grad_sums
+    )
+    grad_sums = lax.psum(grad_sums, "dp")
     scattered = scattered + [grad_projected]
-    back_in1 = return_hidden(grid, after(sums_in1, *scattered))
-    back_out1 = return_hidden(grid, after(sums_back1, *scattered))
-    centroid_parts = grid.sum_tensor(after(centroid_parts, *scattered))
-    centroid_parts = centroid_parts + grid.over_core(centroid_parts)
-    grad_centroid = lax.dynamic_slice_in_dim(centroid_parts, core, 1, 0)
+    out_pieces = out_gather.finish(*scattered, over=2)
 
     def own(rows):
         return lax.dynamic_slice_in_dim(rows, me * tok_rows, tok_rows, 0)
@@ -946,16 +963,18 @@
     grad_input = own(grad_mixed).astype(F32) + own_scale * (
         grad_normed - mean_plain - own_normed * mean_cross
     )
-    grad_tokens = gather_rows(grid, grad_input.astype(BF16))
-    output = combine(out_pieces, out_first, place, after(sent, *scattered))[0]
+    grad_tokens, halfway, gathered = gather_rows(grid, grad_input.astype(BF16))
+    output = combine(out_pieces, first, place, after(sent, *scattered))[0]
     norm_total = jnp.stack([jnp.sum(grad_ln * own_normed, axis=0), jnp.sum(grad_ln, axis=0)])
-    norm_total = grid.sum_all(norm_total)
+    norm_total = grid.sum_tensor(after(norm_total, *halfway))
+    halfway = halfway + [norm_total]
+    back_in1 = return_hidden(grid, after(sums_in1, *halfway))
+    back_out1 = return_hidden(grid, after(sums_back1, *halfway))
+    norm_total = grid.sum_dp(norm_total)
     norm_total = lax.dynamic_slice_in_dim(
         norm_total, me * (model_width // shards), model_width // shards, 1
     )
-    grad_qkv, grad_out_weight = lax.psum(
-        (grad_qkv_local.astype(BF16), grad_out_local.astype(BF16)), "dp"
-    )
+    grad_qkv, grad_out_weight = [after(total, *gathered) for total in grad_sums]
     grad_qkv = grad_qkv.astype(F32).reshape(model_width, 3, heads, head_size)[:, :, :heads_here]
     grad_qkv_weight = jnp.swapaxes(grad_qkv, 1, 2).reshape(model_width, heads_here, 3 * head_size)
     return (

time: 991 us -> 924 us (0.932)
  waiting for transfers between devices: 420 us -> 353 us
    reduce_scatter x4, waiting for transfers between devices: 55.7 us -> 6.11 us  [sum_hidden(): lax.psum_scatter(pieces, 'tensor', scatter_dimension=0, axis_index_groups...]
    ppermute x28, waiting for transfers between devices: 250 us -> 219 us  [over_tensor(): lax.ppermute(value, 'tensor', [(t, t ^ other) for t in range(self.size)])]
    all_to_all x4, waiting for transfers between devices: 51.7 us -> 71.9 us  [exchange_depth(): lax.all_to_all(value, 'dp', split_axis=0, concat_axis=0, axis_index_group...]
    unnamed x89 -> x85, local copies, waits for them, and re-layouts: 26.4 us -> 20.4 us
  transfers between devices with their start and end apart: 62 -> 62, of which waited for: 27 -> 30; matrix products, arithmetic and copies ran while one was open for 11% -> 12% of each run, Pallas kernels for 31% -> 33%
where the time goes in v6:
time: 924 us; the launch traced here: 919 us
  waiting for transfers between devices  353 us (38%)
  Pallas kernels  335 us (36%)
  other arithmetic  68.5 us (7%)
  local copies, waits for them, and re-layouts  66.5 us (7%)
  starting transfers between devices  59 us (6%)
  matrix products  22.5 us (2%)
  between operations  14.8 us (2%)
    ppermute x28, waiting for transfers between devices, over_tensor(): lax.ppermute(value, 'tensor', [(t, t ^ other) for t in range(self.size)])  219 us
    all_to_all x4, waiting for transfers between devices, exchange_depth(): lax.all_to_all(value, 'dp', split_axis=0, concat_axis=0, axis_index_group...  71.9 us
    pallas_call x2, Pallas kernels, combine(): pl.pallas_call(functools.partial(kernel, count), grid_spec=pltpu.Prefetch...  66.4 us
    pallas_call x4, Pallas kernels, outer(): pl.pallas_call(functools.partial(outer_kernel, count), grid=(blocks, step...  56.6 us
    pallas_call x4, Pallas kernels, expert_backward(): pl.pallas_call(kernel, grid=(rows // tile,), in_specs=specs, out_specs=[r...  55.2 us
    pallas_call x4, Pallas kernels, expert_forward(): pl.pallas_call(kernel, grid=(rows // tile,), in_specs=specs, out_specs=[r...  53 us
    ppermute x28, starting transfers between devices, over_tensor(): lax.ppermute(value, 'tensor', [(t, t ^ other) for t in range(self.size)])  30.1 us
    pallas_call x1, Pallas kernels, attend_back(): pl.pallas_call(functools.partial(attend_back_kernel, head_size, group, ti...  26.9 us
  transfers between devices with their start and end apart: 62, of which 30 were waited for; matrix products, arithmetic and copies ran while one was open for 12% of the time, Pallas kernels for 33%

profile of v6, /device:TPU:0, one launch (start us, length us, event | category | flops | bytes accessed | tf_op | source)
XLA Modules:
  0.0 919.3 jit_solution(3827781468477269836)
XLA Ops:
  44.1 24.6 %shard_map.190 = (bf16[3072,256]{1,0:T(8,128)(2,1)S(1)}, f32[3,2,2,1024]{3,2,1,0:T(2,128)S(1)}) custom-call(s32[3]{0:T(128)S(1)} %copy-done.14, bf16[3072,768]{1,0:T(8,128)(2,1)S(1)} %copy-done.1, bf16[3072,768]{1,0:T(8,128)(2,1)S(1)} %copy-done.1, bf16[3072,768]{1,0:T(8,128)(2,1)S(1)} %copy-done.1), custom_call_target="tpu_custom_call" | custom-call | flops 3221225472 | bytes 6291456 | tf_op jit(solution)/shard_map/pallas_call | solution.py:121
  87.0 43.9 %collective-permute-done.1.refs_2_ = bf16[3072,256]{1,0:T(8,128)(2,1)} collective-permute-done((bf16[3072,256]{1,0:T(8,128)(2,1)S(1)}, bf16[3072,256]{1,0:T(8,128)(2,1)}, u32[]{:S(2)}, u32[]{:S(2)}) %collective-permute-start.1) | collective-permute-done | bytes 1572896 | tf_op jit(solution)/shard_map/ppermute | solution.py:641
  149.5 23.1 %collective-permute-done.5 = bf16[256,1024]{1,0:T(8,128)(2,1)} collective-permute-done((bf16[256,1024]{1,0:T(8,128)(2,1)S(1)}, bf16[256,1024]{1,0:T(8,128)(2,1)}, u32[]{:S(2)}, u32[]{:S(2)}) %collective-permute-start.5) | collective-permute-done | bytes 524320 | tf_op jit(solution)/shard_map/ppermute | solution.py:641
  203.2 39.7 %all-to-all-done = bf16[4,224,1024]{2,1,0:T(8,128)(2,1)S(1)} async-done(((bf16[4,224,1024]{2,1,0:T(8,128)(2,1)}), bf16[4,224,1024]{2,1,0:T(8,128)(2,1)S(1)}, u32[]{:S(2)}, u32[]{:S(2)}) %all-to-all-start) | async-done | bytes 1835040 | tf_op jit(solution)/shard_map/all_to_all | solution.py:660
  246.8 12.6 %shard_map.195 = (bf16[896,2048]{1,0:T(8,128)(2,1)}, bf16[896,2048]{1,0:T(8,128)(2,1)}, bf16[896,1024]{1,0:T(8,128)(2,1)S(1)}) custom-call(bf16[896,1024]{1,0:T(8,128)(2,1)} %collective-permute-done.9.refs_0_.refs_1_, bf16[2,1024,1024]{2,1,0:T(8,128)(2,1)} %bitcast.158, bf16[2,1024,1024]{2,1,0:T(8,128)(2,1)} %bitcast.159, bf16[2,1024,1024]{2,1,0:T(8,128)(2,1)} %bitcast.166, ...), custom_call_target="tpu_custom_call" | custom-call | flops 7516192768 | bytes 21233664 | tf_op jit(solution)/shard_map/pallas_call | solution.py:506
  261.9 13.7 %shard_map.194 = (bf16[896,2048]{1,0:T(8,128)(2,1)S(1)}, bf16[896,2048]{1,0:T(8,128)(2,1)}, f32[896,1024]{1,0:T(8,128)}) custom-call(bf16[896,1024]{1,0:T(8,128)(2,1)S(1)} %bitcast.114, f32[896,1024]{1,0:T(8,128)} %bitcast_convert_fusion.base_ref, bf16[2,1024,1024]{2,1,0:T(8,128)(2,1)} %bitcast.160, bf16[2,1024,1024]{2,1,0:T(8,128)(2,1)} %bitcast.161, ...), custom_call_target="tpu_custom_call" | custom-call | flops 7516192768 | bytes 21233664 | tf_op jit(solution)/shard_map/pallas_call | solution.py:506
  295.8 23.3 %all-gather.15.cloned.1.call-done = bf16[2048,1024]{1,0:T(8,128)(2,1)} async-done(((bf16[1024,1024]{1,0:T(8,128)(2,1)}), bf16[2048,1024]{1,0:T(8,128)(2,1)}) %all-gather.15.cloned.1.call-update) | async-done | bytes 4194320 | tf_op jit(solution)/shard_map/all_gather | solution.py:686
  319.1 13.0 %shard_map.198 = (bf16[896,2048]{1,0:T(8,128)(2,1)}, bf16[896,2048]{1,0:T(8,128)(2,1)}, bf16[896,1024]{1,0:T(8,128)(2,1)}) custom-call(bf16[896,1024]{1,0:T(8,128)(2,1)} %collective-permute-done.14.refs_0_.refs_1_, bf16[2,1024,1024]{2,1,0:T(8,128)(2,1)} %bitcast.174, bf16[2,1024,1024]{2,1,0:T(8,128)(2,1)} %bitcast.175, bf16[2,1024,1024]{2,1,0:T(8,128)(2,1)} %bitcast.182, ...), custom_call_target="tpu_custom_call" | custom-call | flops 7516192768 | bytes 21233664 | tf_op jit(solution)/shard_map/pallas_call | solution.py:506
  336.2 13.8 %shard_map.196 = (bf16[896,2048]{1,0:T(8,128)(2,1)S(1)}, bf16[896,2048]{1,0:T(8,128)(2,1)}, f32[896,1024]{1,0:T(8,128)}) custom-call(bf16[896,1024]{1,0:T(8,128)(2,1)} %get-tuple-element.133.x_ref.refs_0_, f32[896,1024]{1,0:T(8,128)} %get-tuple-element.134.base_ref, bf16[2,1024,1024]{2,1,0:T(8,128)(2,1)} %bitcast.176, bf16[2,1024,1024]{2,1,0:T(8,128)(2,1)} %bitcast.177, ...), custom_call_target="tpu_custom_call" | custom-call | flops 7516192768 | bytes 21233664 | tf_op jit(solution)/shard_map/pallas_call | solution.py:506
  358.8 14.0 %shard_map.197 = (bf16[896,2048]{1,0:T(8,128)(2,1)S(1)}, f32[896,1024]{1,0:T(8,128)}) custom-call(bf16[896,1024]{1,0:T(8,128)(2,1)S(1)} %get-tuple-element.151.g_ref.refs_2_, bf16[896,2048]{1,0:T(8,128)(2,1)} %get-tuple-element.79.slope_ref, f32[896,1024]{1,0:T(8,128)} %get-tuple-element.152.base_ref, bf16[2,1024,1024]{2,1,0:T(8,128)(2,1)} %bitcast.178, ...), custom_call_target="tpu_custom_call" | custom-call | flops 7516192768 | bytes 21233664 | tf_op jit(solution)/shard_map/pallas_call | solution.py:574
  372.8 14.0 %shard_map.199 = (bf16[896,2048]{1,0:T(8,128)(2,1)}, bf16[896,1024]{1,0:T(8,128)(2,1)S(1)}) custom-call(bf16[896,1024]{1,0:T(8,128)(2,1)S(1)} %collective-permute-done.13.refs_0_.refs_3_, bf16[896,2048]{1,0:T(8,128)(2,1)} %get-tuple-element.81.refs_1_, bf16[2,1024,1024]{2,1,0:T(8,128)(2,1)} %bitcast.180, bf16[2,1024,1024]{2,1,0:T(8,128)(2,1)} %bitcast.181, ...), custom_call_target="tpu_custom_call" | custom-call | flops 7516192768 | bytes 21233664 | tf_op jit(solution)/shard_map/pallas_call | solution.py:574
  388.1 15.1 %shard_map.202 = bf16[2,1024,1024]{2,1,0:T(8,128)(2,1)} custom-call(bf16[896,1024]{1,0:T(8,128)(2,1)} %get-tuple-element.133.x_ref.refs_0_, bf16[896,1024]{1,0:T(8,128)(2,1)} %collective-permute-done.14.refs_0_.refs_1_, bf16[896,2048]{1,0:T(8,128)(2,1)} %copy-done.21, bf16[896,2048]{1,0:T(8,128)(2,1)} %get-tuple-element.90.refs_3_), custom_call_target="tpu_custom_call" | custom-call | flops 7516192768 | bytes 18874368 | tf_op jit(solution)/shard_map/pallas_call | solution.py:616
  439.1 14.7 %shard_map.200 = (bf16[896,2048]{1,0:T(8,128)(2,1)S(1)}, f32[896,1024]{1,0:T(8,128)}) custom-call(bf16[896,1024]{1,0:T(8,128)(2,1)} %get-tuple-element.131.g_ref.refs_2_, bf16[896,2048]{1,0:T(8,128)(2,1)} %get-tuple-element.83.slope_ref, f32[896,1024]{1,0:T(8,128)} %get-tuple-element.132.base_ref, bf16[2,1024,1024]{2,1,0:T(8,128)(2,1)} %bitcast.164, ...), custom_call_target="tpu_custom_call" | custom-call | flops 7516192768 | bytes 21233664 | tf_op jit(solution)/shard_map/pallas_call | solution.py:574
  471.6 15.0 %shard_map.204 = bf16[2,1024,1024]{2,1,0:T(8,128)(2,1)} custom-call(bf16[896,1024]{1,0:T(8,128)(2,1)S(1)} %bitcast.116, bf16[896,1024]{1,0:T(8,128)(2,1)} %collective-permute-done.9.refs_0_.refs_1_, bf16[896,2048]{1,0:T(8,128)(2,1)} %copy-done.20, bf16[896,2048]{1,0:T(8,128)(2,1)} %get-tuple-element.94.refs_3_), custom_call_target="tpu_custom_call" | custom-call | flops 7516192768 | bytes 18874368 | tf_op jit(solution)/shard_map/pallas_call | solution.py:616
  486.6 13.9 %shard_map.205 = bf16[2,1024,1024]{2,1,0:T(8,128)(2,1)} custom-call(bf16[896,2048]{1,0:T(8,128)(2,1)} %copy-done.23, bf16[896,2048]{1,0:T(8,128)(2,1)} %get-tuple-element.96.refs_1_, bf16[896,1024]{1,0:T(8,128)(2,1)} %get-tuple-element.131.g_ref.refs_2_, bf16[896,1024]{1,0:T(8,128)(2,1)} %collective-permute-done.16.refs_0_.refs_3_), custom_call_target="tpu_custom_call" | custom-call | flops 7516192768 | bytes 18874368 | tf_op jit(solution)/shard_map/pallas_call | solution.py:616
  508.2 39.9 %collective-permute-done.22.refs_1_ = bf16[896,1024]{1,0:T(8,128)(2,1)S(1)} collective-permute-done((bf16[896,1024]{1,0:T(8,128)(2,1)}, bf16[896,1024]{1,0:T(8,128)(2,1)S(1)}, u32[]{:S(2)}, u32[]{:S(2)}) %collective-permute-start.22) | collective-permute-done | bytes 1835040 | tf_op jit(solution)/shard_map/ppermute | solution.py:641
  573.8 26.2 %all-to-all-done.3 = bf16[4,224,1024]{2,1,0:T(8,128)(2,1)S(1)} async-done(((bf16[4,224,1024]{2,1,0:T(8,128)(2,1)}), bf16[4,224,1024]{2,1,0:T(8,128)(2,1)S(1)}, u32[]{:S(2)}, u32[]{:S(2)}) %all-to-all-start.3) | async-done | bytes 1835040 | tf_op jit(solution)/shard_map/all_to_all | solution.py:660
  605.1 34.6 %shard_map.206 = (bf16[3072,1024]{1,0:T(8,128)(2,1)}, bf16[3072,256]{1,0:T(8,128)(2,1)S(1)}) custom-call(s32[4]{0:T(128)S(1)} %pad_add_fusion.first_ref, s32[3072,1]{1,0:T(8,128)S(1)} %copy-done.8, bf16[3072,1024]{1,0:T(8,128)(2,1)} %base_ref.1, bf16[896,1024]{1,0:T(8,128)(2,1)} %bitcast.44.refs_0_, bf16[896,1024]{1,0:T(8,128)(2,1)} %copy-done.37, ...), custom_call_target="tpu_custom_call" | custom-call | flops 24159191040 | bytes 19922944 | tf_op jit(solution)/shard_map/pallas_call | solution.py:431
  639.8 26.9 %shard_map.207 = bf16[3072,768]{1,0:T(8,128)(2,1)} custom-call(s32[3]{0:T(128)S(1)} %copy-done.15, bf16[3072,768]{1,0:T(8,128)(2,1)} %copy-done, bf16[3072,768]{1,0:T(8,128)(2,1)} %copy-done, bf16[3072,768]{1,0:T(8,128)(2,1)} %copy-done, bf16[3072,256]{1,0:T(8,128)(2,1)S(1)} %copy-done.3, bf16[3072,256]{1,0:T(8,128)(2,1)S(1)} %get-tuple-element.98.do_ref, ...), custom_call_target="tpu_custom_call" | custom-call | flops 8053063680 | bytes 12582912 | tf_op jit(solution)/shard_map/pallas_call | solution.py:230
  733.5 15.6 %collective-permute-done.31 = bf16[768,512]{1,0:T(8,128)(2,1)} collective-permute-done((bf16[768,512]{1,0:T(8,128)(2,1)S(1)}, bf16[768,512]{1,0:T(8,128)(2,1)}, u32[]{:S(2)}, u32[]{:S(2)}) %collective-permute-start.31) | collective-permute-done | bytes 786464 | tf_op jit(solution)/shard_map/ppermute | solution.py:641
  767.6 16.0 %collective-permute-done.36 = bf16[384,1024]{1,0:T(8,128)(2,1)S(1)} collective-permute-done((bf16[384,1024]{1,0:T(8,128)(2,1)}, bf16[384,1024]{1,0:T(8,128)(2,1)S(1)}, u32[]{:S(2)}, u32[]{:S(2)}) %collective-permute-start.36) | collective-permute-done | bytes 786464 | tf_op jit(solution)/shard_map/ppermute | solution.py:641
  785.7 12.9 %collective-permute-done.42 = f32[2,1024]{1,0:T(2,128)S(1)} collective-permute-done((f32[2,1024]{1,0:T(2,128)S(1)}, f32[2,1024]{1,0:T(2,128)S(1)}, u32[]{:S(2)}, u32[]{:S(2)}) %collective-permute-start.42) | collective-permute-done | bytes 8224 | tf_op jit(solution)/shard_map/ppermute | solution.py:641
  801.2 39.4 %collective-permute-done.43 = f32[2,1024]{1,0:T(2,128)S(1)} collective-permute-done((f32[2,1024]{1,0:T(2,128)S(1)}, f32[2,1024]{1,0:T(2,128)S(1)}, u32[]{:S(2)}, u32[]{:S(2)}) %collective-permute-start.43) | collective-permute-done | bytes 8224 | tf_op jit(solution)/shard_map/ppermute | solution.py:641
  868.4 31.8 %shard_map.208 = bf16[3072,1024]{1,0:T(8,128)(2,1)} custom-call(s32[4]{0:T(128)S(1)} %pad_add_fusion.first_ref, s32[3072,1]{1,0:T(8,128)S(1)} %copy-done.9, bf16[3072,1024]{1,0:T(8,128)(2,1)} %shard_map.191.rows_ref.base_ref, bf16[896,1024]{1,0:T(8,128)(2,1)S(1)} %bitcast.119, bf16[896,1024]{1,0:T(8,128)(2,1)} %collective-permute-done.27.refs_1_, ...), custom_call_target="tpu_custom_call" | custom-call | flops 22548578304 | bytes 19922944 | tf_op jit(solution)/shard_map/pallas_call | solution.py:431
  (296 shorter events, 366.9 us)
Async XLA Ops:
  7.2 235.7 %all-gather.9.cloned.1.call-start = ((), (), s32[]{:S(2)}) async-start(), calls=%async_computation.12 | async-start | bytes 6291456 | tf_op jit(solution)/shard_map/all_gather | solution.py:686
  39.3 203.6 %all-gather.11.cloned.1.call-start = ((), (), s32[]{:S(2)}) async-start(), calls=%async_computation.13 | async-start | bytes 6291456 | tf_op jit(solution)/shard_map/all_gather | solution.py:686
  68.7 62.1 %collective-permute-start.1 = (bf16[3072,256]{1,0:T(8,128)(2,1)S(1)}, bf16[3072,256]{1,0:T(8,128)(2,1)}, u32[]{:S(2)}, u32[]{:S(2)}) collective-permute-start(bf16[3072,256]{1,0:T(8,128)(2,1)S(1)} %get-tuple-element.72.refs_0_.o_ref), channel_id=1, source_target_pairs={{0,2},{1,3},{2,0},{3,1},{4,6},{5,7},{6,4},{7,5},{8,10},{9,11},{10,... | collective-permute-start | bytes 4718600 | tf_op jit(solution)/shard_map/ppermute | solution.py:641
  70.9 102.8 %collective-permute-start = (bf16[3072,256]{1,0:T(8,128)(2,1)S(1)}, bf16[3072,256]{1,0:T(8,128)(2,1)}, u32[]{:S(2)}, u32[]{:S(2)}) collective-permute-start(bf16[3072,256]{1,0:T(8,128)(2,1)S(1)} %get-tuple-element.72.refs_0_.o_ref), channel_id=1, source_target_pairs={{0,1},{1,0},{2,3},{3,2},{4,5},{5,4},{6,7},{7,6},{8,9},{9,8},{10,11... | collective-permute-start | bytes 4718600 | tf_op jit(solution)/shard_map/ppermute | solution.py:641
  73.0 74.4 %collective-permute-start.3 = (bf16[256,1024]{1,0:T(8,128)(2,1)S(1)}, bf16[256,1024]{1,0:T(8,128)(2,1)S(1)}, u32[]{:S(2)}, u32[]{:S(2)}) collective-permute-start(bf16[256,1024]{1,0:T(8,128)(2,1)S(1)} %bitcast.122), channel_id=1, source_target_pairs={{0,1},{1,0},{2,3},{3,2},{4,5},{5,4},{6,7},{7,6},{8,9},{9,8},{10,11... | collective-permute-start | bytes 1572872 | tf_op jit(solution)/shard_map/ppermute | solution.py:641
  73.1 76.4 %collective-permute-start.4 = (bf16[256,1024]{1,0:T(8,128)(2,1)S(1)}, bf16[256,1024]{1,0:T(8,128)(2,1)S(1)}, u32[]{:S(2)}, u32[]{:S(2)}) collective-permute-start(bf16[256,1024]{1,0:T(8,128)(2,1)S(1)} %bitcast.123), channel_id=1, source_target_pairs={{0,2},{1,3},{2,0},{3,1},{4,6},{5,7},{6,4},{7,5},{8,10},{9,11},{10,... | collective-permute-start | bytes 1572872 | tf_op jit(solution)/shard_map/ppermute | solution.py:641
  74.4 127.8 %collective-permute-start.11 = (bf16[1024,1024]{1,0:T(8,128)(2,1)}, bf16[1024,1024]{1,0:T(8,128)(2,1)}, u32[]{:S(2)}, u32[]{:S(2)}) collective-permute-start(bf16[1024,1024]{1,0:T(8,128)(2,1)} %get-tuple-element.149), channel_id=1, source_target_pairs={{0,4},{1,0},{2,6},{3,2},{4,5},{5,1},{6,7},{7,3},{8,12},{9,8},{10,1... | collective-permute-start | bytes 6291464 | tf_op jit(solution)/shard_map/ppermute | solution.py:681
  202.2 93.6 %all-gather.13.cloned.1.call-start = ((), (), s32[]{:S(2)}) async-start(), calls=%async_computation.14 | async-start | bytes 6291456 | tf_op jit(solution)/shard_map/all_gather | solution.py:686
  202.9 116.2 %all-gather.15.cloned.1.call-start = ((), (), s32[]{:S(2)}) async-start(), calls=%async_computation.15 | async-start | bytes 6291456 | tf_op jit(solution)/shard_map/all_gather | solution.py:686
  290.9 60.9 %all-to-all-start.1 = ((bf16[4,224,1024]{2,1,0:T(8,128)(2,1)}), bf16[4,224,1024]{2,1,0:T(8,128)(2,1)}, u32[]{:S(2)}, u32[]{:S(2)}) async-start(bf16[4,224,1024]{2,1,0:T(8,128)(2,1)} %bitcast.120), calls=%async_computation.1 | async-start | bytes 3670016 | tf_op jit(solution)/shard_map/all_to_all | solution.py:660
  295.3 306.9 %reduce-scatter.5.cloned.1.call-start = ((), (), s32[]{:S(2)}) async-start(), calls=%async_computation.8 | async-start | bytes 6291456 | tf_op jit(solution)/shard_map/reduce_scatter | solution.py:697
  403.2 199.4 %reduce-scatter.7.cloned.1.call-start = ((), (), s32[]{:S(2)}) async-start(), calls=%async_computation.9 | async-start | bytes 6291456 | tf_op jit(solution)/shard_map/reduce_scatter | solution.py:697
  463.3 221.8 %reduce-scatter.9.cloned.1.call-start = ((), (), s32[]{:S(2)}) async-start(), calls=%async_computation.10 | async-start | bytes 6291456 | tf_op jit(solution)/shard_map/reduce_scatter | solution.py:697
  552.5 138.7 %reduce-scatter.11.cloned.1.call-start = ((), (), s32[]{:S(2)}) async-start(), calls=%async_computation.11 | async-start | bytes 6291456 | tf_op jit(solution)/shard_map/reduce_scatter | solution.py:697
  557.9 296.7 %all-reduce.3.cloned.1.call-start = ((), (), s32[]{:S(2)}) async-start(), calls=%async_computation.16 | async-start | bytes 4194304 | tf_op jit(solution)/shard_map/psum | solution.py:949
  600.0 76.3 %collective-permute-start.27 = (bf16[896,1024]{1,0:T(8,128)(2,1)S(1)}, bf16[896,1024]{1,0:T(8,128)(2,1)}, u32[]{:S(2)}, u32[]{:S(2)}) collective-permute-start(bf16[896,1024]{1,0:T(8,128)(2,1)S(1)} %bitcast.117), channel_id=1, source_target_pairs={{0,1},{1,0},{2,3},{3,2},{4,5},{5,4},{6,7},{7,6},{8,9},{9,8},{10,11... | collective-permute-start | bytes 5505032 | tf_op jit(solution)/shard_map/ppermute | solution.py:641
  601.6 74.8 %collective-permute-start.28 = (bf16[896,1024]{1,0:T(8,128)(2,1)S(1)}, bf16[896,1024]{1,0:T(8,128)(2,1)}, u32[]{:S(2)}, u32[]{:S(2)}) collective-permute-start(bf16[896,1024]{1,0:T(8,128)(2,1)S(1)} %bitcast.118), channel_id=1, source_target_pairs={{0,2},{1,3},{2,0},{3,1},{4,6},{5,7},{6,4},{7,5},{8,10},{9,11},{10,... | collective-permute-start | bytes 5505032 | tf_op jit(solution)/shard_map/ppermute | solution.py:641
  602.2 74.2 %collective-permute-start.25 = (bf16[1024,1024]{1,0:T(8,128)(2,1)}, bf16[1024,1024]{1,0:T(8,128)(2,1)}, u32[]{:S(2)}, u32[]{:S(2)}) collective-permute-start(bf16[1024,1024]{1,0:T(8,128)(2,1)} %bitcast.190), channel_id=1, source_target_pairs={{4,0},{0,1},{6,2},{2,3},{5,4},{1,5},{7,6},{3,7},{12,8},{8,9},{14,1... | collective-permute-start | bytes 6291464 | tf_op jit(solution)/shard_map/ppermute | solution.py:704
  602.5 82.5 %collective-permute-start.26 = (bf16[1024,1024]{1,0:T(8,128)(2,1)}, bf16[1024,1024]{1,0:T(8,128)(2,1)}, u32[]{:S(2)}, u32[]{:S(2)}) collective-permute-start(bf16[1024,1024]{1,0:T(8,128)(2,1)} %bitcast.191), channel_id=1, source_target_pairs={{4,0},{0,1},{6,2},{2,3},{5,4},{1,5},{7,6},{3,7},{12,8},{8,9},{14,1... | collective-permute-start | bytes 6291464 | tf_op jit(solution)/shard_map/ppermute | solution.py:704
  763.8 104.6 %collective-permute-start.33 = (bf16[896,1024]{1,0:T(8,128)(2,1)}, bf16[896,1024]{1,0:T(8,128)(2,1)}, u32[]{:S(2)}, u32[]{:S(2)}) collective-permute-start(bf16[896,1024]{1,0:T(8,128)(2,1)} %collective-permute-done.27.refs_1_), channel_id=1, source_target_pairs={{0,2},{1,3},{2,0},{3,1},{4,6},{5,7},{6,4},{7,5},{8,10},{9,11},{10,... | collective-permute-start | bytes 5505032 | tf_op jit(solution)/shard_map/ppermute | solution.py:641
  765.5 77.4 %collective-permute-start.37 = (bf16[384,1024]{1,0:T(8,128)(2,1)}, bf16[384,1024]{1,0:T(8,128)(2,1)}, u32[]{:S(2)}, u32[]{:S(2)}) collective-permute-start(bf16[384,1024]{1,0:T(8,128)(2,1)} %get-tuple-element.153), channel_id=1, source_target_pairs={{0,1},{1,0},{2,3},{3,2},{4,5},{5,4},{6,7},{7,6},{8,9},{9,8},{10,11... | collective-permute-start | bytes 2359304 | tf_op jit(solution)/shard_map/ppermute | solution.py:641
  767.0 79.7 %collective-permute-start.38 = (bf16[384,1024]{1,0:T(8,128)(2,1)}, bf16[384,1024]{1,0:T(8,128)(2,1)}, u32[]{:S(2)}, u32[]{:S(2)}) collective-permute-start(bf16[384,1024]{1,0:T(8,128)(2,1)} %get-tuple-element.154), channel_id=1, source_target_pairs={{0,2},{1,3},{2,0},{3,1},{4,6},{5,7},{6,4},{7,5},{8,10},{9,11},{10,... | collective-permute-start | bytes 2359304 | tf_op jit(solution)/shard_map/ppermute | solution.py:641
  799.7 55.4 %collective-permute-start.40 = (bf16[384,1024]{1,0:T(8,128)(2,1)S(1)}, bf16[384,1024]{1,0:T(8,128)(2,1)}, u32[]{:S(2)}, u32[]{:S(2)}) collective-permute-start(bf16[384,1024]{1,0:T(8,128)(2,1)S(1)} %collective-permute-done.36), channel_id=1, source_target_pairs={{0,2},{1,3},{2,0},{3,1},{4,6},{5,7},{6,4},{7,5},{8,10},{9,11},{10,... | collective-permute-start | bytes 2359304 | tf_op jit(solution)/shard_map/ppermute | solution.py:641
  853.4 53.0 %collective-permute-start.48 = (bf16[1024,1024]{1,0:T(8,128)(2,1)}, bf16[1024,1024]{1,0:T(8,128)(2,1)}, u32[]{:S(2)}, u32[]{:S(2)}) collective-permute-start(bf16[1024,1024]{1,0:T(8,128)(2,1)} %bitcast.48), channel_id=1, source_target_pairs={{4,0},{0,1},{6,2},{2,3},{5,4},{1,5},{7,6},{3,7},{12,8},{8,9},{14,1... | collective-permute-start | bytes 6291464 | tf_op jit(solution)/shard_map/ppermute | solution.py:704
  (80 other events, 1485.7 us)
Sparse Core Ops, SparseCore 0:
  39.4 82.6 all-gather.8
  123.7 74.4 all-gather.10
  204.6 56.3 all-gather.12
  262.3 56.7 all-gather.14
  403.3 54.3 reduce-scatter.4
  459.9 57.6 reduce-scatter.6
  552.6 56.4 reduce-scatter.8
  611.4 79.6 reduce-scatter.10
  767.7 65.4 all-reduce.2

commit v7 on v6

--- a/solution.py
+++ b/solution.py
@@ -967,10 +967,9 @@
     output = combine(out_pieces, first, place, after(sent, *scattered))[0]
     norm_total = jnp.stack([jnp.sum(grad_ln * own_normed, axis=0), jnp.sum(grad_ln, axis=0)])
     norm_total = grid.sum_tensor(after(norm_total, *halfway))
-    halfway = halfway + [norm_total]
     back_in1 = return_hidden(grid, after(sums_in1, *halfway))
     back_out1 = return_hidden(grid, after(sums_back1, *halfway))
-    norm_total = grid.sum_dp(norm_total)
+    norm_total = grid.sum_dp(after(norm_total, output))
     norm_total = lax.dynamic_slice_in_dim(
         norm_total, me * (model_width // shards), model_width // shards, 1
     )

time: 924 us -> 913 us (0.988)
    unnamed x85 -> x83, local copies, waits for them, and re-layouts: 20.4 us -> 17.6 us
  transfers between devices with their start and end apart: 62 -> 62, of which waited for: 30 -> 29; matrix products, arithmetic and copies ran while one was open for 12% -> 12% of each run, Pallas kernels for 33% -> 34%
where the time goes in v7:
time: 913 us; the launch traced here: 908 us
  waiting for transfers between devices  347 us (38%)
  Pallas kernels  335 us (37%)
  other arithmetic  69.2 us (8%)
  local copies, waits for them, and re-layouts  60.9 us (7%)
  starting transfers between devices  58.6 us (6%)
  matrix products  22.5 us (2%)
  between operations  14.8 us (2%)
    ppermute x28, waiting for transfers between devices, over_tensor(): lax.ppermute(value, 'tensor', [(t, t ^ other) for t in range(self.size)])  213 us
    all_to_all x4, waiting for transfers between devices, exchange_depth(): lax.all_to_all(value, 'dp', split_axis=0, concat_axis=0, axis_index_group...  71.8 us
    pallas_call x2, Pallas kernels, combine(): pl.pallas_call(functools.partial(kernel, count), grid_spec=pltpu.Prefetch...  66.6 us
    pallas_call x4, Pallas kernels, outer(): pl.pallas_call(functools.partial(outer_kernel, count), grid=(blocks, step...  56.5 us
    pallas_call x4, Pallas kernels, expert_backward(): pl.pallas_call(kernel, grid=(rows // tile,), in_specs=specs, out_specs=[r...  55.2 us
    pallas_call x4, Pallas kernels, expert_forward(): pl.pallas_call(kernel, grid=(rows // tile,), in_specs=specs, out_specs=[r...  53 us
    ppermute x28, starting transfers between devices, over_tensor(): lax.ppermute(value, 'tensor', [(t, t ^ other) for t in range(self.size)])  29.6 us
    pallas_call x1, Pallas kernels, attend_back(): pl.pallas_call(functools.partial(attend_back_kernel, head_size, group, ti...  26.8 us
  transfers between devices with their start and end apart: 62, of which 29 were waited for; matrix products, arithmetic and copies ran while one was open for 12% of the time, Pallas kernels for 34%

profile of v7, /device:TPU:0, one launch (start us, length us, event | category | flops | bytes accessed | tf_op | source)
XLA Modules:
  0.0 908.2 jit_solution(5232278151853766632)
XLA Ops:
  44.1 24.6 %shard_map.190 = (bf16[3072,256]{1,0:T(8,128)(2,1)S(1)}, f32[3,2,2,1024]{3,2,1,0:T(2,128)S(1)}) custom-call(s32[3]{0:T(128)S(1)} %copy-done.14, bf16[3072,768]{1,0:T(8,128)(2,1)S(1)} %copy-done.1, bf16[3072,768]{1,0:T(8,128)(2,1)S(1)} %copy-done.1, bf16[3072,768]{1,0:T(8,128)(2,1)S(1)} %copy-done.1), custom_call_target="tpu_custom_call" | custom-call | flops 3221225472 | bytes 6291456 | tf_op jit(solution)/shard_map/pallas_call | solution.py:121
  87.0 43.9 %collective-permute-done.1.refs_2_ = bf16[3072,256]{1,0:T(8,128)(2,1)} collective-permute-done((bf16[3072,256]{1,0:T(8,128)(2,1)S(1)}, bf16[3072,256]{1,0:T(8,128)(2,1)}, u32[]{:S(2)}, u32[]{:S(2)}) %collective-permute-start.1) | collective-permute-done | bytes 1572896 | tf_op jit(solution)/shard_map/ppermute | solution.py:641
  149.5 23.1 %collective-permute-done.5 = bf16[256,1024]{1,0:T(8,128)(2,1)} collective-permute-done((bf16[256,1024]{1,0:T(8,128)(2,1)S(1)}, bf16[256,1024]{1,0:T(8,128)(2,1)}, u32[]{:S(2)}, u32[]{:S(2)}) %collective-permute-start.5) | collective-permute-done | bytes 524320 | tf_op jit(solution)/shard_map/ppermute | solution.py:641
  203.1 39.7 %all-to-all-done = bf16[4,224,1024]{2,1,0:T(8,128)(2,1)S(1)} async-done(((bf16[4,224,1024]{2,1,0:T(8,128)(2,1)}), bf16[4,224,1024]{2,1,0:T(8,128)(2,1)S(1)}, u32[]{:S(2)}, u32[]{:S(2)}) %all-to-all-start) | async-done | bytes 1835040 | tf_op jit(solution)/shard_map/all_to_all | solution.py:660
  246.8 12.6 %shard_map.195 = (bf16[896,2048]{1,0:T(8,128)(2,1)}, bf16[896,2048]{1,0:T(8,128)(2,1)}, bf16[896,1024]{1,0:T(8,128)(2,1)S(1)}) custom-call(bf16[896,1024]{1,0:T(8,128)(2,1)} %collective-permute-done.9.refs_0_.refs_1_, bf16[2,1024,1024]{2,1,0:T(8,128)(2,1)} %bitcast.158, bf16[2,1024,1024]{2,1,0:T(8,128)(2,1)} %bitcast.159, bf16[2,1024,1024]{2,1,0:T(8,128)(2,1)} %bitcast.166, ...), custom_call_target="tpu_custom_call" | custom-call | flops 7516192768 | bytes 21233664 | tf_op jit(solution)/shard_map/pallas_call | solution.py:506
  261.9 13.7 %shard_map.194 = (bf16[896,2048]{1,0:T(8,128)(2,1)S(1)}, bf16[896,2048]{1,0:T(8,128)(2,1)}, f32[896,1024]{1,0:T(8,128)}) custom-call(bf16[896,1024]{1,0:T(8,128)(2,1)S(1)} %bitcast.114, f32[896,1024]{1,0:T(8,128)} %bitcast_convert_fusion.base_ref, bf16[2,1024,1024]{2,1,0:T(8,128)(2,1)} %bitcast.160, bf16[2,1024,1024]{2,1,0:T(8,128)(2,1)} %bitcast.161, ...), custom_call_target="tpu_custom_call" | custom-call | flops 7516192768 | bytes 21233664 | tf_op jit(solution)/shard_map/pallas_call | solution.py:506
  295.8 23.3 %all-gather.15.cloned.1.call-done = bf16[2048,1024]{1,0:T(8,128)(2,1)} async-done(((bf16[1024,1024]{1,0:T(8,128)(2,1)}), bf16[2048,1024]{1,0:T(8,128)(2,1)}) %all-gather.15.cloned.1.call-update) | async-done | bytes 4194320 | tf_op jit(solution)/shard_map/all_gather | solution.py:686
  319.1 13.0 %shard_map.198 = (bf16[896,2048]{1,0:T(8,128)(2,1)}, bf16[896,2048]{1,0:T(8,128)(2,1)}, bf16[896,1024]{1,0:T(8,128)(2,1)}) custom-call(bf16[896,1024]{1,0:T(8,128)(2,1)} %collective-permute-done.14.refs_0_.refs_1_, bf16[2,1024,1024]{2,1,0:T(8,128)(2,1)} %bitcast.174, bf16[2,1024,1024]{2,1,0:T(8,128)(2,1)} %bitcast.175, bf16[2,1024,1024]{2,1,0:T(8,128)(2,1)} %bitcast.182, ...), custom_call_target="tpu_custom_call" | custom-call | flops 7516192768 | bytes 21233664 | tf_op jit(solution)/shard_map/pallas_call | solution.py:506
  336.1 13.8 %shard_map.196 = (bf16[896,2048]{1,0:T(8,128)(2,1)S(1)}, bf16[896,2048]{1,0:T(8,128)(2,1)}, f32[896,1024]{1,0:T(8,128)}) custom-call(bf16[896,1024]{1,0:T(8,128)(2,1)} %get-tuple-element.135.x_ref.refs_0_, f32[896,1024]{1,0:T(8,128)} %get-tuple-element.136.base_ref, bf16[2,1024,1024]{2,1,0:T(8,128)(2,1)} %bitcast.176, bf16[2,1024,1024]{2,1,0:T(8,128)(2,1)} %bitcast.177, ...), custom_call_target="tpu_custom_call" | custom-call | flops 7516192768 | bytes 21233664 | tf_op jit(solution)/shard_map/pallas_call | solution.py:506
  358.8 14.0 %shard_map.197 = (bf16[896,2048]{1,0:T(8,128)(2,1)S(1)}, f32[896,1024]{1,0:T(8,128)}) custom-call(bf16[896,1024]{1,0:T(8,128)(2,1)S(1)} %get-tuple-element.153.g_ref.refs_2_, bf16[896,2048]{1,0:T(8,128)(2,1)} %get-tuple-element.80.slope_ref, f32[896,1024]{1,0:T(8,128)} %get-tuple-element.154.base_ref, bf16[2,1024,1024]{2,1,0:T(8,128)(2,1)} %bitcast.178, ...), custom_call_target="tpu_custom_call" | custom-call | flops 7516192768 | bytes 21233664 | tf_op jit(solution)/shard_map/pallas_call | solution.py:574
  372.8 14.0 %shard_map.199 = (bf16[896,2048]{1,0:T(8,128)(2,1)}, bf16[896,1024]{1,0:T(8,128)(2,1)S(1)}) custom-call(bf16[896,1024]{1,0:T(8,128)(2,1)S(1)} %collective-permute-done.13.refs_0_.refs_3_, bf16[896,2048]{1,0:T(8,128)(2,1)} %get-tuple-element.82.refs_1_, bf16[2,1024,1024]{2,1,0:T(8,128)(2,1)} %bitcast.180, bf16[2,1024,1024]{2,1,0:T(8,128)(2,1)} %bitcast.181, ...), custom_call_target="tpu_custom_call" | custom-call | flops 7516192768 | bytes 21233664 | tf_op jit(solution)/shard_map/pallas_call | solution.py:574
  388.0 15.1 %shard_map.202 = bf16[2,1024,1024]{2,1,0:T(8,128)(2,1)} custom-call(bf16[896,1024]{1,0:T(8,128)(2,1)} %get-tuple-element.135.x_ref.refs_0_, bf16[896,1024]{1,0:T(8,128)(2,1)} %collective-permute-done.14.refs_0_.refs_1_, bf16[896,2048]{1,0:T(8,128)(2,1)} %copy-done.21, bf16[896,2048]{1,0:T(8,128)(2,1)} %get-tuple-element.91.refs_3_), custom_call_target="tpu_custom_call" | custom-call | flops 7516192768 | bytes 18874368 | tf_op jit(solution)/shard_map/pallas_call | solution.py:616
  439.0 14.7 %shard_map.200 = (bf16[896,2048]{1,0:T(8,128)(2,1)S(1)}, f32[896,1024]{1,0:T(8,128)}) custom-call(bf16[896,1024]{1,0:T(8,128)(2,1)} %get-tuple-element.133.g_ref.refs_2_, bf16[896,2048]{1,0:T(8,128)(2,1)} %get-tuple-element.84.slope_ref, f32[896,1024]{1,0:T(8,128)} %get-tuple-element.134.base_ref, bf16[2,1024,1024]{2,1,0:T(8,128)(2,1)} %bitcast.164, ...), custom_call_target="tpu_custom_call" | custom-call | flops 7516192768 | bytes 21233664 | tf_op jit(solution)/shard_map/pallas_call | solution.py:574
  471.7 15.0 %shard_map.204 = bf16[2,1024,1024]{2,1,0:T(8,128)(2,1)} custom-call(bf16[896,1024]{1,0:T(8,128)(2,1)S(1)} %bitcast.116, bf16[896,1024]{1,0:T(8,128)(2,1)} %collective-permute-done.9.refs_0_.refs_1_, bf16[896,2048]{1,0:T(8,128)(2,1)} %copy-done.20, bf16[896,2048]{1,0:T(8,128)(2,1)} %get-tuple-element.95.refs_3_), custom_call_target="tpu_custom_call" | custom-call | flops 7516192768 | bytes 18874368 | tf_op jit(solution)/shard_map/pallas_call | solution.py:616
  486.7 13.9 %shard_map.205 = bf16[2,1024,1024]{2,1,0:T(8,128)(2,1)} custom-call(bf16[896,2048]{1,0:T(8,128)(2,1)} %copy-done.23, bf16[896,2048]{1,0:T(8,128)(2,1)} %get-tuple-element.97.refs_1_, bf16[896,1024]{1,0:T(8,128)(2,1)} %get-tuple-element.133.g_ref.refs_2_, bf16[896,1024]{1,0:T(8,128)(2,1)} %collective-permute-done.16.refs_0_.refs_3_), custom_call_target="tpu_custom_call" | custom-call | flops 7516192768 | bytes 18874368 | tf_op jit(solution)/shard_map/pallas_call | solution.py:616
  508.3 39.9 %collective-permute-done.22.refs_1_ = bf16[896,1024]{1,0:T(8,128)(2,1)S(1)} collective-permute-done((bf16[896,1024]{1,0:T(8,128)(2,1)}, bf16[896,1024]{1,0:T(8,128)(2,1)S(1)}, u32[]{:S(2)}, u32[]{:S(2)}) %collective-permute-start.22) | collective-permute-done | bytes 1835040 | tf_op jit(solution)/shard_map/ppermute | solution.py:641
  573.9 26.1 %all-to-all-done.3 = bf16[4,224,1024]{2,1,0:T(8,128)(2,1)S(1)} async-done(((bf16[4,224,1024]{2,1,0:T(8,128)(2,1)}), bf16[4,224,1024]{2,1,0:T(8,128)(2,1)S(1)}, u32[]{:S(2)}, u32[]{:S(2)}) %all-to-all-start.3) | async-done | bytes 1835040 | tf_op jit(solution)/shard_map/all_to_all | solution.py:660
  605.1 34.6 %shard_map.206 = (bf16[3072,1024]{1,0:T(8,128)(2,1)}, bf16[3072,256]{1,0:T(8,128)(2,1)S(1)}) custom-call(s32[4]{0:T(128)S(1)} %pad_add_fusion.first_ref, s32[3072,1]{1,0:T(8,128)S(1)} %copy-done.8, bf16[3072,1024]{1,0:T(8,128)(2,1)} %base_ref.1, bf16[896,1024]{1,0:T(8,128)(2,1)} %bitcast.44.refs_0_, bf16[896,1024]{1,0:T(8,128)(2,1)} %copy-done.36, ...), custom_call_target="tpu_custom_call" | custom-call | flops 24159191040 | bytes 19922944 | tf_op jit(solution)/shard_map/pallas_call | solution.py:431
  639.8 26.8 %shard_map.207 = bf16[3072,768]{1,0:T(8,128)(2,1)} custom-call(s32[3]{0:T(128)S(1)} %copy-done.15, bf16[3072,768]{1,0:T(8,128)(2,1)} %copy-done, bf16[3072,768]{1,0:T(8,128)(2,1)} %copy-done, bf16[3072,768]{1,0:T(8,128)(2,1)} %copy-done, bf16[3072,256]{1,0:T(8,128)(2,1)S(1)} %copy-done.3, bf16[3072,256]{1,0:T(8,128)(2,1)S(1)} %get-tuple-element.99.do_ref, ...), custom_call_target="tpu_custom_call" | custom-call | flops 8053063680 | bytes 12582912 | tf_op jit(solution)/shard_map/pallas_call | solution.py:230
  725.5 12.8 %collective-permute-done.31 = bf16[768,512]{1,0:T(8,128)(2,1)} collective-permute-done((bf16[768,512]{1,0:T(8,128)(2,1)S(1)}, bf16[768,512]{1,0:T(8,128)(2,1)}, u32[]{:S(2)}, u32[]{:S(2)}) %collective-permute-start.31) | collective-permute-done | bytes 786464 | tf_op jit(solution)/shard_map/ppermute | solution.py:641
  740.4 12.9 %collective-permute-done.34 = bf16[768,512]{1,0:T(8,128)(2,1)} collective-permute-done((bf16[768,512]{1,0:T(8,128)(2,1)}, bf16[768,512]{1,0:T(8,128)(2,1)}, u32[]{:S(2)}, u32[]{:S(2)}) %collective-permute-start.34) | collective-permute-done | bytes 786464 | tf_op jit(solution)/shard_map/ppermute | solution.py:641
  774.3 16.0 %collective-permute-done.36 = bf16[384,1024]{1,0:T(8,128)(2,1)S(1)} collective-permute-done((bf16[384,1024]{1,0:T(8,128)(2,1)}, bf16[384,1024]{1,0:T(8,128)(2,1)S(1)}, u32[]{:S(2)}, u32[]{:S(2)}) %collective-permute-start.36) | collective-permute-done | bytes 786464 | tf_op jit(solution)/shard_map/ppermute | solution.py:641
  790.3 21.0 %collective-permute-done.39 = bf16[384,1024]{1,0:T(8,128)(2,1)S(1)} collective-permute-done((bf16[384,1024]{1,0:T(8,128)(2,1)}, bf16[384,1024]{1,0:T(8,128)(2,1)S(1)}, u32[]{:S(2)}, u32[]{:S(2)}) %collective-permute-start.39) | collective-permute-done | bytes 786464 | tf_op jit(solution)/shard_map/ppermute | solution.py:641
  843.7 32.0 %shard_map.208 = bf16[3072,1024]{1,0:T(8,128)(2,1)} custom-call(s32[4]{0:T(128)S(1)} %pad_add_fusion.first_ref, s32[3072,1]{1,0:T(8,128)S(1)} %copy-done.9, bf16[3072,1024]{1,0:T(8,128)(2,1)} %shard_map.191.rows_ref.base_ref, bf16[896,1024]{1,0:T(8,128)(2,1)S(1)} %bitcast.119, bf16[896,1024]{1,0:T(8,128)(2,1)} %collective-permute-done.27.refs_1_, ...), custom_call_target="tpu_custom_call" | custom-call | flops 22548578304 | bytes 19922944 | tf_op jit(solution)/shard_map/pallas_call | solution.py:431
  (294 shorter events, 377.0 us)
Async XLA Ops:
  7.2 235.7 %all-gather.9.cloned.1.call-start = ((), (), s32[]{:S(2)}) async-start(), calls=%async_computation.12 | async-start | bytes 6291456 | tf_op jit(solution)/shard_map/all_gather | solution.py:686
  39.3 203.6 %all-gather.11.cloned.1.call-start = ((), (), s32[]{:S(2)}) async-start(), calls=%async_computation.13 | async-start | bytes 6291456 | tf_op jit(solution)/shard_map/all_gather | solution.py:686
  68.7 62.1 %collective-permute-start.1 = (bf16[3072,256]{1,0:T(8,128)(2,1)S(1)}, bf16[3072,256]{1,0:T(8,128)(2,1)}, u32[]{:S(2)}, u32[]{:S(2)}) collective-permute-start(bf16[3072,256]{1,0:T(8,128)(2,1)S(1)} %get-tuple-element.73.refs_0_.o_ref), channel_id=1, source_target_pairs={{0,2},{1,3},{2,0},{3,1},{4,6},{5,7},{6,4},{7,5},{8,10},{9,11},{10,... | collective-permute-start | bytes 4718600 | tf_op jit(solution)/shard_map/ppermute | solution.py:641
  70.9 102.8 %collective-permute-start = (bf16[3072,256]{1,0:T(8,128)(2,1)S(1)}, bf16[3072,256]{1,0:T(8,128)(2,1)}, u32[]{:S(2)}, u32[]{:S(2)}) collective-permute-start(bf16[3072,256]{1,0:T(8,128)(2,1)S(1)} %get-tuple-element.73.refs_0_.o_ref), channel_id=1, source_target_pairs={{0,1},{1,0},{2,3},{3,2},{4,5},{5,4},{6,7},{7,6},{8,9},{9,8},{10,11... | collective-permute-start | bytes 4718600 | tf_op jit(solution)/shard_map/ppermute | solution.py:641
  73.0 74.4 %collective-permute-start.3 = (bf16[256,1024]{1,0:T(8,128)(2,1)S(1)}, bf16[256,1024]{1,0:T(8,128)(2,1)S(1)}, u32[]{:S(2)}, u32[]{:S(2)}) collective-permute-start(bf16[256,1024]{1,0:T(8,128)(2,1)S(1)} %bitcast.122), channel_id=1, source_target_pairs={{0,1},{1,0},{2,3},{3,2},{4,5},{5,4},{6,7},{7,6},{8,9},{9,8},{10,11... | collective-permute-start | bytes 1572872 | tf_op jit(solution)/shard_map/ppermute | solution.py:641
  73.1 76.4 %collective-permute-start.4 = (bf16[256,1024]{1,0:T(8,128)(2,1)S(1)}, bf16[256,1024]{1,0:T(8,128)(2,1)S(1)}, u32[]{:S(2)}, u32[]{:S(2)}) collective-permute-start(bf16[256,1024]{1,0:T(8,128)(2,1)S(1)} %bitcast.123), channel_id=1, source_target_pairs={{0,2},{1,3},{2,0},{3,1},{4,6},{5,7},{6,4},{7,5},{8,10},{9,11},{10,... | collective-permute-start | bytes 1572872 | tf_op jit(solution)/shard_map/ppermute | solution.py:641
  74.4 127.8 %collective-permute-start.11 = (bf16[1024,1024]{1,0:T(8,128)(2,1)}, bf16[1024,1024]{1,0:T(8,128)(2,1)}, u32[]{:S(2)}, u32[]{:S(2)}) collective-permute-start(bf16[1024,1024]{1,0:T(8,128)(2,1)} %get-tuple-element.151), channel_id=1, source_target_pairs={{0,4},{1,0},{2,6},{3,2},{4,5},{5,1},{6,7},{7,3},{8,12},{9,8},{10,1... | collective-permute-start | bytes 6291464 | tf_op jit(solution)/shard_map/ppermute | solution.py:681
  202.2 93.6 %all-gather.13.cloned.1.call-start = ((), (), s32[]{:S(2)}) async-start(), calls=%async_computation.14 | async-start | bytes 6291456 | tf_op jit(solution)/shard_map/all_gather | solution.py:686
  202.9 116.2 %all-gather.15.cloned.1.call-start = ((), (), s32[]{:S(2)}) async-start(), calls=%async_computation.15 | async-start | bytes 6291456 | tf_op jit(solution)/shard_map/all_gather | solution.py:686
  290.9 60.9 %all-to-all-start.1 = ((bf16[4,224,1024]{2,1,0:T(8,128)(2,1)}), bf16[4,224,1024]{2,1,0:T(8,128)(2,1)}, u32[]{:S(2)}, u32[]{:S(2)}) async-start(bf16[4,224,1024]{2,1,0:T(8,128)(2,1)} %bitcast.120), calls=%async_computation.1 | async-start | bytes 3670016 | tf_op jit(solution)/shard_map/all_to_all | solution.py:660
  295.3 306.9 %reduce-scatter.5.cloned.1.call-start = ((), (), s32[]{:S(2)}) async-start(), calls=%async_computation.8 | async-start | bytes 6291456 | tf_op jit(solution)/shard_map/reduce_scatter | solution.py:697
  403.2 199.4 %reduce-scatter.7.cloned.1.call-start = ((), (), s32[]{:S(2)}) async-start(), calls=%async_computation.9 | async-start | bytes 6291456 | tf_op jit(solution)/shard_map/reduce_scatter | solution.py:697
  463.4 221.7 %reduce-scatter.9.cloned.1.call-start = ((), (), s32[]{:S(2)}) async-start(), calls=%async_computation.10 | async-start | bytes 6291456 | tf_op jit(solution)/shard_map/reduce_scatter | solution.py:697
  552.5 138.7 %reduce-scatter.11.cloned.1.call-start = ((), (), s32[]{:S(2)}) async-start(), calls=%async_computation.11 | async-start | bytes 6291456 | tf_op jit(solution)/shard_map/reduce_scatter | solution.py:697
  557.8 326.0 %all-reduce.3.cloned.1.call-start = ((), (), s32[]{:S(2)}) async-start(), calls=%async_computation.16 | async-start | bytes 4194304 | tf_op jit(solution)/shard_map/psum | solution.py:949
  600.0 76.3 %collective-permute-start.27 = (bf16[896,1024]{1,0:T(8,128)(2,1)S(1)}, bf16[896,1024]{1,0:T(8,128)(2,1)}, u32[]{:S(2)}, u32[]{:S(2)}) collective-permute-start(bf16[896,1024]{1,0:T(8,128)(2,1)S(1)} %bitcast.117), channel_id=1, source_target_pairs={{0,1},{1,0},{2,3},{3,2},{4,5},{5,4},{6,7},{7,6},{8,9},{9,8},{10,11... | collective-permute-start | bytes 5505032 | tf_op jit(solution)/shard_map/ppermute | solution.py:641
  601.5 74.7 %collective-permute-start.28 = (bf16[896,1024]{1,0:T(8,128)(2,1)S(1)}, bf16[896,1024]{1,0:T(8,128)(2,1)}, u32[]{:S(2)}, u32[]{:S(2)}) collective-permute-start(bf16[896,1024]{1,0:T(8,128)(2,1)S(1)} %bitcast.118), channel_id=1, source_target_pairs={{0,2},{1,3},{2,0},{3,1},{4,6},{5,7},{6,4},{7,5},{8,10},{9,11},{10,... | collective-permute-start | bytes 5505032 | tf_op jit(solution)/shard_map/ppermute | solution.py:641
  602.2 74.1 %collective-permute-start.25 = (bf16[1024,1024]{1,0:T(8,128)(2,1)}, bf16[1024,1024]{1,0:T(8,128)(2,1)}, u32[]{:S(2)}, u32[]{:S(2)}) collective-permute-start(bf16[1024,1024]{1,0:T(8,128)(2,1)} %bitcast.192), channel_id=1, source_target_pairs={{4,0},{0,1},{6,2},{2,3},{5,4},{1,5},{7,6},{3,7},{12,8},{8,9},{14,1... | collective-permute-start | bytes 6291464 | tf_op jit(solution)/shard_map/ppermute | solution.py:704
  602.5 82.6 %collective-permute-start.26 = (bf16[1024,1024]{1,0:T(8,128)(2,1)}, bf16[1024,1024]{1,0:T(8,128)(2,1)}, u32[]{:S(2)}, u32[]{:S(2)}) collective-permute-start(bf16[1024,1024]{1,0:T(8,128)(2,1)} %bitcast.193), channel_id=1, source_target_pairs={{4,0},{0,1},{6,2},{2,3},{5,4},{1,5},{7,6},{3,7},{12,8},{8,9},{14,1... | collective-permute-start | bytes 6291464 | tf_op jit(solution)/shard_map/ppermute | solution.py:704
  738.9 104.8 %collective-permute-start.33 = (bf16[896,1024]{1,0:T(8,128)(2,1)}, bf16[896,1024]{1,0:T(8,128)(2,1)}, u32[]{:S(2)}, u32[]{:S(2)}) collective-permute-start(bf16[896,1024]{1,0:T(8,128)(2,1)} %collective-permute-done.27.refs_1_), channel_id=1, source_target_pairs={{0,2},{1,3},{2,0},{3,1},{4,6},{5,7},{6,4},{7,5},{8,10},{9,11},{10,... | collective-permute-start | bytes 5505032 | tf_op jit(solution)/shard_map/ppermute | solution.py:641
  772.2 56.1 %collective-permute-start.38 = (bf16[384,1024]{1,0:T(8,128)(2,1)}, bf16[384,1024]{1,0:T(8,128)(2,1)}, u32[]{:S(2)}, u32[]{:S(2)}) collective-permute-start(bf16[384,1024]{1,0:T(8,128)(2,1)} %get-tuple-element.156), channel_id=1, source_target_pairs={{0,2},{1,3},{2,0},{3,1},{4,6},{5,7},{6,4},{7,5},{8,10},{9,11},{10,... | collective-permute-start | bytes 2359304 | tf_op jit(solution)/shard_map/ppermute | solution.py:641
  811.8 77.3 %collective-permute-start.47 = (bf16[1024,1024]{1,0:T(8,128)(2,1)}, bf16[1024,1024]{1,0:T(8,128)(2,1)}, u32[]{:S(2)}, u32[]{:S(2)}) collective-permute-start(bf16[1024,1024]{1,0:T(8,128)(2,1)} %bitcast.190), channel_id=1, source_target_pairs={{4,0},{0,1},{6,2},{2,3},{5,4},{1,5},{7,6},{3,7},{12,8},{8,9},{14,1... | collective-permute-start | bytes 6291464 | tf_op jit(solution)/shard_map/ppermute | solution.py:704
  814.2 81.1 %collective-permute-start.48 = (bf16[1024,1024]{1,0:T(8,128)(2,1)}, bf16[1024,1024]{1,0:T(8,128)(2,1)}, u32[]{:S(2)}, u32[]{:S(2)}) collective-permute-start(bf16[1024,1024]{1,0:T(8,128)(2,1)} %bitcast.191), channel_id=1, source_target_pairs={{4,0},{0,1},{6,2},{2,3},{5,4},{1,5},{7,6},{3,7},{12,8},{8,9},{14,1... | collective-permute-start | bytes 6291464 | tf_op jit(solution)/shard_map/ppermute | solution.py:704
  816.3 62.1 %collective-permute-start.40 = (bf16[384,1024]{1,0:T(8,128)(2,1)S(1)}, bf16[384,1024]{1,0:T(8,128)(2,1)S(1)}, u32[]{:S(2)}, u32[]{:S(2)}) collective-permute-start(bf16[384,1024]{1,0:T(8,128)(2,1)S(1)} %collective-permute-done.36), channel_id=1, source_target_pairs={{0,2},{1,3},{2,0},{3,1},{4,6},{5,7},{6,4},{7,5},{8,10},{9,11},{10,... | collective-permute-start | bytes 2359304 | tf_op jit(solution)/shard_map/ppermute | solution.py:641
  (79 other events, 1491.2 us)
Sparse Core Ops, SparseCore 0:
  39.4 82.6 all-gather.8
  123.7 74.4 all-gather.10
  204.5 56.3 all-gather.12
  262.3 56.7 all-gather.14
  403.3 54.3 reduce-scatter.4
  459.9 57.5 reduce-scatter.6
  552.6 56.4 reduce-scatter.8
  611.4 79.6 reduce-scatter.10
  774.4 64.3 all-reduce.2

commit v8 on v7

--- a/solution.py
+++ b/solution.py
@@ -95,12 +95,14 @@
             k_a, v_a, spare = heads[a]
             mine_q = (lane_q >= a * head_size) & (lane_q < (a + 1) * head_size)
             q_a = jnp.where(mine_q, q, jnp.where(lane_q == spare, 1.0, 0.0).astype(BF16))
-            scores = dot(k_a[:end], q_a, ((1,), (1,)))
-            last = jnp.where(causal, scores[i * tile :], MASKED)
-            scores = jnp.concatenate([scores[: i * tile], last], axis=0) if i else last
-            top = jnp.max(scores, axis=0, keepdims=True)
-            probs = jnp.exp(scores - top).astype(BF16)
-            result = dot(v_a[:end], probs, ((0,), (0,)))
+            last = jnp.where(causal, dot(k_a[i * tile : end], q_a, ((1,), (1,))), MASKED)
+            top = jnp.max(last, axis=0, keepdims=True)
+            if i:
+                scores = dot(k_a[: i * tile], q_a, ((1,), (1,)))
+                top = jnp.maximum(top, jnp.max(scores, axis=0, keepdims=True))
+            result = dot(v_a[i * tile : end], jnp.exp(last - top).astype(BF16), ((0,), (0,)))
+            if i:
+                result += dot(v_a[: i * tile], jnp.exp(scores - top).astype(BF16), ((0,), (0,)))
             total = result[spare : spare + 1, :]
             lse_ref[0, 0, a : a + 1, i * tile : end] = top + jnp.log(total)
             result = result / total

time: 913 us -> 912 us (level)
  transfers between devices with their start and end apart: 62 -> 62, of which waited for: 29 -> 29; matrix products, arithmetic and copies ran while one was open for 12% -> 13% of each run, Pallas kernels for 34% -> 33%
where the time goes in v8:
time: 912 us; the launch traced here: 907 us
  waiting for transfers between devices  348 us (38%)
  Pallas kernels  333 us (37%)
  other arithmetic  69.2 us (8%)
  local copies, waits for them, and re-layouts  60.9 us (7%)
  starting transfers between devices  59.1 us (6%)
  matrix products  22.5 us (2%)
  between operations  14.8 us (2%)
    ppermute x28, waiting for transfers between devices, over_tensor(): lax.ppermute(value, 'tensor', [(t, t ^ other) for t in range(self.size)])  212 us
    all_to_all x4, waiting for transfers between devices, exchange_depth(): lax.all_to_all(value, 'dp', split_axis=0, concat_axis=0, axis_index_group...  72 us
    pallas_call x2, Pallas kernels, combine(): pl.pallas_call(functools.partial(kernel, count), grid_spec=pltpu.Prefetch...  66.6 us
    pallas_call x4, Pallas kernels, outer(): pl.pallas_call(functools.partial(outer_kernel, count), grid=(blocks, step...  56.5 us
    pallas_call x4, Pallas kernels, expert_backward(): pl.pallas_call(kernel, grid=(rows // tile,), in_specs=specs, out_specs=[r...  55.2 us
    pallas_call x4, Pallas kernels, expert_forward(): pl.pallas_call(kernel, grid=(rows // tile,), in_specs=specs, out_specs=[r...  53 us
    ppermute x28, starting transfers between devices, over_tensor(): lax.ppermute(value, 'tensor', [(t, t ^ other) for t in range(self.size)])  30.2 us
    pallas_call x1, Pallas kernels, attend_back(): pl.pallas_call(functools.partial(attend_back_kernel, head_size, group, ti...  26.8 us
  transfers between devices with their start and end apart: 62, of which 29 were waited for; matrix products, arithmetic and copies ran while one was open for 13% of the time, Pallas kernels for 33%

profile of v8, /device:TPU:0, one launch (start us, length us, event | category | flops | bytes accessed | tf_op | source)
XLA Modules:
  0.0 907.4 jit_solution(14409310031150992089)
XLA Ops:
  44.1 21.9 %shard_map.190 = (bf16[3072,256]{1,0:T(8,128)(2,1)S(1)}, f32[3,2,2,1024]{3,2,1,0:T(2,128)S(1)}) custom-call(s32[3]{0:T(128)S(1)} %copy-done.14, bf16[3072,768]{1,0:T(8,128)(2,1)S(1)} %copy-done.1, bf16[3072,768]{1,0:T(8,128)(2,1)S(1)} %copy-done.1, bf16[3072,768]{1,0:T(8,128)(2,1)S(1)} %copy-done.1), custom_call_target="tpu_custom_call" | custom-call | flops 3221225472 | bytes 6291456 | tf_op jit(solution)/shard_map/pallas_call | solution.py:123
  87.0 43.8 %collective-permute-done.1.refs_2_ = bf16[3072,256]{1,0:T(8,128)(2,1)} collective-permute-done((bf16[3072,256]{1,0:T(8,128)(2,1)S(1)}, bf16[3072,256]{1,0:T(8,128)(2,1)}, u32[]{:S(2)}, u32[]{:S(2)}) %collective-permute-start.1) | collective-permute-done | bytes 1572896 | tf_op jit(solution)/shard_map/ppermute | solution.py:643
  149.5 23.2 %collective-permute-done.5 = bf16[256,1024]{1,0:T(8,128)(2,1)} collective-permute-done((bf16[256,1024]{1,0:T(8,128)(2,1)S(1)}, bf16[256,1024]{1,0:T(8,128)(2,1)}, u32[]{:S(2)}, u32[]{:S(2)}) %collective-permute-start.5) | collective-permute-done | bytes 524320 | tf_op jit(solution)/shard_map/ppermute | solution.py:643
  202.3 39.8 %all-to-all-done = bf16[4,224,1024]{2,1,0:T(8,128)(2,1)S(1)} async-done(((bf16[4,224,1024]{2,1,0:T(8,128)(2,1)}), bf16[4,224,1024]{2,1,0:T(8,128)(2,1)S(1)}, u32[]{:S(2)}, u32[]{:S(2)}) %all-to-all-start) | async-done | bytes 1835040 | tf_op jit(solution)/shard_map/all_to_all | solution.py:662
  246.1 12.6 %shard_map.195 = (bf16[896,2048]{1,0:T(8,128)(2,1)}, bf16[896,2048]{1,0:T(8,128)(2,1)}, bf16[896,1024]{1,0:T(8,128)(2,1)S(1)}) custom-call(bf16[896,1024]{1,0:T(8,128)(2,1)} %collective-permute-done.9.refs_0_.refs_1_, bf16[2,1024,1024]{2,1,0:T(8,128)(2,1)} %bitcast.158, bf16[2,1024,1024]{2,1,0:T(8,128)(2,1)} %bitcast.159, bf16[2,1024,1024]{2,1,0:T(8,128)(2,1)} %bitcast.166, ...), custom_call_target="tpu_custom_call" | custom-call | flops 7516192768 | bytes 21233664 | tf_op jit(solution)/shard_map/pallas_call | solution.py:508
  261.2 13.7 %shard_map.194 = (bf16[896,2048]{1,0:T(8,128)(2,1)S(1)}, bf16[896,2048]{1,0:T(8,128)(2,1)}, f32[896,1024]{1,0:T(8,128)}) custom-call(bf16[896,1024]{1,0:T(8,128)(2,1)S(1)} %bitcast.114, f32[896,1024]{1,0:T(8,128)} %bitcast_convert_fusion.base_ref, bf16[2,1024,1024]{2,1,0:T(8,128)(2,1)} %bitcast.160, bf16[2,1024,1024]{2,1,0:T(8,128)(2,1)} %bitcast.161, ...), custom_call_target="tpu_custom_call" | custom-call | flops 7516192768 | bytes 21233664 | tf_op jit(solution)/shard_map/pallas_call | solution.py:508
  295.1 23.2 %all-gather.15.cloned.1.call-done = bf16[2048,1024]{1,0:T(8,128)(2,1)} async-done(((bf16[1024,1024]{1,0:T(8,128)(2,1)}), bf16[2048,1024]{1,0:T(8,128)(2,1)}) %all-gather.15.cloned.1.call-update) | async-done | bytes 4194320 | tf_op jit(solution)/shard_map/all_gather | solution.py:688
  318.3 13.0 %shard_map.198 = (bf16[896,2048]{1,0:T(8,128)(2,1)}, bf16[896,2048]{1,0:T(8,128)(2,1)}, bf16[896,1024]{1,0:T(8,128)(2,1)}) custom-call(bf16[896,1024]{1,0:T(8,128)(2,1)} %collective-permute-done.14.refs_0_.refs_1_, bf16[2,1024,1024]{2,1,0:T(8,128)(2,1)} %bitcast.174, bf16[2,1024,1024]{2,1,0:T(8,128)(2,1)} %bitcast.175, bf16[2,1024,1024]{2,1,0:T(8,128)(2,1)} %bitcast.182, ...), custom_call_target="tpu_custom_call" | custom-call | flops 7516192768 | bytes 21233664 | tf_op jit(solution)/shard_map/pallas_call | solution.py:508
  335.3 13.8 %shard_map.196 = (bf16[896,2048]{1,0:T(8,128)(2,1)S(1)}, bf16[896,2048]{1,0:T(8,128)(2,1)}, f32[896,1024]{1,0:T(8,128)}) custom-call(bf16[896,1024]{1,0:T(8,128)(2,1)} %get-tuple-element.135.x_ref.refs_0_, f32[896,1024]{1,0:T(8,128)} %get-tuple-element.136.base_ref, bf16[2,1024,1024]{2,1,0:T(8,128)(2,1)} %bitcast.176, bf16[2,1024,1024]{2,1,0:T(8,128)(2,1)} %bitcast.177, ...), custom_call_target="tpu_custom_call" | custom-call | flops 7516192768 | bytes 21233664 | tf_op jit(solution)/shard_map/pallas_call | solution.py:508
  358.0 14.0 %shard_map.197 = (bf16[896,2048]{1,0:T(8,128)(2,1)S(1)}, f32[896,1024]{1,0:T(8,128)}) custom-call(bf16[896,1024]{1,0:T(8,128)(2,1)S(1)} %get-tuple-element.153.g_ref.refs_2_, bf16[896,2048]{1,0:T(8,128)(2,1)} %get-tuple-element.80.slope_ref, f32[896,1024]{1,0:T(8,128)} %get-tuple-element.154.base_ref, bf16[2,1024,1024]{2,1,0:T(8,128)(2,1)} %bitcast.178, ...), custom_call_target="tpu_custom_call" | custom-call | flops 7516192768 | bytes 21233664 | tf_op jit(solution)/shard_map/pallas_call | solution.py:576
  372.0 14.0 %shard_map.199 = (bf16[896,2048]{1,0:T(8,128)(2,1)}, bf16[896,1024]{1,0:T(8,128)(2,1)S(1)}) custom-call(bf16[896,1024]{1,0:T(8,128)(2,1)S(1)} %collective-permute-done.13.refs_0_.refs_3_, bf16[896,2048]{1,0:T(8,128)(2,1)} %get-tuple-element.82.refs_1_, bf16[2,1024,1024]{2,1,0:T(8,128)(2,1)} %bitcast.180, bf16[2,1024,1024]{2,1,0:T(8,128)(2,1)} %bitcast.181, ...), custom_call_target="tpu_custom_call" | custom-call | flops 7516192768 | bytes 21233664 | tf_op jit(solution)/shard_map/pallas_call | solution.py:576
  387.2 15.1 %shard_map.202 = bf16[2,1024,1024]{2,1,0:T(8,128)(2,1)} custom-call(bf16[896,1024]{1,0:T(8,128)(2,1)} %get-tuple-element.135.x_ref.refs_0_, bf16[896,1024]{1,0:T(8,128)(2,1)} %collective-permute-done.14.refs_0_.refs_1_, bf16[896,2048]{1,0:T(8,128)(2,1)} %copy-done.21, bf16[896,2048]{1,0:T(8,128)(2,1)} %get-tuple-element.91.refs_3_), custom_call_target="tpu_custom_call" | custom-call | flops 7516192768 | bytes 18874368 | tf_op jit(solution)/shard_map/pallas_call | solution.py:618
  438.2 14.7 %shard_map.200 = (bf16[896,2048]{1,0:T(8,128)(2,1)S(1)}, f32[896,1024]{1,0:T(8,128)}) custom-call(bf16[896,1024]{1,0:T(8,128)(2,1)} %get-tuple-element.133.g_ref.refs_2_, bf16[896,2048]{1,0:T(8,128)(2,1)} %get-tuple-element.84.slope_ref, f32[896,1024]{1,0:T(8,128)} %get-tuple-element.134.base_ref, bf16[2,1024,1024]{2,1,0:T(8,128)(2,1)} %bitcast.164, ...), custom_call_target="tpu_custom_call" | custom-call | flops 7516192768 | bytes 21233664 | tf_op jit(solution)/shard_map/pallas_call | solution.py:576
  470.9 15.0 %shard_map.204 = bf16[2,1024,1024]{2,1,0:T(8,128)(2,1)} custom-call(bf16[896,1024]{1,0:T(8,128)(2,1)S(1)} %bitcast.116, bf16[896,1024]{1,0:T(8,128)(2,1)} %collective-permute-done.9.refs_0_.refs_1_, bf16[896,2048]{1,0:T(8,128)(2,1)} %copy-done.20, bf16[896,2048]{1,0:T(8,128)(2,1)} %get-tuple-element.95.refs_3_), custom_call_target="tpu_custom_call" | custom-call | flops 7516192768 | bytes 18874368 | tf_op jit(solution)/shard_map/pallas_call | solution.py:618
  485.9 13.9 %shard_map.205 = bf16[2,1024,1024]{2,1,0:T(8,128)(2,1)} custom-call(bf16[896,2048]{1,0:T(8,128)(2,1)} %copy-done.23, bf16[896,2048]{1,0:T(8,128)(2,1)} %get-tuple-element.97.refs_1_, bf16[896,1024]{1,0:T(8,128)(2,1)} %get-tuple-element.133.g_ref.refs_2_, bf16[896,1024]{1,0:T(8,128)(2,1)} %collective-permute-done.16.refs_0_.refs_3_), custom_call_target="tpu_custom_call" | custom-call | flops 7516192768 | bytes 18874368 | tf_op jit(solution)/shard_map/pallas_call | solution.py:618
  507.5 39.9 %collective-permute-done.22.refs_1_ = bf16[896,1024]{1,0:T(8,128)(2,1)S(1)} collective-permute-done((bf16[896,1024]{1,0:T(8,128)(2,1)}, bf16[896,1024]{1,0:T(8,128)(2,1)S(1)}, u32[]{:S(2)}, u32[]{:S(2)}) %collective-permute-start.22) | collective-permute-done | bytes 1835040 | tf_op jit(solution)/shard_map/ppermute | solution.py:643
  573.1 26.1 %all-to-all-done.3 = bf16[4,224,1024]{2,1,0:T(8,128)(2,1)S(1)} async-done(((bf16[4,224,1024]{2,1,0:T(8,128)(2,1)}), bf16[4,224,1024]{2,1,0:T(8,128)(2,1)S(1)}, u32[]{:S(2)}, u32[]{:S(2)}) %all-to-all-start.3) | async-done | bytes 1835040 | tf_op jit(solution)/shard_map/all_to_all | solution.py:662
  604.3 34.6 %shard_map.206 = (bf16[3072,1024]{1,0:T(8,128)(2,1)}, bf16[3072,256]{1,0:T(8,128)(2,1)S(1)}) custom-call(s32[4]{0:T(128)S(1)} %pad_add_fusion.first_ref, s32[3072,1]{1,0:T(8,128)S(1)} %copy-done.8, bf16[3072,1024]{1,0:T(8,128)(2,1)} %base_ref.1, bf16[896,1024]{1,0:T(8,128)(2,1)} %bitcast.44.refs_0_, bf16[896,1024]{1,0:T(8,128)(2,1)} %copy-done.36, ...), custom_call_target="tpu_custom_call" | custom-call | flops 24159191040 | bytes 19922944 | tf_op jit(solution)/shard_map/pallas_call | solution.py:433
  638.9 26.8 %shard_map.207 = bf16[3072,768]{1,0:T(8,128)(2,1)} custom-call(s32[3]{0:T(128)S(1)} %copy-done.15, bf16[3072,768]{1,0:T(8,128)(2,1)} %copy-done, bf16[3072,768]{1,0:T(8,128)(2,1)} %copy-done, bf16[3072,768]{1,0:T(8,128)(2,1)} %copy-done, bf16[3072,256]{1,0:T(8,128)(2,1)S(1)} %copy-done.3, bf16[3072,256]{1,0:T(8,128)(2,1)S(1)} %get-tuple-element.99.do_ref, ...), custom_call_target="tpu_custom_call" | custom-call | flops 8053063680 | bytes 12582912 | tf_op jit(solution)/shard_map/pallas_call | solution.py:232
  724.7 12.8 %collective-permute-done.31 = bf16[768,512]{1,0:T(8,128)(2,1)} collective-permute-done((bf16[768,512]{1,0:T(8,128)(2,1)S(1)}, bf16[768,512]{1,0:T(8,128)(2,1)}, u32[]{:S(2)}, u32[]{:S(2)}) %collective-permute-start.31) | collective-permute-done | bytes 786464 | tf_op jit(solution)/shard_map/ppermute | solution.py:643
  739.6 12.9 %collective-permute-done.34 = bf16[768,512]{1,0:T(8,128)(2,1)} collective-permute-done((bf16[768,512]{1,0:T(8,128)(2,1)}, bf16[768,512]{1,0:T(8,128)(2,1)}, u32[]{:S(2)}, u32[]{:S(2)}) %collective-permute-start.34) | collective-permute-done | bytes 786464 | tf_op jit(solution)/shard_map/ppermute | solution.py:643
  773.5 16.0 %collective-permute-done.36 = bf16[384,1024]{1,0:T(8,128)(2,1)S(1)} collective-permute-done((bf16[384,1024]{1,0:T(8,128)(2,1)}, bf16[384,1024]{1,0:T(8,128)(2,1)S(1)}, u32[]{:S(2)}, u32[]{:S(2)}) %collective-permute-start.36) | collective-permute-done | bytes 786464 | tf_op jit(solution)/shard_map/ppermute | solution.py:643
  789.5 21.0 %collective-permute-done.39 = bf16[384,1024]{1,0:T(8,128)(2,1)S(1)} collective-permute-done((bf16[384,1024]{1,0:T(8,128)(2,1)}, bf16[384,1024]{1,0:T(8,128)(2,1)S(1)}, u32[]{:S(2)}, u32[]{:S(2)}) %collective-permute-start.39) | collective-permute-done | bytes 786464 | tf_op jit(solution)/shard_map/ppermute | solution.py:643
  842.9 32.0 %shard_map.208 = bf16[3072,1024]{1,0:T(8,128)(2,1)} custom-call(s32[4]{0:T(128)S(1)} %pad_add_fusion.first_ref, s32[3072,1]{1,0:T(8,128)S(1)} %copy-done.9, bf16[3072,1024]{1,0:T(8,128)(2,1)} %shard_map.191.rows_ref.base_ref, bf16[896,1024]{1,0:T(8,128)(2,1)S(1)} %bitcast.119, bf16[896,1024]{1,0:T(8,128)(2,1)} %collective-permute-done.27.refs_1_, ...), custom_call_target="tpu_custom_call" | custom-call | flops 22548578304 | bytes 19922944 | tf_op jit(solution)/shard_map/pallas_call | solution.py:433
  (294 shorter events, 378.9 us)
Async XLA Ops:
  7.2 235.0 %all-gather.9.cloned.1.call-start = ((), (), s32[]{:S(2)}) async-start(), calls=%async_computation.12 | async-start | bytes 6291456 | tf_op jit(solution)/shard_map/all_gather | solution.py:688
  39.3 202.9 %all-gather.11.cloned.1.call-start = ((), (), s32[]{:S(2)}) async-start(), calls=%async_computation.13 | async-start | bytes 6291456 | tf_op jit(solution)/shard_map/all_gather | solution.py:688
  66.0 64.8 %collective-permute-start.1 = (bf16[3072,256]{1,0:T(8,128)(2,1)S(1)}, bf16[3072,256]{1,0:T(8,128)(2,1)}, u32[]{:S(2)}, u32[]{:S(2)}) collective-permute-start(bf16[3072,256]{1,0:T(8,128)(2,1)S(1)} %get-tuple-element.73.refs_0_.o_ref), channel_id=1, source_target_pairs={{0,2},{1,3},{2,0},{3,1},{4,6},{5,7},{6,4},{7,5},{8,10},{9,11},{10,... | collective-permute-start | bytes 4718600 | tf_op jit(solution)/shard_map/ppermute | solution.py:643
  70.3 103.5 %collective-permute-start = (bf16[3072,256]{1,0:T(8,128)(2,1)S(1)}, bf16[3072,256]{1,0:T(8,128)(2,1)}, u32[]{:S(2)}, u32[]{:S(2)}) collective-permute-start(bf16[3072,256]{1,0:T(8,128)(2,1)S(1)} %get-tuple-element.73.refs_0_.o_ref), channel_id=1, source_target_pairs={{0,1},{1,0},{2,3},{3,2},{4,5},{5,4},{6,7},{7,6},{8,9},{9,8},{10,11... | collective-permute-start | bytes 4718600 | tf_op jit(solution)/shard_map/ppermute | solution.py:643
  70.4 77.1 %collective-permute-start.3 = (bf16[256,1024]{1,0:T(8,128)(2,1)S(1)}, bf16[256,1024]{1,0:T(8,128)(2,1)S(1)}, u32[]{:S(2)}, u32[]{:S(2)}) collective-permute-start(bf16[256,1024]{1,0:T(8,128)(2,1)S(1)} %bitcast.122), channel_id=1, source_target_pairs={{0,1},{1,0},{2,3},{3,2},{4,5},{5,4},{6,7},{7,6},{8,9},{9,8},{10,11... | collective-permute-start | bytes 1572872 | tf_op jit(solution)/shard_map/ppermute | solution.py:643
  72.4 77.1 %collective-permute-start.4 = (bf16[256,1024]{1,0:T(8,128)(2,1)S(1)}, bf16[256,1024]{1,0:T(8,128)(2,1)S(1)}, u32[]{:S(2)}, u32[]{:S(2)}) collective-permute-start(bf16[256,1024]{1,0:T(8,128)(2,1)S(1)} %bitcast.123), channel_id=1, source_target_pairs={{0,2},{1,3},{2,0},{3,1},{4,6},{5,7},{6,4},{7,5},{8,10},{9,11},{10,... | collective-permute-start | bytes 1572872 | tf_op jit(solution)/shard_map/ppermute | solution.py:643
  74.4 127.0 %collective-permute-start.11 = (bf16[1024,1024]{1,0:T(8,128)(2,1)}, bf16[1024,1024]{1,0:T(8,128)(2,1)}, u32[]{:S(2)}, u32[]{:S(2)}) collective-permute-start(bf16[1024,1024]{1,0:T(8,128)(2,1)} %get-tuple-element.151), channel_id=1, source_target_pairs={{0,4},{1,0},{2,6},{3,2},{4,5},{5,1},{6,7},{7,3},{8,12},{9,8},{10,1... | collective-permute-start | bytes 6291464 | tf_op jit(solution)/shard_map/ppermute | solution.py:683
  201.4 93.7 %all-gather.13.cloned.1.call-start = ((), (), s32[]{:S(2)}) async-start(), calls=%async_computation.14 | async-start | bytes 6291456 | tf_op jit(solution)/shard_map/all_gather | solution.py:688
  202.1 116.2 %all-gather.15.cloned.1.call-start = ((), (), s32[]{:S(2)}) async-start(), calls=%async_computation.15 | async-start | bytes 6291456 | tf_op jit(solution)/shard_map/all_gather | solution.py:688
  290.2 60.8 %all-to-all-start.1 = ((bf16[4,224,1024]{2,1,0:T(8,128)(2,1)}), bf16[4,224,1024]{2,1,0:T(8,128)(2,1)}, u32[]{:S(2)}, u32[]{:S(2)}) async-start(bf16[4,224,1024]{2,1,0:T(8,128)(2,1)} %bitcast.120), calls=%async_computation.1 | async-start | bytes 3670016 | tf_op jit(solution)/shard_map/all_to_all | solution.py:662
  294.6 306.8 %reduce-scatter.5.cloned.1.call-start = ((), (), s32[]{:S(2)}) async-start(), calls=%async_computation.8 | async-start | bytes 6291456 | tf_op jit(solution)/shard_map/reduce_scatter | solution.py:699
  402.3 199.4 %reduce-scatter.7.cloned.1.call-start = ((), (), s32[]{:S(2)}) async-start(), calls=%async_computation.9 | async-start | bytes 6291456 | tf_op jit(solution)/shard_map/reduce_scatter | solution.py:699
  462.6 221.7 %reduce-scatter.9.cloned.1.call-start = ((), (), s32[]{:S(2)}) async-start(), calls=%async_computation.10 | async-start | bytes 6291456 | tf_op jit(solution)/shard_map/reduce_scatter | solution.py:699
  551.7 138.7 %reduce-scatter.11.cloned.1.call-start = ((), (), s32[]{:S(2)}) async-start(), calls=%async_computation.11 | async-start | bytes 6291456 | tf_op jit(solution)/shard_map/reduce_scatter | solution.py:699
  557.0 326.0 %all-reduce.3.cloned.1.call-start = ((), (), s32[]{:S(2)}) async-start(), calls=%async_computation.16 | async-start | bytes 4194304 | tf_op jit(solution)/shard_map/psum | solution.py:951
  599.2 76.3 %collective-permute-start.27 = (bf16[896,1024]{1,0:T(8,128)(2,1)S(1)}, bf16[896,1024]{1,0:T(8,128)(2,1)}, u32[]{:S(2)}, u32[]{:S(2)}) collective-permute-start(bf16[896,1024]{1,0:T(8,128)(2,1)S(1)} %bitcast.117), channel_id=1, source_target_pairs={{0,1},{1,0},{2,3},{3,2},{4,5},{5,4},{6,7},{7,6},{8,9},{9,8},{10,11... | collective-permute-start | bytes 5505032 | tf_op jit(solution)/shard_map/ppermute | solution.py:643
  600.7 74.7 %collective-permute-start.28 = (bf16[896,1024]{1,0:T(8,128)(2,1)S(1)}, bf16[896,1024]{1,0:T(8,128)(2,1)}, u32[]{:S(2)}, u32[]{:S(2)}) collective-permute-start(bf16[896,1024]{1,0:T(8,128)(2,1)S(1)} %bitcast.118), channel_id=1, source_target_pairs={{0,2},{1,3},{2,0},{3,1},{4,6},{5,7},{6,4},{7,5},{8,10},{9,11},{10,... | collective-permute-start | bytes 5505032 | tf_op jit(solution)/shard_map/ppermute | solution.py:643
  601.3 74.1 %collective-permute-start.25 = (bf16[1024,1024]{1,0:T(8,128)(2,1)}, bf16[1024,1024]{1,0:T(8,128)(2,1)}, u32[]{:S(2)}, u32[]{:S(2)}) collective-permute-start(bf16[1024,1024]{1,0:T(8,128)(2,1)} %bitcast.192), channel_id=1, source_target_pairs={{4,0},{0,1},{6,2},{2,3},{5,4},{1,5},{7,6},{3,7},{12,8},{8,9},{14,1... | collective-permute-start | bytes 6291464 | tf_op jit(solution)/shard_map/ppermute | solution.py:706
  601.7 82.6 %collective-permute-start.26 = (bf16[1024,1024]{1,0:T(8,128)(2,1)}, bf16[1024,1024]{1,0:T(8,128)(2,1)}, u32[]{:S(2)}, u32[]{:S(2)}) collective-permute-start(bf16[1024,1024]{1,0:T(8,128)(2,1)} %bitcast.193), channel_id=1, source_target_pairs={{4,0},{0,1},{6,2},{2,3},{5,4},{1,5},{7,6},{3,7},{12,8},{8,9},{14,1... | collective-permute-start | bytes 6291464 | tf_op jit(solution)/shard_map/ppermute | solution.py:706
  738.1 104.8 %collective-permute-start.33 = (bf16[896,1024]{1,0:T(8,128)(2,1)}, bf16[896,1024]{1,0:T(8,128)(2,1)}, u32[]{:S(2)}, u32[]{:S(2)}) collective-permute-start(bf16[896,1024]{1,0:T(8,128)(2,1)} %collective-permute-done.27.refs_1_), channel_id=1, source_target_pairs={{0,2},{1,3},{2,0},{3,1},{4,6},{5,7},{6,4},{7,5},{8,10},{9,11},{10,... | collective-permute-start | bytes 5505032 | tf_op jit(solution)/shard_map/ppermute | solution.py:643
  771.4 56.1 %collective-permute-start.38 = (bf16[384,1024]{1,0:T(8,128)(2,1)}, bf16[384,1024]{1,0:T(8,128)(2,1)}, u32[]{:S(2)}, u32[]{:S(2)}) collective-permute-start(bf16[384,1024]{1,0:T(8,128)(2,1)} %get-tuple-element.156), channel_id=1, source_target_pairs={{0,2},{1,3},{2,0},{3,1},{4,6},{5,7},{6,4},{7,5},{8,10},{9,11},{10,... | collective-permute-start | bytes 2359304 | tf_op jit(solution)/shard_map/ppermute | solution.py:643
  811.0 77.3 %collective-permute-start.47 = (bf16[1024,1024]{1,0:T(8,128)(2,1)}, bf16[1024,1024]{1,0:T(8,128)(2,1)}, u32[]{:S(2)}, u32[]{:S(2)}) collective-permute-start(bf16[1024,1024]{1,0:T(8,128)(2,1)} %bitcast.190), channel_id=1, source_target_pairs={{4,0},{0,1},{6,2},{2,3},{5,4},{1,5},{7,6},{3,7},{12,8},{8,9},{14,1... | collective-permute-start | bytes 6291464 | tf_op jit(solution)/shard_map/ppermute | solution.py:706
  813.4 81.1 %collective-permute-start.48 = (bf16[1024,1024]{1,0:T(8,128)(2,1)}, bf16[1024,1024]{1,0:T(8,128)(2,1)}, u32[]{:S(2)}, u32[]{:S(2)}) collective-permute-start(bf16[1024,1024]{1,0:T(8,128)(2,1)} %bitcast.191), channel_id=1, source_target_pairs={{4,0},{0,1},{6,2},{2,3},{5,4},{1,5},{7,6},{3,7},{12,8},{8,9},{14,1... | collective-permute-start | bytes 6291464 | tf_op jit(solution)/shard_map/ppermute | solution.py:706
  815.5 62.1 %collective-permute-start.40 = (bf16[384,1024]{1,0:T(8,128)(2,1)S(1)}, bf16[384,1024]{1,0:T(8,128)(2,1)S(1)}, u32[]{:S(2)}, u32[]{:S(2)}) collective-permute-start(bf16[384,1024]{1,0:T(8,128)(2,1)S(1)} %collective-permute-done.36), channel_id=1, source_target_pairs={{0,2},{1,3},{2,0},{3,1},{4,6},{5,7},{6,4},{7,5},{8,10},{9,11},{10,... | collective-permute-start | bytes 2359304 | tf_op jit(solution)/shard_map/ppermute | solution.py:643
  (79 other events, 1496.8 us)
Sparse Core Ops, SparseCore 0:
  39.4 85.3 all-gather.8
  126.4 71.7 all-gather.10
  203.7 56.3 all-gather.12
  261.5 56.7 all-gather.14
  402.5 54.3 reduce-scatter.4
  459.1 57.5 reduce-scatter.6
  551.8 56.4 reduce-scatter.8
  610.6 79.6 reduce-scatter.10
  773.6 64.3 all-reduce.2
